TPU v7x, 32 devices: a whole 2x2x4 slice. The times are simulated.
32 devices in a mesh: rep: 4 (over y, core), shard: 4 (over z), ctx: 2 (over x).
Axes of the slice: x: 2, y: 2, z: 4, core: 2. Of those that a mesh axis runs over, the one named last changes fastest.
Arguments:
- tokens: bfloat16 [2, 4, 512, 2048], P(None, 'rep', ('shard', 'ctx')), may hold values from -6 to 6
- span_starts: int32 [2, 4], P(None, 'rep'), may hold values from 0 to 256
- cotangent: bfloat16 [2, 4, 512, 2048], P(None, 'rep', ('shard', 'ctx')), may hold values from -6 to 6
- w_query: bfloat16 [2048, 2048], P('shard'), may hold values from -0.125 to 0.125
- key_weight: bfloat16 [2048, 1024], P('shard'), may hold values from -0.125 to 0.125
- value_weight: bfloat16 [2048, 1024], P('shard'), may hold values from -0.125 to 0.125
- w_out: bfloat16 [2048, 2048], P('shard'), may hold values from -0.75 to 0.75
- attn_gain: bfloat16 [2048], P('shard'), may hold values from 0.099609375 to 1.8984375
- query_gain: bfloat16 [128], P('shard'), may hold values from 0.099609375 to 1.8984375
- key_gain: bfloat16 [128], P('shard'), may hold values from 0.099609375 to 1.8984375
- w_gate: bfloat16 [2048, 6144], P('shard'), may hold values from -0.125 to 0.125
- w_up: bfloat16 [2048, 6144], P('shard'), may hold values from -0.125 to 0.125
- w_down: bfloat16 [6144, 2048], P('shard'), may hold values from -0.078125 to 0.078125
- ffn_gain: bfloat16 [2048], P('shard'), may hold values from 0.099609375 to 1.8984375
Outputs:
- output: bfloat16 [2, 4, 512, 2048], P(None, 'rep', ('shard', 'ctx'))
- input_grad: float32 [2, 4, 512, 2048], P(None, 'rep', ('shard', 'ctx'))
- grad_query: float32 [2048, 2048], P('shard')
- grad_key: float32 [2048, 1024], P('shard')
- grad_value: float32 [2048, 1024], P('shard')
- grad_out: float32 [2048, 2048], P('shard')
- grad_attn_gain: float32 [2048], P('shard')
- grad_query_gain: float32 [128], P('shard')
- grad_key_gain: float32 [128], P('shard')
- grad_gate: float32 [2048, 6144], P('shard')
- grad_up: float32 [2048, 6144], P('shard')
- grad_down: float32 [6144, 2048], P('shard')
- grad_ffn_gain: float32 [2048], P('shard')
Inputs may be any that keep to these rules, and one draw needn't show every extreme that they name: `span_starts`: each sequence's picture span covers positions start to start + 255 of that sequence.
All inputs are finite; a program needn't handle non-finite values.
Results may differ from a plain program's by a relative error of at most 0.023.
Values may be sent and summed in bfloat16 or wider, within the bound.
No kernel may reach another device: no remote copies, remote signals or barrier semaphores. Data moves between devices by JAX's collectives and lax.ppermute only.
A program may use at most 448 MiB of HBM per device.

v0:
```python
from functools import partial

import jax
import jax.numpy as jnp
from jax import lax
from jax.sharding import PartitionSpec as P

QUERY_HEADS = 16
KEY_VALUE_HEADS = 8
HEAD_SIZE = 128
PIC = 256


EPSILON = 1e-06
THETA = 1000000.0


def apply_rotation(values):
    half_width = values.shape[-1] // 2
    return jnp.concatenate([-values[..., half_width:], values[..., :half_width]], axis=-1)


def rotate_back(values):
    half_width = values.shape[-1] // 2
    return jnp.concatenate([values[..., half_width:], -values[..., :half_width]], axis=-1)


def spin_tables(positions):
    inverse = THETA ** (-jnp.arange(HEAD_SIZE // 2, dtype=jnp.float32) * 2.0 / HEAD_SIZE)
    angles = positions.astype(jnp.float32)[:, None] * inverse[None, :]
    cosine_table = jnp.concatenate([jnp.cos(angles), jnp.cos(angles)], axis=-1)[:, None, :]
    sine_values = jnp.concatenate([jnp.sin(angles), jnp.sin(angles)], axis=-1)[:, None, :]
    return (cosine_table, sine_values)


def recip_rms(values):
    return lax.rsqrt(jnp.mean(values * values, axis=-1, keepdims=True) + EPSILON)


def norm_back(unit, recip, gain, d_normed):
    d_unit = d_normed * gain
    return recip * (d_unit - unit * jnp.mean(d_unit * unit, axis=-1, keepdims=True))


def over_rows(left, right):
    return lax.dot_general(
        left, right, (((0,), (0,)), ((), ())), preferred_element_type=jnp.float32
    )


def compared_to(left, right):
    return lax.dot_general(
        left, right, (((1,), (1,)), ((), ())), preferred_element_type=jnp.float32
    )


def attention_set(w_query, key_weight, value_weight, w_out, attn_gain, query_gain, key_gain):
    return (
        lax.all_gather(w_query, "shard", axis=0, tiled=True),
        lax.all_gather(key_weight, "shard", axis=0, tiled=True),
        lax.all_gather(value_weight, "shard", axis=0, tiled=True),
        lax.all_gather(w_out, "shard", axis=0, tiled=True),
        lax.all_gather(attn_gain, "shard", axis=0, tiled=True),
        lax.all_gather(query_gain, "shard", axis=0, tiled=True),
        lax.all_gather(key_gain, "shard", axis=0, tiled=True),
    )


def feedforward_set(w_gate, w_up, w_down, ffn_gain):
    return (
        lax.all_gather(w_gate, "shard", axis=0, tiled=True),
        lax.all_gather(w_up, "shard", axis=0, tiled=True),
        lax.all_gather(w_down, "shard", axis=0, tiled=True),
        lax.all_gather(ffn_gain, "shard", axis=0, tiled=True),
    )


def masked_scores(allowed, q_head, k_head):
    scores = jnp.einsum(
        "tgd,sd->gts", q_head, k_head, preferred_element_type=jnp.float32
    ) * HEAD_SIZE ** (-0.5)
    return jnp.where(allowed, scores, -1e30)


def head_forward(allowed, pieces):
    q_head, k_head, v_head = pieces
    scores = masked_scores(allowed, q_head, k_head)
    highest = jnp.max(scores, axis=-1, keepdims=True)
    log_total = highest + jnp.log(jnp.sum(jnp.exp(scores - highest), axis=-1, keepdims=True))
    probs_low = jnp.exp(scores - log_total).astype(jnp.bfloat16)
    mixed = jnp.einsum("gts,sd->tgd", probs_low, v_head, preferred_element_type=jnp.float32)
    return (mixed, log_total)


def head_backward(allowed, pieces):
    q_head, k_head, v_head, d_mix_head, log_total = pieces
    probs = jnp.exp(masked_scores(allowed, q_head, k_head) - log_total)
    probs_low = probs.astype(jnp.bfloat16)
    d_probs = jnp.einsum("tgd,sd->gts", d_mix_head, v_head, preferred_element_type=jnp.float32)
    d_values = jnp.einsum("gts,tgd->sd", probs_low, d_mix_head, preferred_element_type=jnp.float32)
    row_dot = jnp.sum(probs * d_probs, axis=-1, keepdims=True)
    d_scores = (probs * (d_probs - row_dot)).astype(jnp.bfloat16)
    d_queries = jnp.einsum(
        "gts,sd->tgd", d_scores, k_head, preferred_element_type=jnp.float32
    ) * HEAD_SIZE ** (-0.5)
    d_keys = jnp.einsum(
        "gts,tgd->sd", d_scores, q_head, preferred_element_type=jnp.float32
    ) * HEAD_SIZE ** (-0.5)
    return (d_queries, d_keys, d_values)


def shards(
    tokens,
    span_starts,
    cotangent,
    w_query,
    key_weight,
    value_weight,
    w_out,
    attn_gain,
    query_gain,
    key_gain,
    w_gate,
    w_up,
    w_down,
    ffn_gain,
):
    seq_count = lax.axis_size(("shard", "ctx"))
    seq_rank = lax.axis_index(("shard", "ctx"))
    token_rows = tokens.shape[2]
    token_length = token_rows * seq_count
    group_width = QUERY_HEADS // KEY_VALUE_HEADS
    local_pos = seq_rank * token_rows + jnp.arange(token_rows, dtype=jnp.int32)
    key_pos = jnp.arange(token_length, dtype=jnp.int32)
    cosine_table, sine_values = spin_tables(local_pos)
    cos_keys = cosine_table[:, 0, :][None]
    sin_keys = sine_values[:, 0, :][None]
    out_list = []
    grad_list = []
    stored = []
    totals = None
    for micro_index in range(tokens.shape[0]):
        span_start = span_starts[micro_index, 0]
        inside_q = (local_pos >= span_start) & (local_pos < span_start + PIC)
        inside_k = (key_pos >= span_start) & (key_pos < span_start + PIC)
        allowed = (key_pos[None, :] <= local_pos[:, None]) | inside_q[:, None] & inside_k[None, :]
        hidden_in = tokens[micro_index, 0].astype(jnp.float32)
        full_query, full_key, full_value, complete_output, gain_attn, gain_query, gain_key = (
            attention_set(w_query, key_weight, value_weight, w_out, attn_gain, query_gain, key_gain)
        )
        gain_attn = gain_attn.astype(jnp.float32)
        gain_query = gain_query.astype(jnp.float32)
        gain_key = gain_key.astype(jnp.float32)
        recip_h = recip_rms(hidden_in)
        unit_h = hidden_in * recip_h
        normalized_rows = (unit_h * gain_attn).astype(jnp.bfloat16)
        q_pre = jnp.dot(normalized_rows, full_query, preferred_element_type=jnp.float32).reshape(
            token_rows, QUERY_HEADS, HEAD_SIZE
        )
        key_before_rotation = jnp.transpose(
            jnp.dot(normalized_rows, full_key, preferred_element_type=jnp.float32).reshape(
                token_rows, KEY_VALUE_HEADS, HEAD_SIZE
            ),
            (1, 0, 2),
        )
        value_local = jnp.transpose(
            jnp.dot(normalized_rows, full_value, preferred_element_type=jnp.float32)
            .astype(jnp.bfloat16)
            .reshape(token_rows, KEY_VALUE_HEADS, HEAD_SIZE),
            (1, 0, 2),
        )
        recip_q = recip_rms(q_pre)
        unit_query = q_pre * recip_q
        recip_k = recip_rms(key_before_rotation)
        unit_k = key_before_rotation * recip_k
        scaled_q = unit_query * gain_query
        scaled_k = unit_k * gain_key
        query_rows = jnp.transpose(
            (scaled_q * cosine_table + apply_rotation(scaled_q) * sine_values)
            .astype(jnp.bfloat16)
            .reshape(token_rows, KEY_VALUE_HEADS, group_width, HEAD_SIZE),
            (1, 0, 2, 3),
        )
        key_local = (scaled_k * cos_keys + apply_rotation(scaled_k) * sin_keys).astype(jnp.bfloat16)
        key_rows, value_matrix = (
            lax.all_gather(key_local, ("shard", "ctx"), axis=1, tiled=True),
            lax.all_gather(value_local, ("shard", "ctx"), axis=1, tiled=True),
        )
        mixed_split, log_total = lax.map(
            partial(head_forward, allowed), (query_rows, key_rows, value_matrix)
        )
        mixed_heads = (
            jnp.transpose(mixed_split, (1, 0, 2, 3))
            .reshape(token_rows, QUERY_HEADS * HEAD_SIZE)
            .astype(jnp.bfloat16)
        )
        middle = hidden_in + jnp.dot(
            mixed_heads, complete_output, preferred_element_type=jnp.float32
        )
        full_gate, full_up, full_down, gain_ffn = feedforward_set(w_gate, w_up, w_down, ffn_gain)
        gain_ffn = gain_ffn.astype(jnp.float32)
        recip_m = recip_rms(middle)
        unit_m = middle * recip_m
        ffn_in = (unit_m * gain_ffn).astype(jnp.bfloat16)
        gate_pre = jnp.dot(ffn_in, full_gate, preferred_element_type=jnp.float32)
        up_pre = jnp.dot(ffn_in, full_up, preferred_element_type=jnp.float32)
        sigma = jax.nn.sigmoid(gate_pre)
        act_gate = gate_pre * sigma
        inner_act = (act_gate * up_pre).astype(jnp.bfloat16)
        result = middle + jnp.dot(inner_act, full_down, preferred_element_type=jnp.float32)
        out_list.append(result.astype(jnp.bfloat16))
        cot_rows = cotangent[micro_index, 0]
        cot_float = cot_rows.astype(jnp.float32)
        d_inner = compared_to(cot_rows, full_down)
        d_gate = (d_inner * up_pre * sigma * (1.0 + gate_pre * (1.0 - sigma))).astype(jnp.bfloat16)
        d_up = (d_inner * act_gate).astype(jnp.bfloat16)
        d_ffn_in = compared_to(d_gate, full_gate) + compared_to(d_up, full_up)
        ffn_gain_part = jnp.sum(d_ffn_in * unit_m, axis=0)
        d_middle = cot_float + norm_back(unit_m, recip_m, gain_ffn, d_ffn_in)
        branch_gradient = d_middle.astype(jnp.bfloat16)
        d_mixed = jnp.transpose(
            compared_to(branch_gradient, complete_output)
            .astype(jnp.bfloat16)
            .reshape(token_rows, KEY_VALUE_HEADS, group_width, HEAD_SIZE),
            (1, 0, 2, 3),
        )
        d_split_q, d_keys, d_values = lax.map(
            partial(head_backward, allowed),
            (query_rows, key_rows, value_matrix, d_mixed, log_total),
        )
        d_queries = jnp.transpose(d_split_q, (1, 0, 2, 3)).reshape(
            token_rows, QUERY_HEADS, HEAD_SIZE
        )
        d_key_local, d_value_local = (
            lax.psum_scatter(
                d_keys.astype(jnp.bfloat16), ("shard", "ctx"), scatter_dimension=1, tiled=True
            ).astype(jnp.float32),
            lax.psum_scatter(
                d_values.astype(jnp.bfloat16), ("shard", "ctx"), scatter_dimension=1, tiled=True
            ).astype(jnp.float32),
        )
        d_unit_q = d_queries * cosine_table + rotate_back(d_queries * sine_values)
        d_unit_k = d_key_local * cos_keys + rotate_back(d_key_local * sin_keys)
        query_gain_part = jnp.sum(d_unit_q * unit_query, axis=(0, 1))
        key_gain_part = jnp.sum(d_unit_k * unit_k, axis=(0, 1))
        d_q_pre = (
            norm_back(unit_query, recip_q, gain_query, d_unit_q)
            .astype(jnp.bfloat16)
            .reshape(token_rows, QUERY_HEADS * HEAD_SIZE)
        )
        d_k_pre = jnp.transpose(
            norm_back(unit_k, recip_k, gain_key, d_unit_k).astype(jnp.bfloat16), (1, 0, 2)
        ).reshape(token_rows, KEY_VALUE_HEADS * HEAD_SIZE)
        d_v_pre = jnp.transpose(d_value_local.astype(jnp.bfloat16), (1, 0, 2)).reshape(
            token_rows, KEY_VALUE_HEADS * HEAD_SIZE
        )
        d_normed = (
            compared_to(d_q_pre, full_query)
            + compared_to(d_k_pre, full_key)
            + compared_to(d_v_pre, full_value)
        )
        attn_gain_part = jnp.sum(d_normed * unit_h, axis=0)
        grad_list.append(d_middle + norm_back(unit_h, recip_h, gain_attn, d_normed))
        stored.append(
            (
                normalized_rows,
                d_q_pre,
                d_k_pre,
                d_v_pre,
                mixed_heads,
                branch_gradient,
                ffn_in,
                d_gate,
                d_up,
                inner_act,
                cot_rows,
            )
        )
        parts = (attn_gain_part, query_gain_part, key_gain_part, ffn_gain_part)
        if totals is None:
            totals = parts
        else:
            totals = tuple((older + newer for older, newer in zip(totals, parts)))
    joined = [
        jnp.concatenate([saved_set[member] for saved_set in stored], axis=0) for member in range(11)
    ]
    (
        normed_all,
        dq_all,
        dk_all,
        dv_all,
        mixed_all,
        branch_all,
        ffn_all,
        gate_all,
        up_all,
        inner_all,
        cot_all,
    ) = joined
    totals = (
        lax.psum_scatter(
            over_rows(normed_all, dq_all).astype(jnp.bfloat16),
            "shard",
            scatter_dimension=0,
            tiled=True,
        ).astype(jnp.float32),
        lax.psum_scatter(
            over_rows(normed_all, dk_all).astype(jnp.bfloat16),
            "shard",
            scatter_dimension=0,
            tiled=True,
        ).astype(jnp.float32),
        lax.psum_scatter(
            over_rows(normed_all, dv_all).astype(jnp.bfloat16),
            "shard",
            scatter_dimension=0,
            tiled=True,
        ).astype(jnp.float32),
        lax.psum_scatter(
            over_rows(mixed_all, branch_all).astype(jnp.bfloat16),
            "shard",
            scatter_dimension=0,
            tiled=True,
        ).astype(jnp.float32),
        lax.psum_scatter(
            totals[0].astype(jnp.bfloat16), "shard", scatter_dimension=0, tiled=True
        ).astype(jnp.float32),
        lax.psum_scatter(
            totals[1].astype(jnp.bfloat16), "shard", scatter_dimension=0, tiled=True
        ).astype(jnp.float32),
        lax.psum_scatter(
            totals[2].astype(jnp.bfloat16), "shard", scatter_dimension=0, tiled=True
        ).astype(jnp.float32),
        lax.psum_scatter(
            over_rows(ffn_all, gate_all).astype(jnp.bfloat16),
            "shard",
            scatter_dimension=0,
            tiled=True,
        ).astype(jnp.float32),
        lax.psum_scatter(
            over_rows(ffn_all, up_all).astype(jnp.bfloat16),
            "shard",
            scatter_dimension=0,
            tiled=True,
        ).astype(jnp.float32),
        lax.psum_scatter(
            over_rows(inner_all, cot_all).astype(jnp.bfloat16),
            "shard",
            scatter_dimension=0,
            tiled=True,
        ).astype(jnp.float32),
        lax.psum_scatter(
            totals[3].astype(jnp.bfloat16), "shard", scatter_dimension=0, tiled=True
        ).astype(jnp.float32),
    )
    summed = (
        lax.psum(totals[0].astype(jnp.bfloat16), ("rep", "ctx")).astype(jnp.float32),
        lax.psum(totals[1].astype(jnp.bfloat16), ("rep", "ctx")).astype(jnp.float32),
        lax.psum(totals[2].astype(jnp.bfloat16), ("rep", "ctx")).astype(jnp.float32),
        lax.psum(totals[3].astype(jnp.bfloat16), ("rep", "ctx")).astype(jnp.float32),
        lax.psum(totals[4].astype(jnp.bfloat16), ("rep", "ctx")).astype(jnp.float32),
        lax.psum(totals[5].astype(jnp.bfloat16), ("rep", "ctx")).astype(jnp.float32),
        lax.psum(totals[6].astype(jnp.bfloat16), ("rep", "ctx")).astype(jnp.float32),
        lax.psum(totals[7].astype(jnp.bfloat16), ("rep", "ctx")).astype(jnp.float32),
        lax.psum(totals[8].astype(jnp.bfloat16), ("rep", "ctx")).astype(jnp.float32),
        lax.psum(totals[9].astype(jnp.bfloat16), ("rep", "ctx")).astype(jnp.float32),
        lax.psum(totals[10].astype(jnp.bfloat16), ("rep", "ctx")).astype(jnp.float32),
    )
    output = jnp.stack(out_list)[:, None]
    input_grad = jnp.stack(grad_list)[:, None]
    return (
        output,
        input_grad,
        summed[0],
        summed[1],
        summed[2],
        summed[3],
        summed[4],
        summed[5],
        summed[6],
        summed[7],
        summed[8],
        summed[9],
        summed[10],
    )


def solution(mesh):
    in_specs = (
        P(None, "rep", ("shard", "ctx"), None),
        P(None, "rep"),
        P(None, "rep", ("shard", "ctx"), None),
        P("shard", None),
        P("shard", None),
        P("shard", None),
        P("shard", None),
        P("shard"),
        P("shard"),
        P("shard"),
        P("shard", None),
        P("shard", None),
        P("shard", None),
        P("shard"),
    )
    out_specs = (
        P(None, "rep", ("shard", "ctx"), None),
        P(None, "rep", ("shard", "ctx"), None),
        P("shard", None),
        P("shard", None),
        P("shard", None),
        P("shard", None),
        P("shard"),
        P("shard"),
        P("shard"),
        P("shard", None),
        P("shard", None),
        P("shard", None),
        P("shard"),
    )
    return jax.shard_map(shards, mesh=mesh, in_specs=in_specs, out_specs=out_specs, check_vma=False)
```

profile of v0, /device:TPU:14, one launch (start us, length us, event | category | flops | bytes accessed | tf_op | source)
XLA Modules:
  0.0 4426.3 jit_solution(448300715896860769)
XLA Ops:
  9.5 12.1 all-gather
  23.4 8.9 all-reduce.9
  33.0 56.4 %all-gather.18.cloned.1.call-done = bf16[2048,1024]{1,0:T(8,128)(2,1)} async-done(((bf16[512,1024]{1,0:T(8,128)(2,1)}), bf16[2048,1024]{1,0:T(8,128)(2,1)}) %all-gather.18.cloned.1.call-update) | async-done | bytes 4194320 | tf_op jit(solution)/shard_map/all_gather | solution.py:60
  89.4 6.4 copy.52
  95.8 3.8 multiply_reduce_fusion.18
  103.6 66.6 %all-gather.14.cloned.1.call-done = bf16[2048,1024]{1,0:T(8,128)(2,1)} async-done(((bf16[512,1024]{1,0:T(8,128)(2,1)}), bf16[2048,1024]{1,0:T(8,128)(2,1)}) %all-gather.14.cloned.1.call-update) | async-done | bytes 4194320 | tf_op jit(solution)/shard_map/all_gather | solution.py:61
  170.2 3.0 fusion.113
  174.6 3.0 fusion.114
  181.3 12.7 all-gather.1
  198.5 121.3 %all-gather.22.cloned.1.call-done = bf16[2048,2048]{1,0:T(8,128)(2,1)} async-done(((bf16[512,2048]{1,0:T(8,128)(2,1)}), bf16[2048,2048]{1,0:T(8,128)(2,1)}) %all-gather.22.cloned.1.call-update) | async-done | bytes 8388624 | tf_op jit(solution)/shard_map/all_gather | solution.py:59
  319.8 12.2 copy.53
  332.0 6.3 multiply_reduce_fusion.11
  338.4 2.8 multiply_reduce_fusion.13
  342.8 18.9 all-gather.20.cloned.1.call-done
  361.7 41.6 all-gather.16.cloned.1.call-done
  403.3 21.4 while.56
  425.9 19.0 all-gather.34.cloned.1.call-done
  444.9 41.7 all-gather.32.cloned.1.call-done
  486.7 21.6 while.57
  508.9 126.8 %all-gather.24.cloned.1.call-done = bf16[2048,2048]{1,0:T(8,128)(2,1)} async-done(((bf16[512,2048]{1,0:T(8,128)(2,1)}), bf16[2048,2048]{1,0:T(8,128)(2,1)}) %all-gather.24.cloned.1.call-update) | async-done | bytes 8388624 | tf_op jit(solution)/shard_map/all_gather | solution.py:62
  635.8 5.2 multiply_reduce_fusion.12
  643.4 417.4 %all-gather.26.cloned.1.call-done = bf16[2048,6144]{1,0:T(8,128)(2,1)} async-done(((bf16[512,6144]{1,0:T(8,128)(2,1)}), bf16[2048,6144]{1,0:T(8,128)(2,1)}) %all-gather.26.cloned.1.call-update) | async-done | bytes 25165840 | tf_op jit(solution)/shard_map/all_gather | solution.py:71
  1060.8 11.6 fusion.214
  1072.4 413.2 %all-gather.28.cloned.1.call-done = bf16[2048,6144]{1,0:T(8,128)(2,1)} async-done(((bf16[512,6144]{1,0:T(8,128)(2,1)}), bf16[2048,6144]{1,0:T(8,128)(2,1)}) %all-gather.28.cloned.1.call-update) | async-done | bytes 25165840 | tf_op jit(solution)/shard_map/all_gather | solution.py:72
  1485.6 11.8 fusion.215
  1497.4 413.2 %all-gather.30.cloned.1.call-done = bf16[6144,2048]{1,0:T(8,128)(2,1)} async-done(((bf16[1536,2048]{1,0:T(8,128)(2,1)}), bf16[6144,2048]{1,0:T(8,128)(2,1)}) %all-gather.30.cloned.1.call-update) | async-done | bytes 25165840 | tf_op jit(solution)/shard_map/all_gather | solution.py:73
  1910.6 13.7 multiply_convert_fusion.4
  1924.3 13.5 fusion.218
  1937.8 14.1 multiply_reduce_fusion.3
  1951.9 11.8 fusion.217
  1963.7 11.6 fusion.216
  1975.3 13.8 multiply_convert_fusion.2
  1989.2 13.3 fusion.219
  2002.4 14.4 multiply_reduce_fusion.2
  2019.7 6.0 convolution_convert_fusion.7
  2029.0 55.3 %while.59 = (s32[]{:T(128)}, f32[8,64,2,128]{3,1,2,0:T(8,128)S(1)}, bf16[8,512,128]{2,1,0:T(8,128)(2,1)}, bf16[8,512,128]{2,1,0:T(8,128)(2,1)}, bf16[8,512,128]{...) while((s32[]{:T(128)}, f32[8,64,2,128]{3,1,2,0:T(8,128)S(1)}, ...), condition=%wide.region_28.29_spmd.clone, body=%wide.region_26.28_spmd.clone.sunk | while | flops 84656000 | bytes 3154369 | solution.py:227
  2084.3 7.0 convolution_convert_fusion.8
  2098.0 60.2 %while.58 = (s32[]{:T(128)}, f32[8,64,2,128]{3,1,2,0:T(8,128)}, bf16[8,512,128]{2,1,0:T(8,128)(2,1)}, bf16[8,512,128]{2,1,0:T(8,128)(2,1)}, bf16[8,512,128]{2,1,...) while((s32[]{:T(128)}, f32[8,64,2,128]{3,1,2,0:T(8,128)}, ...), condition=%wide.region_19.20_spmd.clone, body=%wide.region_17.19_spmd.clone.sunk | while | flops 84656000 | bytes 3154369 | solution.py:227
  2161.4 65.6 %reduce-scatter.14.cloned.1.call-done = bf16[8,64,128]{2,1,0:T(8,128)(2,1)} async-done(((bf16[8,512,128]{2,1,0:T(8,128)(2,1)}), bf16[8,64,128]{2,1,0:T(8,128)(2,1)}) %reduce-scatter.14.cloned.1.call-update) | async-done | bytes 131088 | tf_op jit(solution)/shard_map/reduce_scatter | solution.py:238
  2227.9 4.2 convolution_convert_fusion.5
  2232.4 61.3 %reduce-scatter.16.cloned.1.call-done = bf16[8,64,128]{2,1,0:T(8,128)(2,1)} async-done(((bf16[8,512,128]{2,1,0:T(8,128)(2,1)}), bf16[8,64,128]{2,1,0:T(8,128)(2,1)}) %reduce-scatter.16.cloned.1.call-update) | async-done | bytes 131088 | tf_op jit(solution)/shard_map/reduce_scatter | solution.py:235
  2293.7 67.1 %reduce-scatter.12.cloned.1.call-done = bf16[8,64,128]{2,1,0:T(8,128)(2,1)} async-done(((bf16[8,512,128]{2,1,0:T(8,128)(2,1)}), bf16[8,64,128]{2,1,0:T(8,128)(2,1)}) %reduce-scatter.12.cloned.1.call-update) | async-done | bytes 131088 | tf_op jit(solution)/shard_map/reduce_scatter | solution.py:235
  2366.0 3.4 convolution_convert_fusion.6
  2370.5 6.8 convolution_convert_fusion.3
  2383.1 5.8 convolution_convert_fusion.4
  2389.1 13.0 convolution_convert_fusion.1
  2403.3 12.9 convolution_convert_fusion.2
  2417.5 13.0 convolution_convert_fusion
  2430.8 8.6 reduce-scatter.24.cloned.1.call-done
  2439.4 80.1 %reduce-scatter.22.cloned.1.call-done = bf16[512,1024]{1,0:T(8,128)(2,1)} async-done(((bf16[2048,1024]{1,0:T(8,128)(2,1)}), bf16[512,1024]{1,0:T(8,128)(2,1)}) %reduce-scatter.22.cloned.1.call-update) | async-done | bytes 1048592 | tf_op jit(solution)/shard_map/reduce_scatter | solution.py:307
  2519.5 147.5 %reduce-scatter.26.cloned.1.call-done = bf16[512,2048]{1,0:T(8,128)(2,1)} async-done(((bf16[2048,2048]{1,0:T(8,128)(2,1)}), bf16[512,2048]{1,0:T(8,128)(2,1)}) %reduce-scatter.26.cloned.1.call-update) | async-done | bytes 2097168 | tf_op jit(solution)/shard_map/reduce_scatter | solution.py:319
  2667.0 148.2 %reduce-scatter.20.cloned.1.call-done = bf16[512,2048]{1,0:T(8,128)(2,1)} async-done(((bf16[2048,2048]{1,0:T(8,128)(2,1)}), bf16[512,2048]{1,0:T(8,128)(2,1)}) %reduce-scatter.20.cloned.1.call-update) | async-done | bytes 2097168 | tf_op jit(solution)/shard_map/reduce_scatter | solution.py:301
  2815.2 417.4 %reduce-scatter.30.cloned.1.call-done = bf16[512,6144]{1,0:T(8,128)(2,1)} async-done(((bf16[2048,6144]{1,0:T(8,128)(2,1)}), bf16[512,6144]{1,0:T(8,128)(2,1)}) %reduce-scatter.30.cloned.1.call-update) | async-done | bytes 6291472 | tf_op jit(solution)/shard_map/reduce_scatter | solution.py:340
  3232.5 418.7 %reduce-scatter.28.cloned.1.call-done = bf16[512,6144]{1,0:T(8,128)(2,1)} async-done(((bf16[2048,6144]{1,0:T(8,128)(2,1)}), bf16[512,6144]{1,0:T(8,128)(2,1)}) %reduce-scatter.28.cloned.1.call-update) | async-done | bytes 6291472 | tf_op jit(solution)/shard_map/reduce_scatter | solution.py:334
  3651.2 418.6 %reduce-scatter.32.cloned.1.call-done = bf16[1536,2048]{1,0:T(8,128)(2,1)} async-done(((bf16[6144,2048]{1,0:T(8,128)(2,1)}), bf16[1536,2048]{1,0:T(8,128)(2,1)}) %reduce-scatter.32.cloned.1.call-update) | async-done | bytes 6291472 | tf_op jit(solution)/shard_map/reduce_scatter | solution.py:346
  4072.4 10.7 fusion.101
  4083.1 11.8 fusion.100
  4098.5 2.7 fusion.198
  4108.1 10.9 all-reduce.8
  4119.2 13.5 all-reduce.6
  4139.0 250.0 %all-reduce.12.cloned.1.call-done = (bf16[512,2048]{1,0:T(8,128)(2,1)}, bf16[512,1024]{1,0:T(8,128)(2,1)}, bf16[512,1024]{1,0:T(8,128)(2,1)}, bf16[512,2048]{1,0...) async-done(((bf16[512,2048]{1,0:T(8,128)(2,1)}, bf16[512,1024]{1,0:T(8,128)(2,1)}, bf16[512,1024]{1,0:T(8,128)(2,1)}, ...) | async-done | bytes 25165840 | tf_op jit(solution)/shard_map/psum | solution.py:357
  4389.0 9.4 convert_element_type.355
  4398.4 6.4 convert_element_type.357
  4404.8 6.3 convert_element_type.359
  (585 shorter events, 236.6 us)
Async XLA Ops:
  7.2 14.5 copy-start.89
  7.2 15.7 copy-start.102
  7.2 16.0 copy-start.103
  7.2 25.5 copy-start.5
  7.2 82.1 %all-gather.18.cloned.1.call-start = ((), (), s32[]{:S(2)}) async-start(), calls=%async_computation.13 | async-start | bytes 5242880 | tf_op jit(solution)/shard_map/all_gather | solution.py:60
  8.0 162.2 %all-gather.14.cloned.1.call-start = ((), (), s32[]{:S(2)}) async-start(), calls=%async_computation.11 | async-start | bytes 5242880 | tf_op jit(solution)/shard_map/all_gather | solution.py:61
  8.7 311.1 %all-gather.22.cloned.1.call-start = ((), (), s32[]{:S(2)}) async-start(), calls=%async_computation.15 | async-start | bytes 10485760 | tf_op jit(solution)/shard_map/all_gather | solution.py:59
  9.5 352.3 %all-gather.20.cloned.1.call-start = ((), (), s32[]{:S(2)}) async-start(), calls=%async_computation.14 | async-start | bytes 1179648 | tf_op jit(solution)/shard_map/all_gather | solution.py:186
  21.7 316.7 %copy-start.59 = (f32[4,1,512]{2,1,0:T(1,128)}, f32[4,1,512]{2,1,0:T(1,128)S(1)}, u32[]{:S(2)}) copy-start(f32[4,1,512]{2,1,0:T(1,128)S(1)} %convert_element_type.364) | copy-start | bytes 24580
  32.4 68.8 %copy-start.87 = (f32[128]{0:T(128)}, f32[128]{0:T(128)S(1)}, u32[]{:S(2)}) copy-start(f32[128]{0:T(128)S(1)} %convert_element_type.293) | copy-start | bytes 1540
  32.7 2328.0 %copy-start.58 = (f32[64,128]{1,0:T(8,128)}, f32[64,128]{1,0:T(8,128)S(1)}, u32[]{:S(2)}) copy-start(f32[64,128]{1,0:T(8,128)S(1)} %get-tuple-element.560) | copy-start | bytes 98308
  32.7 2329.3 %copy-start.56 = (f32[64,128]{1,0:T(8,128)}, f32[64,128]{1,0:T(8,128)S(1)}, u32[]{:S(2)}) copy-start(f32[64,128]{1,0:T(8,128)S(1)} %get-tuple-element.559) | copy-start | bytes 98308
  33.0 299.1 %copy-start.77 = (f32[64]{0:T(128)}, f32[64]{0:T(128)S(1)}, u32[]{:S(2)}) copy-start(f32[64]{0:T(128)S(1)} %get-tuple-element.557) | copy-start | bytes 772
  33.0 305.4 %copy-start.75 = (f32[64]{0:T(128)}, f32[64]{0:T(128)S(1)}, u32[]{:S(2)}) copy-start(f32[64]{0:T(128)S(1)} %get-tuple-element.558) | copy-start | bytes 772
  103.3 300.0 %all-gather.16.cloned.1.call-start = ((), (), s32[]{:S(2)}) async-start(), calls=%async_computation.12 | async-start | bytes 1179648 | tf_op jit(solution)/shard_map/all_gather | solution.py:187
  103.6 74.0 %copy-start.20 = (bf16[64,2048]{1,0:T(8,128)(2,1)}, bf16[64,2048]{1,0:T(8,128)(2,1)S(1)}, u32[]{:S(2)}) copy-start(bf16[64,2048]{1,0:T(8,128)(2,1)S(1)} %get-tuple-element.493) | copy-start | bytes 786436
  103.6 74.0 %copy-start.23 = (bf16[64,2048]{1,0:T(8,128)(2,1)}, bf16[64,2048]{1,0:T(8,128)(2,1)S(1)}, u32[]{:S(2)}) copy-start(bf16[64,2048]{1,0:T(8,128)(2,1)S(1)} %get-tuple-element.494) | copy-start | bytes 786436
  173.9 271.0 %all-gather.34.cloned.1.call-start = ((), (), s32[]{:S(2)}) async-start(), calls=%async_computation.21 | async-start | bytes 1179648 | tf_op jit(solution)/shard_map/all_gather | solution.py:186
  174.5 312.1 %all-gather.32.cloned.1.call-start = ((), (), s32[]{:S(2)}) async-start(), calls=%async_computation.20 | async-start | bytes 1179648 | tf_op jit(solution)/shard_map/all_gather | solution.py:187
  178.3 457.4 %all-gather.24.cloned.1.call-start = ((), (), s32[]{:S(2)}) async-start(), calls=%async_computation.16 | async-start | bytes 10485760 | tf_op jit(solution)/shard_map/all_gather | solution.py:62
  179.1 881.7 %all-gather.26.cloned.1.call-start = ((), (), s32[]{:S(2)}) async-start(), calls=%async_computation.17 | async-start | bytes 31457280 | tf_op jit(solution)/shard_map/all_gather | solution.py:71
  179.8 1305.8 %all-gather.28.cloned.1.call-start = ((), (), s32[]{:S(2)}) async-start(), calls=%async_computation.18 | async-start | bytes 31457280 | tf_op jit(solution)/shard_map/all_gather | solution.py:72
  180.4 13.6 copy-start.90
  180.4 1730.2 %all-gather.30.cloned.1.call-start = ((), (), s32[]{:S(2)}) async-start(), calls=%async_computation.19 | async-start | bytes 31457280 | tf_op jit(solution)/shard_map/all_gather | solution.py:73
  181.2 1978.6 %reduce-scatter.18.cloned.1.call-start = ((), (), s32[]{:S(2)}) async-start(), calls=%async_computation.25 | async-start | bytes 1179648 | tf_op jit(solution)/shard_map/reduce_scatter | solution.py:238
  181.3 150.8 %copy-start.44 = (bf16[8,64,2,128]{3,1,2,0:T(8,128)(2,1)}, bf16[8,64,2,128]{3,1,2,0:T(8,128)(2,1)S(1)}, u32[]{:S(2)}) copy-start(bf16[8,64,2,128]{3,1,2,0:T(8,128)(2,1)S(1)} %fusion.209) | copy-start | bytes 786436
  181.3 159.9 %copy-start.80 = (f32[128]{0:T(128)}, f32[128]{0:T(128)S(1)}, u32[]{:S(2)}) copy-start(f32[128]{0:T(128)S(1)} %convert_element_type.296) | copy-start | bytes 1540
  342.0 61.3 %copy-start.46 = (bf16[8,64,2,128]{3,1,2,0:T(8,128)(2,1)S(1)}, bf16[8,64,2,128]{3,1,2,0:T(8,128)(2,1)}, u32[]{:S(2)}) copy-start(bf16[8,64,2,128]{3,1,2,0:T(8,128)(2,1)} %copy-done.44) | copy-start | bytes 786436
  342.8 143.8 %copy-start.45 = (bf16[8,64,2,128]{3,1,2,0:T(8,128)(2,1)S(1)}, bf16[8,64,2,128]{3,1,2,0:T(8,128)(2,1)}, u32[]{:S(2)}) copy-start(bf16[8,64,2,128]{3,1,2,0:T(8,128)(2,1)} %copy-done.44) | copy-start | bytes 786436
  425.9 215.1 %copy-start.38 = (bf16[64,2048]{1,0:T(8,128)(2,1)}, bf16[64,2048]{1,0:T(8,128)(2,1)S(1)}, u32[]{:S(2)}) copy-start(bf16[64,2048]{1,0:T(8,128)(2,1)S(1)} %convert_element_type.300) | copy-start | bytes 786436
  508.9 132.1 %copy-start.40 = (bf16[64,2048]{1,0:T(8,128)(2,1)}, bf16[64,2048]{1,0:T(8,128)(2,1)S(1)}, u32[]{:S(2)}) copy-start(bf16[64,2048]{1,0:T(8,128)(2,1)S(1)} %convert_element_type.316) | copy-start | bytes 786436
  641.5 1375.3 %copy-start.85 = (f32[64]{0:T(128)}, f32[64]{0:T(128)S(1)}, u32[]{:S(2)}) copy-start(f32[64]{0:T(128)S(1)} %add_rsqrt_fusion.6) | copy-start | bytes 772
  643.3 1373.6 %copy-start.83 = (f32[64]{0:T(128)}, f32[64]{0:T(128)S(1)}, u32[]{:S(2)}) copy-start(f32[64]{0:T(128)S(1)} %add_rsqrt_fusion.4) | copy-start | bytes 772
  643.4 842.2 %copy-start.19 = (bf16[64,2048]{1,0:T(8,128)(2,1)}, bf16[64,2048]{1,0:T(8,128)(2,1)S(1)}, u32[]{:S(2)}) copy-start(bf16[64,2048]{1,0:T(8,128)(2,1)S(1)} %multiply_convert_fusion.11) | copy-start | bytes 786436
  1072.4 838.2 %copy-start.11 = (bf16[2,1,64,2048]{3,2,1,0:T(8,128)(2,1)S(1)}, bf16[2,1,64,2048]{3,2,1,0:T(8,128)(2,1)}, u32[]{:S(2)}) copy-start(bf16[2,1,64,2048]{3,2,1,0:T(8,128)(2,1)} %param.24) | copy-start | bytes 1572868
  1924.3 13.5 copy-start.10
  2094.9 132.1 %reduce-scatter.14.cloned.1.call-start = ((), (), s32[]{:S(2)}) async-start(), calls=%async_computation.23 | async-start | bytes 1179648 | tf_op jit(solution)/shard_map/reduce_scatter | solution.py:238
  2098.0 129.9 %copy-start.21 = (bf16[64,2048]{1,0:T(8,128)(2,1)S(1)}, bf16[64,2048]{1,0:T(8,128)(2,1)}, u32[]{:S(2)}) copy-start(bf16[64,2048]{1,0:T(8,128)(2,1)} %copy-done.20) | copy-start | bytes 786436
  2098.0 129.9 %copy-start.24 = (bf16[64,2048]{1,0:T(8,128)(2,1)S(1)}, bf16[64,2048]{1,0:T(8,128)(2,1)}, u32[]{:S(2)}) copy-start(bf16[64,2048]{1,0:T(8,128)(2,1)} %copy-done.23) | copy-start | bytes 786436
  2158.3 135.4 %reduce-scatter.16.cloned.1.call-start = ((), (), s32[]{:S(2)}) async-start(), calls=%async_computation.24 | async-start | bytes 1179648 | tf_op jit(solution)/shard_map/reduce_scatter | solution.py:235
  2158.8 201.9 %reduce-scatter.12.cloned.1.call-start = ((), (), s32[]{:S(2)}) async-start(), calls=%async_computation.22 | async-start | bytes 1179648 | tf_op jit(solution)/shard_map/reduce_scatter | solution.py:235
  2159.4 280.0 %reduce-scatter.24.cloned.1.call-start = ((), (), s32[]{:S(2)}) async-start(), calls=%async_computation.28 | async-start | bytes 5242880 | tf_op jit(solution)/shard_map/reduce_scatter | solution.py:313
  2232.1 130.0 %copy-start.70 = (f32[8,64]{1,0:T(8,128)S(1)}, f32[8,64]{1,0:T(8,128)}, u32[]{:S(2)}) copy-start(f32[8,64]{1,0:T(8,128)} %copy-done.69) | copy-start | bytes 6148
  2232.1 130.0 %copy-start.72 = (f32[8,64]{1,0:T(8,128)S(1)}, f32[8,64]{1,0:T(8,128)}, u32[]{:S(2)}) copy-start(f32[8,64]{1,0:T(8,128)} %copy-done.71) | copy-start | bytes 6148
  2232.1 130.0 %copy-start.88 = (f32[128]{0:T(128)S(1)}, f32[128]{0:T(128)}, u32[]{:S(2)}) copy-start(f32[128]{0:T(128)} %copy-done.87) | copy-start | bytes 1540
  2232.2 287.4 %reduce-scatter.22.cloned.1.call-start = ((), (), s32[]{:S(2)}) async-start(), calls=%async_computation.27 | async-start | bytes 5242880 | tf_op jit(solution)/shard_map/reduce_scatter | solution.py:307
  2369.4 297.6 %reduce-scatter.26.cloned.1.call-start = ((), (), s32[]{:S(2)}) async-start(), calls=%async_computation.29 | async-start | bytes 10485760 | tf_op jit(solution)/shard_map/reduce_scatter | solution.py:319
  2377.3 437.8 %reduce-scatter.20.cloned.1.call-start = ((), (), s32[]{:S(2)}) async-start(), calls=%async_computation.26 | async-start | bytes 10485760 | tf_op jit(solution)/shard_map/reduce_scatter | solution.py:301
  2388.9 843.7 %reduce-scatter.30.cloned.1.call-start = ((), (), s32[]{:S(2)}) async-start(), calls=%async_computation.31 | async-start | bytes 31457280 | tf_op jit(solution)/shard_map/reduce_scatter | solution.py:340
  2402.2 1249.0 %reduce-scatter.28.cloned.1.call-start = ((), (), s32[]{:S(2)}) async-start(), calls=%async_computation.30 | async-start | bytes 31457280 | tf_op jit(solution)/shard_map/reduce_scatter | solution.py:334
  2416.2 1653.6 %reduce-scatter.32.cloned.1.call-start = ((), (), s32[]{:S(2)}) async-start(), calls=%async_computation.32 | async-start | bytes 31457280 | tf_op jit(solution)/shard_map/reduce_scatter | solution.py:346
  2430.5 1958.5 %all-reduce.12.cloned.1.call-start = ((), (), s32[]{:S(2)}) async-start(), calls=%async_computation.33 | async-start | bytes 50331648 | tf_op jit(solution)/shard_map/psum | solution.py:357
  4072.3 10.7 copy-start.14
  4072.3 23.3 slice-start
  4083.0 12.7 slice-start.1
  4083.0 12.7 copy-start.43
  4105.6 29.4 copy-start.28
  4105.6 29.4 copy-start.84
  4105.6 29.4 copy-start.94
  4105.6 30.9 copy-start.27
  4105.6 30.9 copy-start.86
  4105.6 30.9 copy-start.92
  4389.0 9.4 copy-start.26
  4389.0 15.8 slice-start.2
  (67 other events, 177.5 us)
Sparse Core Ops, SparseCore 0:
  9.6 79.6 all-gather.17
  90.9 79.2 all-gather.13
  171.8 147.9 all-gather.21
  322.4 39.2 all-gather.19
  364.3 38.9 all-gather.15
  405.9 38.9 all-gather.33
  447.7 38.9 all-gather.31
  488.2 147.5 all-gather.23
  637.4 423.3 all-gather.25
  1062.2 423.3 all-gather.27
  1487.2 423.3 all-gather.29
  2095.0 64.7 reduce-scatter.17
  2164.1 62.8 reduce-scatter.13
  2230.8 62.8 reduce-scatter.15
  2297.9 62.8 reduce-scatter.11
  2363.5 75.8 reduce-scatter.23
  2442.2 77.2 reduce-scatter.21
  2522.3 144.6 reduce-scatter.25
  2669.9 145.1 reduce-scatter.19
  2817.4 415.1 reduce-scatter.29
  3235.0 416.1 reduce-scatter.27
  3653.6 416.1 reduce-scatter.31
  4075.7 313.2 all-reduce.11
where the time goes:
time: 4440 us; the launch traced here: 4430 us
  waiting for transfers between devices  3830 us (86%)
  matrix products  413 us (9%)
  other arithmetic  63.2 us (1%)
  blocking collectives  58.1 us (1%)
    reduce_scatter x1, waiting for transfers between devices, shards(): lax.psum_scatter(over_rows(ffn_all, gate_all).astype(jnp.bfloat16), 'shar...  419 us
    reduce_scatter x1, waiting for transfers between devices, shards(): lax.psum_scatter(over_rows(inner_all, cot_all).astype(jnp.bfloat16), 'sha...  419 us
    all_gather x1, waiting for transfers between devices, feedforward_set(): lax.all_gather(w_gate, 'shard', axis=0, tiled=True)  417 us
    reduce_scatter x1, waiting for transfers between devices, shards(): lax.psum_scatter(over_rows(ffn_all, up_all).astype(jnp.bfloat16), 'shard'...  417 us
    all_gather x1, waiting for transfers between devices, feedforward_set(): lax.all_gather(w_down, 'shard', axis=0, tiled=True)  413 us
    all_gather x1, waiting for transfers between devices, feedforward_set(): lax.all_gather(w_up, 'shard', axis=0, tiled=True)  413 us
    psum x1, waiting for transfers between devices, shards(): lax.psum(totals[0].astype(jnp.bfloat16), ('rep', 'ctx')).astype(jnp.float32)  250 us
    reduce_scatter x1, waiting for transfers between devices, shards(): lax.psum_scatter(over_rows(normed_all, dq_all).astype(jnp.bfloat16), 'sha...  148 us
  transfers between devices with their start and end apart: 23, of which 23 were waited for; matrix products, arithmetic and copies ran while one was open for 7% of the time, Pallas kernels for 0%

commit v1 on v0

--- a/solution.py
+++ b/solution.py
@@ -3,6 +3,9 @@
 import jax
 import jax.numpy as jnp
 from jax import lax
+from jax.experimental import pallas as pl
+from jax.experimental.pallas import tpu as pltpu
+from jax.sharding import Mesh
 from jax.sharding import PartitionSpec as P
 
 QUERY_HEADS = 16
@@ -109,7 +112,7 @@
     return (d_queries, d_keys, d_values)
 
 
-def shards(
+def shards_general(
     tokens,
     span_starts,
     cotangent,
@@ -385,11 +388,998 @@
     )
 
 
+def from_ring(block, axis, count):
+    return [block] + [
+        lax.ppermute(block, axis, [(i, (i + k) % count) for i in range(count)])
+        for k in range(1, count)
+    ]
+
+
+def send_terms(pieces, axis, count):
+    return [pieces[0]] + [
+        lax.ppermute(
+            pieces[count - k].astype(jnp.bfloat16),
+            axis,
+            [(i, (i + k) % count) for i in range(count)],
+        )
+        for k in range(1, count)
+    ]
+
+
+def sum_terms(terms):
+    return sum(term.astype(jnp.float32) for term in terms)
+
+
+def swap(values, axis):
+    return lax.ppermute(values, axis, [(0, 1), (1, 0)])
+
+
+def after(value, *others):
+    return lax.optimization_barrier((value,) + others)[0] if others else value
+
+
+def in_order(blocks, rank):
+    count = len(blocks)
+    twice = jnp.stack(blocks[::-1] + blocks[:0:-1])
+    return lax.dynamic_slice_in_dim(twice, count - 1 - rank, count, axis=0)
+
+
+def lane_sums(values):
+    return sum(
+        values[:, start : start + 128] for start in range(0, values.shape[1], 128)
+    )
+
+
+def add_sums(step, sums_ref, values):
+    @pl.when(step == 0)
+    def _():
+        sums_ref[...] = values
+
+    @pl.when(step > 0)
+    def _():
+        sums_ref[...] += values
+
+
+def lay_in_kernel(z_ref, full_ref, gate_ref, up_ref, d_gate_ref, d_up_ref, sums_ref):
+    columns = gate_ref.shape[1] // 2
+    total = None
+    for core in range(2):
+        full = full_ref[0, core, 0, 0].astype(jnp.float32)
+        span = slice(core * columns, (core + 1) * columns)
+        d_gate = full[:, :columns]
+        d_up = full[:, columns:]
+        d_gate_ref[:, span] = d_gate
+        d_up_ref[:, span] = d_up
+        both = d_gate * gate_ref[:, span].astype(jnp.float32)
+        both = lane_sums(both + d_up * up_ref[:, span].astype(jnp.float32))
+        total = both if total is None else total + both
+    add_sums(pl.program_id(1), sums_ref, total)
+
+
+def lay_in(rank, full, w_gate, w_up):
+    n_hi, _, n_ctx, n_shard, rows, both = full.shape
+    shape = jax.ShapeDtypeStruct(w_gate.shape, jnp.float32)
+    block = pl.BlockSpec((rows, both), lambda i, j, z: (i, (z[0] - j + n_shard) % n_shard))
+    return pl.pallas_call(
+        lay_in_kernel,
+        grid_spec=pltpu.PrefetchScalarGridSpec(
+            num_scalar_prefetch=1,
+            grid=(n_hi * n_ctx, n_shard),
+            in_specs=[
+                pl.BlockSpec(
+                    (1, 2, 1, 1, rows, both),
+                    lambda i, j, z: (i // n_ctx, 0, i % n_ctx, j, 0, 0),
+                ),
+                block,
+                block,
+            ],
+            out_specs=[block, block, pl.BlockSpec((rows, 128), lambda i, j, z: (i, 0))],
+        ),
+        out_shape=[shape, shape, jax.ShapeDtypeStruct((w_gate.shape[0], 128), jnp.float32)],
+        compiler_params=pltpu.CompilerParams(vmem_limit_bytes=40 << 20),
+        name="lay_in",
+    )(rank.reshape(1), full, w_gate, w_up)
+
+
+def lay_rows_kernel(full_ref, out_ref):
+    out_ref[...] = full_ref[...].reshape(out_ref.shape).astype(jnp.float32)
+
+
+def lay_rows(full):
+    n_hi, _, n_ctx, rows, columns = full.shape
+    n_part = n_hi * n_ctx
+    return pl.pallas_call(
+        lay_rows_kernel,
+        grid=(2, n_part),
+        in_specs=[
+            pl.BlockSpec(
+                (1, 1, 1, rows, columns), lambda i, j: (j // n_ctx, i, j % n_ctx, 0, 0)
+            )
+        ],
+        out_specs=pl.BlockSpec((rows, columns), lambda i, j: (i * n_part + j, 0)),
+        out_shape=jax.ShapeDtypeStruct((2 * n_part * rows, columns), jnp.float32),
+        name="lay_rows",
+    )(full)
+
+
+def lay_heads_kernel(count, at_ref, *refs):
+    mine, theirs = refs[:count], refs[count : 2 * count]
+    wq_ref, wk_ref, wv_ref, dq_ref, dk_ref, dv_ref, d_out_ref, sums_ref = refs[2 * count :]
+    q_cols, kv_cols = wq_ref.shape[1] // 2, wk_ref.shape[1] // 2
+    out_rows = d_out_ref.shape[0] // 2
+    rows = mine[0].shape[1]
+
+    @pl.when(pl.program_id(0) == 0)
+    def _():
+        sums_ref[...] = jnp.zeros_like(sums_ref)
+
+    for k in range(count):
+        part = lax.rem(at_ref[0] - k + count, count)
+        here = pl.ds(pl.multiple_of(part * rows, rows), rows)
+        total = sums_ref[here, :]
+        for core, full_ref in ((at_ref[1], mine[k]), (1 - at_ref[1], theirs[k])):
+            full = full_ref[0].astype(jnp.float32)
+            start = 0
+            for weight_ref, grad_ref, columns in (
+                (wq_ref, dq_ref, q_cols),
+                (wk_ref, dk_ref, kv_cols),
+                (wv_ref, dv_ref, kv_cols),
+            ):
+                grad = full[:, start : start + columns]
+                span = pl.ds(pl.multiple_of(core * columns, 128), columns)
+                grad_ref[here, span] = grad
+                total += lane_sums(grad * weight_ref[here, span].astype(jnp.float32))
+                start += columns
+            d_out_ref[pl.ds(pl.multiple_of(core * out_rows, 128), out_rows), here] = full[
+                :, start:
+            ].T
+        sums_ref[here, :] = total
+
+
+def lay_heads(at, mine, theirs, w_query, key_weight, value_weight):
+    n_part = len(mine)
+    n_shard, rows, columns = mine[0].shape
+    q_cols = w_query.shape[1] // n_shard
+    kv_cols = key_weight.shape[1] // n_shard
+    out_rows = 2 * columns - q_cols - 2 * kv_cols
+    block = pl.BlockSpec((1, rows, columns), lambda j, at: (j, 0, 0))
+
+    def spec(width):
+        return pl.BlockSpec(
+            (n_part * rows, width), lambda j, at: (0, lax.rem(at[2] - j + n_shard, n_shard))
+        )
+
+    return pl.pallas_call(
+        partial(lay_heads_kernel, n_part),
+        grid_spec=pltpu.PrefetchScalarGridSpec(
+            num_scalar_prefetch=1,
+            grid=(n_shard,),
+            in_specs=[block] * (2 * n_part) + [spec(q_cols), spec(kv_cols), spec(kv_cols)],
+            out_specs=[
+                spec(q_cols),
+                spec(kv_cols),
+                spec(kv_cols),
+                pl.BlockSpec((out_rows, n_part * rows), lambda j, at: (0, j)),
+                pl.BlockSpec((n_part * rows, 128), lambda j, at: (0, 0)),
+            ],
+        ),
+        out_shape=[
+            jax.ShapeDtypeStruct(w_query.shape, jnp.float32),
+            jax.ShapeDtypeStruct(key_weight.shape, jnp.float32),
+            jax.ShapeDtypeStruct(value_weight.shape, jnp.float32),
+            jax.ShapeDtypeStruct((out_rows, n_shard * n_part * rows), jnp.float32),
+            jax.ShapeDtypeStruct((n_part * rows, 128), jnp.float32),
+        ],
+        compiler_params=pltpu.CompilerParams(vmem_limit_bytes=48 << 20),
+        name="lay_heads",
+    )(at, *mine, *theirs, w_query, key_weight, value_weight)
+
+
+def exchange_ring(pieces, rank, count):
+    def piece_for(k):
+        return lax.dynamic_index_in_dim(pieces, (rank + k) % count, axis=0, keepdims=False)
+
+    return [piece_for(0)] + [
+        lax.ppermute(piece_for(k), "shard", [(i, (i + k) % count) for i in range(count)])
+        for k in range(1, count)
+    ]
+
+
+def take_columns_kernel(at_ref, *refs):
+    out_ref = refs[-1]
+    start = 0
+    for ref in refs[:-1]:
+        columns = ref.shape[1]
+        out_ref[0, :, start : start + columns] = ref[...]
+        start += columns
+
+
+def take_columns(at, n_part, n_shard, weights):
+    rows = weights[0].shape[0] // n_part
+    widths = [weight.shape[1] // (2 * n_shard) for weight in weights]
+    return pl.pallas_call(
+        take_columns_kernel,
+        grid_spec=pltpu.PrefetchScalarGridSpec(
+            num_scalar_prefetch=1,
+            grid=(n_shard,),
+            in_specs=[
+                pl.BlockSpec((rows, width), lambda j, at: (at[0], 2 * j + at[1]))
+                for width in widths
+            ],
+            out_specs=pl.BlockSpec((1, rows, sum(widths)), lambda j, at: (j, 0, 0)),
+        ),
+        out_shape=jax.ShapeDtypeStruct((n_shard, rows, sum(widths)), weights[0].dtype),
+        name="take_columns",
+    )(at, *weights)
+
+
+def lay_order_kernel(at_ref, *refs):
+    out_ref = refs[-1]
+    count = len(refs) - 1
+    rows = refs[0].shape[1]
+    for k, ref in enumerate(refs[:-1]):
+        owner = lax.rem(at_ref[0] - k + count, count)
+        out_ref[pl.ds(pl.multiple_of(owner * rows, rows), rows), :] = ref[0]
+
+
+def lay_order(at, pieces):
+    n_shard, rows, columns = pieces[0].shape
+    block = len(pieces) * rows
+    return pl.pallas_call(
+        lay_order_kernel,
+        grid_spec=pltpu.PrefetchScalarGridSpec(
+            num_scalar_prefetch=1,
+            grid=(n_shard,),
+            in_specs=[pl.BlockSpec((1, rows, columns), lambda j, at: (j, 0, 0))] * len(pieces),
+            out_specs=pl.BlockSpec((block, columns), lambda j, at: (j, 0)),
+        ),
+        out_shape=jax.ShapeDtypeStruct((n_shard * block, columns), pieces[0].dtype),
+        name="lay_order",
+    )(at, *pieces)
+
+
+def norm_kernel(z_ref, tokens_ref, gain_ref, out_ref):
+    values = tokens_ref[0].astype(jnp.float32)
+    out_ref[...] = (values * recip_rms(values) * gain_ref[...]).astype(jnp.bfloat16)
+
+
+def norm_group(rank, gathered, gain):
+    count, rows, width = gathered.shape
+    return pl.pallas_call(
+        norm_kernel,
+        grid_spec=pltpu.PrefetchScalarGridSpec(
+            num_scalar_prefetch=1,
+            grid=(count,),
+            in_specs=[
+                pl.BlockSpec(
+                    (1, rows, width), lambda k, z: (lax.rem(z[0] - k + count, count), 0, 0)
+                ),
+                pl.BlockSpec((1, width), lambda k, z: (0, 0)),
+            ],
+            out_specs=pl.BlockSpec((rows, width), lambda k, z: (k, 0)),
+        ),
+        out_shape=jax.ShapeDtypeStruct((count * rows, width), jnp.bfloat16),
+        name="norm_group",
+    )(rank.reshape(1), gathered, gain.reshape(1, width))
+
+
+def turn(values, table):
+    return pltpu.roll(values, HEAD_SIZE // 2, 1) * table
+
+
+def project_kernel(n_part, q_cols, at_ref, *refs):
+    tokens = refs[:n_part]
+    pieces = refs[n_part : 2 * n_part]
+    cos_ref, sin_ref, gain_q_ref, gain_k_ref, queries_ref, kv_ref, pre_ref, acc_ref = refs[
+        2 * n_part :
+    ]
+    step = pl.program_id(0)
+    columns = acc_ref.shape[1]
+    kv_cols = (columns - q_cols) // 2
+    total = sum(
+        jnp.dot(block[...], piece[0], preferred_element_type=jnp.float32)
+        for block, piece in zip(tokens, pieces)
+    )
+    add_sums(step, acc_ref, total)
+
+    @pl.when(step == pl.num_programs(0) - 1)
+    def _():
+        rows = 64
+
+        def body(chunk, carry):
+            span = pl.ds(pl.multiple_of(chunk * rows, rows), rows)
+            cosine, sine = cos_ref[span, :], sin_ref[span, :]
+            for start in range(0, q_cols + kv_cols, HEAD_SIZE):
+                values = acc_ref[span, start : start + HEAD_SIZE]
+                pre_ref[span, start : start + HEAD_SIZE] = values
+                gain = gain_q_ref[...] if start < q_cols else gain_k_ref[...]
+                scaled = values * recip_rms(values) * gain
+                turned = (scaled * cosine + turn(scaled, sine)).astype(jnp.bfloat16)
+                if start < q_cols:
+                    queries_ref[span, start : start + HEAD_SIZE] = turned
+                else:
+                    kv_ref[span, start - q_cols : start - q_cols + HEAD_SIZE] = turned
+            kv_ref[span, kv_cols:] = acc_ref[span, q_cols + kv_cols :].astype(jnp.bfloat16)
+            return carry
+
+        lax.fori_loop(0, acc_ref.shape[0] // rows, body, 0)
+
+
+def project(at, q_cols, tokens, pieces, cosine, sine, gain_q, gain_k):
+    n_part = len(pieces)
+    n_shard, slice_rows, columns = pieces[0].shape
+    group, width = tokens.shape
+    kv_cols = (columns - q_cols) // 2
+
+    def token_spec(k):
+        return pl.BlockSpec(
+            (group, slice_rows),
+            lambda j, at: (0, j * n_part + lax.rem(at[0] - k + n_part, n_part)),
+        )
+
+    def whole(shape):
+        return pl.BlockSpec(shape, lambda j, at: (0, 0))
+
+    head = (1, HEAD_SIZE)
+    return pl.pallas_call(
+        partial(project_kernel, n_part, q_cols),
+        grid_spec=pltpu.PrefetchScalarGridSpec(
+            num_scalar_prefetch=1,
+            grid=(n_shard,),
+            in_specs=[token_spec(k) for k in range(n_part)]
+            + [pl.BlockSpec((1, slice_rows, columns), lambda j, at: (j, 0, 0))] * n_part
+            + [whole(cosine.shape), whole(sine.shape), whole(head), whole(head)],
+            out_specs=[
+                whole((group, q_cols)),
+                whole((group, 2 * kv_cols)),
+                whole((group, q_cols + kv_cols)),
+            ],
+            scratch_shapes=[pltpu.VMEM((group, columns), jnp.float32)],
+        ),
+        out_shape=[
+            jax.ShapeDtypeStruct((group, q_cols), jnp.bfloat16),
+            jax.ShapeDtypeStruct((group, 2 * kv_cols), jnp.bfloat16),
+            jax.ShapeDtypeStruct((group, q_cols + kv_cols), jnp.float32),
+        ],
+        compiler_params=pltpu.CompilerParams(vmem_limit_bytes=48 << 20),
+        name="project",
+    )(
+        at,
+        *([tokens] * n_part),
+        *pieces,
+        cosine,
+        sine,
+        gain_q.reshape(head),
+        gain_k.reshape(head),
+    )
+
+
+def head_probs(start, q_pos_ref, k_pos_ref, query, keys):
+    scores = [
+        lax.dot_general(
+            query, key, (((1,), (1,)), ((), ())), preferred_element_type=jnp.float32
+        )
+        for key in keys
+    ]
+    scores = jnp.concatenate(scores, axis=1) * HEAD_SIZE ** (-0.5)
+    q_pos, k_pos = q_pos_ref[...], k_pos_ref[...]
+    inside_q = (q_pos >= start) & (q_pos < start + PIC)
+    inside_k = (k_pos >= start) & (k_pos < start + PIC)
+    allowed = (k_pos <= q_pos) | (inside_q & inside_k)
+    scores = jnp.where(allowed, scores, -1e30)
+    powers = jnp.exp(scores - jnp.max(scores, axis=1, keepdims=True))
+    return powers / jnp.sum(powers, axis=1, keepdims=True)
+
+
+def attend_kernel(n_ctx, core, starts_ref, *refs):
+    kv_refs = refs[:n_ctx]
+    queries_ref, q_pos_ref, k_pos_ref, mixed_ref = refs[n_ctx:]
+    block = queries_ref.shape
+    tokens = block[1] * block[3]
+    start = starts_ref[core, pl.program_id(0)]
+    queries = queries_ref[...].reshape(tokens, block[4])
+    kv = [ref[...].reshape(tokens, ref.shape[4]) for ref in kv_refs]
+    kv_cols = kv[0].shape[1] // 2
+    group_width = block[4] // kv_cols
+    out = []
+    for head in range(block[4] // HEAD_SIZE):
+        key_start = head // group_width * HEAD_SIZE
+        query = queries[:, head * HEAD_SIZE : (head + 1) * HEAD_SIZE]
+        keys = [part[:, key_start : key_start + HEAD_SIZE] for part in kv]
+        values = [
+            part[:, kv_cols + key_start : kv_cols + key_start + HEAD_SIZE] for part in kv
+        ]
+        probs = head_probs(start, q_pos_ref, k_pos_ref, query, keys).astype(jnp.bfloat16)
+        mixed = sum(
+            jnp.dot(
+                probs[:, i * tokens : (i + 1) * tokens], part, preferred_element_type=jnp.float32
+            )
+            for i, part in enumerate(values)
+        )
+        out.append(mixed.astype(jnp.bfloat16))
+    mixed_ref[...] = jnp.concatenate(out, axis=1).reshape(mixed_ref.shape)
+
+
+def sequence_view(values, count, micro, rows):
+    return values.reshape(1, count, micro, rows, values.shape[-1])
+
+
+def attend(core, starts, count, micro, rows, queries, kv_parts, q_pos, k_pos):
+    n_ctx = len(kv_parts)
+
+    def spec(columns):
+        return pl.BlockSpec((1, count, 1, rows, columns), lambda m, s: (0, 0, m, 0, 0))
+
+    view = partial(sequence_view, count=count, micro=micro, rows=rows)
+    columns = queries.shape[1]
+    mixed = pl.pallas_call(
+        partial(attend_kernel, n_ctx, core),
+        grid_spec=pltpu.PrefetchScalarGridSpec(
+            num_scalar_prefetch=1,
+            grid=(micro,),
+            in_specs=[spec(kv_parts[0].shape[1])] * n_ctx
+            + [
+                spec(columns),
+                pl.BlockSpec(q_pos.shape, lambda m, s: (0, 0)),
+                pl.BlockSpec(k_pos.shape, lambda m, s: (0, 0)),
+            ],
+            out_specs=spec(columns),
+        ),
+        out_shape=jax.ShapeDtypeStruct(view(queries).shape, jnp.bfloat16),
+        compiler_params=pltpu.CompilerParams(vmem_limit_bytes=48 << 20),
+        name="attend",
+    )(starts, *[view(part) for part in kv_parts], view(queries), q_pos, k_pos)
+    return mixed.reshape(queries.shape)
+
+
+def norm_turn_back(pre, d_turned, cosine, sine, gain):
+    recip = recip_rms(pre)
+    unit = pre * recip
+    d_unit = d_turned * cosine + pltpu.roll(d_turned * sine, HEAD_SIZE // 2, 1)
+    d_gain = jnp.sum(d_unit * unit, axis=0, keepdims=True)
+    return norm_back(unit, recip, gain, d_unit), d_gain
+
+
+def attend_back_kernel(n_ctx, core, starts_ref, *refs):
+    kv_refs = refs[:n_ctx]
+    queries_ref, pre_ref, d_mixed_ref, q_pos_ref, k_pos_ref, cos_ref, sin_ref, gain_ref = refs[
+        n_ctx : n_ctx + 8
+    ]
+    d_queries_ref, sums_ref = refs[n_ctx + 8 : n_ctx + 10]
+    d_kv_refs = refs[n_ctx + 10 :]
+    block = queries_ref.shape
+    tokens = block[1] * block[3]
+    start = starts_ref[core, pl.program_id(0)]
+    queries = queries_ref[...].reshape(tokens, block[4])
+    d_mixed = d_mixed_ref[...].reshape(tokens, block[4])
+    pre = pre_ref[...].reshape(tokens, pre_ref.shape[4])
+    kv = [ref[...].reshape(tokens, ref.shape[4]) for ref in kv_refs]
+    kv_cols = kv[0].shape[1] // 2
+    group_width = block[4] // kv_cols
+    scale = HEAD_SIZE ** (-0.5)
+    down = (((0,), (0,)), ((), ()))
+    across = (((1,), (1,)), ((), ()))
+    f32 = jnp.float32
+    d_queries, sums = [], 0.0
+    d_keys, d_values = {}, {}
+    for head in range(block[4] // HEAD_SIZE):
+        key_start = head // group_width * HEAD_SIZE
+        span = slice(head * HEAD_SIZE, (head + 1) * HEAD_SIZE)
+        query, d_mix = queries[:, span], d_mixed[:, span]
+        keys = [part[:, key_start : key_start + HEAD_SIZE] for part in kv]
+        values = [
+            part[:, kv_cols + key_start : kv_cols + key_start + HEAD_SIZE] for part in kv
+        ]
+        probs = head_probs(start, q_pos_ref, k_pos_ref, query, keys)
+        d_probs = jnp.concatenate(
+            [lax.dot_general(d_mix, part, across, preferred_element_type=f32) for part in values],
+            axis=1,
+        )
+        row_dot = jnp.sum(probs * d_probs, axis=1, keepdims=True)
+        d_scores = (probs * (d_probs - row_dot)).astype(jnp.bfloat16)
+        probs_low = probs.astype(jnp.bfloat16)
+        d_query = 0.0
+        for i, key in enumerate(keys):
+            piece = slice(i * tokens, (i + 1) * tokens)
+            d_query += jnp.dot(d_scores[:, piece], key, preferred_element_type=f32)
+            d_key = lax.dot_general(d_scores[:, piece], query, down, preferred_element_type=f32)
+            d_value = lax.dot_general(
+                probs_low[:, piece], d_mix, down, preferred_element_type=f32
+            )
+            at = (i, key_start)
+            d_keys[at] = d_keys.get(at, 0.0) + d_key * scale
+            d_values[at] = d_values.get(at, 0.0) + d_value
+        d_pre, d_gain = norm_turn_back(
+            pre[:, span],
+            d_query * scale,
+            cos_ref[...].reshape(tokens, HEAD_SIZE),
+            sin_ref[...].reshape(tokens, HEAD_SIZE),
+            gain_ref[...],
+        )
+        d_queries.append(d_pre.astype(jnp.bfloat16))
+        sums += d_gain
+    d_queries_ref[...] = jnp.concatenate(d_queries, axis=1).reshape(d_queries_ref.shape)
+    for i, ref in enumerate(d_kv_refs):
+        parts = [d_keys[at] for at in sorted(d_keys) if at[0] == i]
+        parts += [d_values[at] for at in sorted(d_values) if at[0] == i]
+        ref[...] = jnp.concatenate(parts, axis=1).astype(ref.dtype).reshape(ref.shape)
+    add_sums(pl.program_id(0), sums_ref, jnp.broadcast_to(sums, sums_ref.shape))
+
+
+def attend_back(
+    core, starts, count, micro, rows, queries, pre, kv_parts, d_mixed, q_pos, k_pos, cosine, sine, gain
+):
+    n_ctx = len(kv_parts)
+    view = partial(sequence_view, count=count, micro=micro, rows=rows)
+
+    def spec(columns):
+        return pl.BlockSpec((1, count, 1, rows, columns), lambda m, s: (0, 0, m, 0, 0))
+
+    def whole(values):
+        return pl.BlockSpec(values.shape, lambda m, s: (0, 0))
+
+    columns, kv_columns = queries.shape[1], kv_parts[0].shape[1]
+    gain = gain.reshape(1, HEAD_SIZE)
+    view_shape = view(d_mixed).shape
+    outs = pl.pallas_call(
+        partial(attend_back_kernel, n_ctx, core),
+        grid_spec=pltpu.PrefetchScalarGridSpec(
+            num_scalar_prefetch=1,
+            grid=(micro,),
+            in_specs=[spec(kv_columns)] * n_ctx
+            + [spec(columns), spec(pre.shape[1]), spec(columns)]
+            + [whole(q_pos), whole(k_pos), spec(HEAD_SIZE), spec(HEAD_SIZE), whole(gain)],
+            out_specs=[spec(columns), pl.BlockSpec((8, HEAD_SIZE), lambda m, s: (0, 0))]
+            + [spec(kv_columns)] * n_ctx,
+        ),
+        out_shape=[
+            jax.ShapeDtypeStruct(view_shape, jnp.bfloat16),
+            jax.ShapeDtypeStruct((8, HEAD_SIZE), jnp.float32),
+        ]
+        + [
+            jax.ShapeDtypeStruct(
+                view_shape[:-1] + (kv_columns,), jnp.float32 if i == 0 else jnp.bfloat16
+            )
+            for i in range(n_ctx)
+        ],
+        compiler_params=pltpu.CompilerParams(vmem_limit_bytes=48 << 20),
+        name="attend_back",
+    )(
+        starts,
+        *[view(part) for part in kv_parts],
+        view(queries),
+        view(pre),
+        view(d_mixed),
+        q_pos,
+        k_pos,
+        view(cosine),
+        view(sine),
+        gain,
+    )
+    flat = [values.reshape(d_mixed.shape[0], -1) for values in outs[:1] + outs[2:]]
+    return flat[0], outs[1][0], flat[1:]
+
+
+def keys_back_kernel(n_got, q_cols, *refs):
+    d_q_ref, own_ref = refs[:2]
+    got_refs = refs[2 : 2 + n_got]
+    pre_ref, cos_ref, sin_ref, gain_ref, out_ref, sums_ref = refs[2 + n_got :]
+    total = own_ref[...]
+    for ref in got_refs:
+        total += ref[...].astype(jnp.float32)
+    kv_cols = total.shape[1] // 2
+    out_ref[:, :q_cols] = d_q_ref[...]
+    out_ref[:, q_cols + kv_cols :] = total[:, kv_cols:].astype(jnp.bfloat16)
+    sums = 0.0
+    for start in range(0, kv_cols, HEAD_SIZE):
+        span = slice(start, start + HEAD_SIZE)
+        at = slice(q_cols + start, q_cols + start + HEAD_SIZE)
+        d_pre, d_gain = norm_turn_back(
+            pre_ref[:, at], total[:, span], cos_ref[...], sin_ref[...], gain_ref[...]
+        )
+        out_ref[:, at] = d_pre.astype(jnp.bfloat16)
+        sums += d_gain
+    sums_ref[...] = jnp.broadcast_to(sums, sums_ref.shape)
+
+
+def keys_back(d_queries, own, got, pre, cosine, sine, gain):
+    rows, q_cols = d_queries.shape
+    out, sums = pl.pallas_call(
+        partial(keys_back_kernel, len(got), q_cols),
+        out_shape=[
+            jax.ShapeDtypeStruct((rows, q_cols + own.shape[1]), jnp.bfloat16),
+            jax.ShapeDtypeStruct((8, HEAD_SIZE), jnp.float32),
+        ],
+        name="keys_back",
+    )(d_queries, own, *got, pre, cosine, sine, gain.reshape(1, HEAD_SIZE))
+    return out, sums[0]
+
+
+def head_gradients_kernel(count, at_ref, *refs):
+    normed, branch = refs[: 2 * count], refs[2 * count : 4 * count]
+    d_qkv, mixed = refs[4 * count : 4 * count + 2], refs[4 * count + 2 : 4 * count + 4]
+    down = (((0,), (0,)), ((), ()))
+    for k, out_ref in enumerate(refs[4 * count + 4 :]):
+        split = d_qkv[0].shape[1]
+        for columns, left, right in (
+            (slice(0, split), normed, d_qkv),
+            (slice(split, out_ref.shape[2]), branch, mixed),
+        ):
+            out_ref[0, :, columns] = sum(
+                lax.dot_general(
+                    left[core * count + k][...],
+                    right[core][...],
+                    down,
+                    preferred_element_type=jnp.float32,
+                )
+                for core in range(2)
+            ).astype(jnp.bfloat16)
+
+
+def head_gradients(at, n_part, n_shard, normed, d_branch, d_qkv, mixed):
+    rows, width = normed[0].shape
+    slice_rows = width // (n_part * n_shard)
+    columns = d_qkv[0].shape[1] + mixed[0].shape[1]
+
+    def spec(k):
+        return pl.BlockSpec(
+            (rows, slice_rows),
+            lambda j, at: (0, j * n_part + lax.rem(at[0] - k + n_part, n_part)),
+        )
+
+    def whole(values):
+        return pl.BlockSpec(values.shape, lambda j, at: (0, 0))
+
+    specs = [spec(k) for k in range(n_part)] * 2
+    out = pl.BlockSpec((1, slice_rows, columns), lambda j, at: (j, 0, 0))
+    return pl.pallas_call(
+        partial(head_gradients_kernel, n_part),
+        grid_spec=pltpu.PrefetchScalarGridSpec(
+            num_scalar_prefetch=1,
+            grid=(n_shard,),
+            in_specs=specs + specs + [whole(values) for values in d_qkv + mixed],
+            out_specs=[out] * n_part,
+        ),
+        out_shape=[jax.ShapeDtypeStruct((n_shard, slice_rows, columns), jnp.bfloat16)] * n_part,
+        compiler_params=pltpu.CompilerParams(vmem_limit_bytes=48 << 20),
+        name="head_gradients",
+    )(
+        at,
+        *[normed[0]] * n_part,
+        *[normed[1]] * n_part,
+        *[d_branch[0]] * n_part,
+        *[d_branch[1]] * n_part,
+        *d_qkv,
+        *mixed,
+    )
+
+
+def reorder_kernel(z_ref, in_ref, out_ref):
+    out_ref[...] = in_ref[0]
+
+
+def ring_order(rank, gathered):
+    count, rows, width = gathered.shape
+    return pl.pallas_call(
+        reorder_kernel,
+        grid_spec=pltpu.PrefetchScalarGridSpec(
+            num_scalar_prefetch=1,
+            grid=(count,),
+            in_specs=[
+                pl.BlockSpec(
+                    (1, rows, width), lambda k, z: (lax.rem(z[0] - k + count, count), 0, 0)
+                )
+            ],
+            out_specs=pl.BlockSpec((rows, width), lambda k, z: (k, 0)),
+        ),
+        out_shape=jax.ShapeDtypeStruct((count * rows, width), gathered.dtype),
+        name="ring_order",
+    )(rank.reshape(1), gathered)
+
+
+def inner_kernel(ffn_ref, gate_ref, up_ref, d_inner_ref, inner_ref, d_gate_ref, d_up_ref):
+    ffn = ffn_ref[...]
+    gate_pre = jnp.dot(ffn, gate_ref[...], preferred_element_type=jnp.float32)
+    up_pre = jnp.dot(ffn, up_ref[...], preferred_element_type=jnp.float32)
+    d_inner = d_inner_ref[...]
+    sigma = jax.nn.sigmoid(gate_pre)
+    act_gate = gate_pre * sigma
+    inner_ref[...] = (act_gate * up_pre).astype(jnp.bfloat16)
+    d_gate = d_inner * up_pre * sigma * (1.0 + gate_pre * (1.0 - sigma))
+    d_gate_ref[...] = d_gate.astype(jnp.bfloat16)
+    d_up_ref[...] = (d_inner * act_gate).astype(jnp.bfloat16)
+
+
+def inner_parts(ffn_in, w_in, d_inner):
+    rows, width = ffn_in.shape
+    ff = w_in.shape[1] // 2
+    block = 256 if ff % 256 == 0 else 128
+    steps = ff // block
+    out = pl.BlockSpec((rows, block), lambda j: (0, j))
+    shape = jax.ShapeDtypeStruct((rows, ff), jnp.bfloat16)
+    return pl.pallas_call(
+        inner_kernel,
+        grid=(steps,),
+        in_specs=[
+            pl.BlockSpec((rows, width), lambda j: (0, 0)),
+            pl.BlockSpec((width, block), lambda j: (0, j)),
+            pl.BlockSpec((width, block), lambda j: (0, steps + j)),
+            out,
+        ],
+        out_specs=[out, out, out],
+        out_shape=[shape, shape, shape],
+        compiler_params=pltpu.CompilerParams(vmem_limit_bytes=48 << 20),
+        name="inner_parts",
+    )(ffn_in, w_in, w_in, d_inner)
+
+
+def grouped_shards(
+    n_hi,
+    n_shard,
+    n_ctx,
+    tokens,
+    span_starts,
+    cotangent,
+    w_query,
+    key_weight,
+    value_weight,
+    w_out,
+    attn_gain,
+    query_gain,
+    key_gain,
+    w_gate,
+    w_up,
+    w_down,
+    ffn_gain,
+):
+    bf16 = jnp.bfloat16
+    f32 = jnp.float32
+    z = lax.axis_index("shard")
+    x = lax.axis_index("ctx")
+    c = lax.axis_index("core")
+    part = lax.axis_index(("hi", "ctx"))
+    n_part = n_hi * n_ctx
+    micro, _, rows, width = tokens.shape
+    own = micro * rows
+    group = n_shard * own
+    n_tp = 2 * n_shard
+    kv_local = KEY_VALUE_HEADS // n_tp
+    q_local = QUERY_HEADS // n_tp
+    group_width = QUERY_HEADS // KEY_VALUE_HEADS
+    q_cols = q_local * HEAD_SIZE
+    kv_cols = kv_local * HEAD_SIZE
+    ff = w_down.shape[0] // 2
+
+    slice_rows = w_query.shape[0] // n_part
+    plain = (((1,), (0,)), ((), ()))
+    turned = (((1,), (1,)), ((), ()))
+
+    def product(left, right, dims):
+        return lax.dot_general(left, right, dims, preferred_element_type=f32)
+
+    def exchange(pieces):
+        return lax.all_to_all(pieces, "shard", 0, 0, tiled=True)
+
+    def gather_plane(values):
+        full = lax.all_gather(values, ("hi", "core", "ctx"), axis=0)
+        return full.reshape((n_hi, 2, n_ctx) + values.shape)
+
+    def send_blocks(mine):
+        return [mine[k * own : (k + 1) * own] for k in range(n_shard)]
+
+    own_tokens = tokens.reshape(own, width)
+    own_cot = cotangent.reshape(own, width)
+    at = jnp.stack([part, c, z])
+    gathered = lax.all_gather(own_tokens, "shard", axis=0)
+    pieces_qkv = take_columns(at, n_part, n_shard, (w_query, key_weight, value_weight))
+    pieces_in = take_columns(at, n_part, n_shard, (w_gate, w_up))
+    got_qkv = after(exchange(pieces_qkv), pieces_in)
+    w_out_rows = lax.dynamic_slice_in_dim(w_out, c * q_cols, q_cols, axis=0)
+    w_down_rows = lax.dynamic_slice_in_dim(w_down, c * ff, ff, axis=0)
+    gain_sizes = (attn_gain.shape[0], query_gain.shape[0], key_gain.shape[0], ffn_gain.shape[0])
+    gains = after(jnp.concatenate([attn_gain, query_gain, key_gain, ffn_gain]), got_qkv)
+    gains = in_order(from_ring(gains, "shard", n_shard), z).astype(f32)
+    starts = after(span_starts.reshape(micro), got_qkv)
+    starts = jnp.stack([starts, swap(starts, "core")])
+    ring_qkv = from_ring(got_qkv, ("hi", "ctx"), n_part)
+    gathered = after(gathered, ring_qkv, gains, starts)
+    ends = [0]
+    for size in gain_sizes:
+        ends.append(ends[-1] + size)
+    gain_attn, gain_query, gain_key, gain_ffn = [
+        gains[:, ends[i] : ends[i + 1]].reshape(-1) for i in range(4)
+    ]
+
+    blocks = jnp.arange(n_shard, dtype=jnp.int32)
+    owners = (z - blocks) % n_shard
+
+    def positions(ctx_rank):
+        start = (owners * n_ctx + ctx_rank) * rows
+        return (start[:, None] + jnp.arange(rows, dtype=jnp.int32)[None, :]).reshape(-1)
+
+    query_pos = positions(x)
+    key_pos = jnp.concatenate([positions((x - k) % n_ctx) for k in range(n_ctx)])
+    cosine, sine = (table[:, 0, :] for table in spin_tables(query_pos))
+    sine = jnp.where(jnp.arange(HEAD_SIZE) < HEAD_SIZE // 2, -1.0, 1.0) * sine
+
+    def by_row(table):
+        table = table.reshape(n_shard, 1, rows, HEAD_SIZE)
+        return jnp.broadcast_to(table, (n_shard, micro, rows, HEAD_SIZE)).reshape(group, HEAD_SIZE)
+
+    cosine, sine = by_row(cosine), by_row(sine)
+    query_pos = query_pos[:, None]
+    key_pos = key_pos[None, :]
+    order = (n_shard, micro, rows)
+
+    normed_mine = norm_group(z, gathered, gain_attn)
+    normed_theirs = swap(normed_mine, "core")
+    got_in = exchange_ring(after(pieces_in, gathered), z, n_shard)
+    cot_all = lax.all_gather(after(own_cot, gathered), "shard", axis=0)
+    turns = (cosine, sine, gain_query, gain_key)
+    q_mine, kv_mine, pre_mine = project(at, q_cols, normed_mine, ring_qkv, *turns)
+    kv_mine_parts = from_ring(kv_mine, "ctx", n_ctx)
+    q_theirs, kv_theirs, pre_theirs = project(
+        at, q_cols, after(normed_theirs, kv_mine), ring_qkv, *turns
+    )
+    kv_theirs_parts = from_ring(kv_theirs, "ctx", n_ctx)
+    w_qkv = lay_order(at, after(ring_qkv, kv_theirs))
+    mixed_mine = attend(
+        0, starts, *order, after(q_mine, w_qkv), kv_mine_parts, query_pos, key_pos
+    )
+    mixed_theirs = attend(
+        1, starts, *order, after(q_theirs, mixed_mine), kv_theirs_parts, query_pos, key_pos
+    )
+    got_in = in_order(after(got_in, mixed_theirs), z)
+    w_in = lax.all_gather(after(got_in, cot_all), ("hi", "ctx"), axis=1, tiled=True)
+    w_in = w_in.reshape(width, -1)
+
+    def core_sum(mine, theirs, right, dims):
+        sent = product(theirs, right, dims).astype(bf16)
+        kept = product(after(mine, sent), right, dims)
+        return kept + after(swap(sent, "core"), kept).astype(f32)
+
+    branch = core_sum(mixed_mine, mixed_theirs, w_out_rows, plain)
+    hidden_in = own_tokens.astype(f32)
+    branch_sent = send_blocks(branch)
+    cot_mine = ring_order(z, after(cot_all, branch))
+    cot_theirs = swap(cot_mine, "core")
+    branch_terms = send_terms(branch_sent, "shard", n_shard)
+    middle = hidden_in + sum_terms(after(branch_terms, w_in, cot_mine))
+
+    recip_m = recip_rms(middle)
+    unit_m = middle * recip_m
+    ffn_own = (unit_m * gain_ffn).astype(bf16)
+    ffn_ring = from_ring(ffn_own, "shard", n_shard)
+    d_inner_mine = product(after(cot_mine, ffn_own), w_down_rows, turned)
+    d_inner_theirs = product(after(cot_theirs, d_inner_mine), w_down_rows, turned)
+    ffn_mine = jnp.concatenate(after(ffn_ring, d_inner_theirs), axis=0)
+    ffn_theirs = swap(ffn_mine, "core")
+    inner_mine, d_gate_mine, d_up_mine = inner_parts(ffn_mine, w_in, d_inner_mine)
+    inner_theirs, d_gate_theirs, d_up_theirs = inner_parts(
+        after(ffn_theirs, inner_mine), w_in, d_inner_theirs
+    )
+    d_pre_mine = jnp.concatenate([d_gate_mine, d_up_mine], axis=1)
+    d_pre_theirs = jnp.concatenate([d_gate_theirs, d_up_theirs], axis=1)
+    d_ffn = core_sum(d_pre_mine, d_pre_theirs, w_in, turned)
+    d_ffn_sent = send_blocks(d_ffn)
+    inner_act = jnp.concatenate([after(inner_mine, d_ffn), inner_theirs], axis=0)
+    cot_rows = jnp.concatenate([cot_mine, cot_theirs], axis=0)
+    grad_rows = over_rows(inner_act, cot_rows).astype(bf16)
+    part_down = lax.psum_scatter(grad_rows, ("hi", "ctx"), scatter_dimension=0, tiled=True)
+    ffn_in = jnp.concatenate([after(ffn_mine, grad_rows), ffn_theirs], axis=0)
+    d_pre = jnp.concatenate([after(d_pre_mine, grad_rows), d_pre_theirs], axis=0)
+    grad_in = over_rows(ffn_in, d_pre).astype(bf16).reshape(n_shard, n_part * slice_rows, -1)
+    d_ffn_in = sum_terms(after(send_terms(d_ffn_sent, "shard", n_shard), grad_in))
+    d_middle = own_cot.astype(f32) + norm_back(unit_m, recip_m, gain_ffn, d_ffn_in)
+
+    d_branch_own = d_middle.astype(bf16)
+    branch_ring = from_ring(d_branch_own, "shard", n_shard)
+    part_in = lax.psum_scatter(
+        after(grad_in, part_down, d_branch_own), ("hi", "ctx"), scatter_dimension=1, tiled=True
+    )
+    branch_mine = jnp.concatenate(after(branch_ring, part_down), axis=0)
+    branch_theirs = swap(branch_mine, "core")
+    d_mixed_mine = product(branch_mine, w_out_rows, turned).astype(bf16)
+    tables = (query_pos, key_pos, cosine, sine, gain_query)
+    d_q_mine, gain_q_mine, d_kv_mine = attend_back(
+        0, starts, *order, q_mine, pre_mine, kv_mine_parts, d_mixed_mine, *tables
+    )
+    d_mixed_theirs = product(after(branch_theirs, d_q_mine), w_out_rows, turned).astype(bf16)
+    d_q_theirs, gain_q_theirs, d_kv_theirs = attend_back(
+        1, starts, *order, q_theirs, pre_theirs, kv_theirs_parts, d_mixed_theirs, *tables
+    )
+    part_in = after(part_in, d_q_theirs)
+
+    def keys_gradient(d_queries, d_kv, pre, *others):
+        got = [
+            lax.ppermute(d_kv[n_ctx - k], "ctx", [(i, (i + k) % n_ctx) for i in range(n_ctx)])
+            for k in range(1, n_ctx)
+        ]
+        got = [after(values, *others) for values in got]
+        return keys_back(d_queries, d_kv[0], got, pre, cosine, sine, gain_key)
+
+    d_qkv_mine, gain_k_mine = keys_gradient(d_q_mine, d_kv_mine, pre_mine, d_q_theirs)
+    d_qkv_theirs, gain_k_theirs = keys_gradient(
+        d_q_theirs, d_kv_theirs, pre_theirs, d_qkv_mine
+    )
+    sent_in = exchange_ring(part_in, z, n_shard)
+    full_rows = gather_plane(after(part_down, part_in))
+    d_in = core_sum(d_qkv_mine, after(d_qkv_theirs, part_in), w_qkv, turned)
+    sent_in = jnp.stack(after(sent_in, d_in))
+    sent = head_gradients(
+        at,
+        n_part,
+        n_shard,
+        (normed_mine, normed_theirs),
+        (branch_mine, branch_theirs),
+        (after(d_qkv_mine, d_in, sent_in), d_qkv_theirs),
+        (mixed_mine, mixed_theirs),
+    )
+    part_heads = send_terms(sent, ("hi", "ctx"), n_part)
+    full_in = gather_plane(after(sent_in, full_rows))
+    head_gains = jnp.stack([gain_q_mine + gain_q_theirs, gain_k_mine + gain_k_theirs])
+    head_gains = sum(after(from_ring(head_gains, "core", 2), sent))
+    part_heads = sum_terms(after(part_heads, head_gains)).astype(bf16)
+    qkv_cols = q_cols + 2 * kv_cols
+    ring_heads = exchange_ring(part_heads[..., :qkv_cols], z, n_shard)
+    head_gains = sum(after(from_ring(head_gains, "hi", n_hi), part_heads))
+    d_normed = send_terms(send_blocks(after(d_in, ring_heads)), "shard", n_shard)
+    ring_heads = after(ring_heads, head_gains)
+    part_heads = jnp.concatenate([jnp.stack(ring_heads), part_heads[..., qkv_cols:]], axis=-1)
+    mine_heads = from_ring(part_heads, ("hi", "ctx"), n_part)
+    result = core_sum(after(inner_mine, part_heads), inner_theirs, w_down_rows, plain)
+    grad_down = lay_rows(after(full_rows, result))
+    head_gains = sum(after(from_ring(head_gains, "ctx", n_ctx), grad_down))
+    d_normed = sum_terms(after(d_normed, grad_down))
+    recip_h = recip_rms(hidden_in)
+    unit_h = hidden_in * recip_h
+    input_grad = d_middle + norm_back(unit_h, recip_h, gain_attn, d_normed)
+    result = send_terms(send_blocks(after(result, input_grad)), "shard", n_shard)
+    mine_heads = after(mine_heads, head_gains, input_grad)
+    theirs_heads = [swap(values, "core") for values in mine_heads]
+    head_gains = sum(from_ring(after(head_gains, mine_heads), "shard", n_shard))
+    head_size = query_gain.shape[0]
+    head_gains = lax.dynamic_slice_in_dim(head_gains, z * head_size, head_size, axis=1)
+    grad_query, grad_key, grad_value, grad_out, attn_sums = lay_heads(
+        at, mine_heads, theirs_heads, w_query, key_weight, value_weight
+    )
+    grad_gate, grad_up, ffn_sums = lay_in(z, after(full_in, grad_query), w_gate, w_up)
+    result = (middle + sum_terms(after(result, grad_gate))).astype(bf16)
+    grad_ffn_gain = jnp.sum(ffn_sums, axis=1) / ffn_gain.astype(f32)
+    grad_attn_gain = jnp.sum(attn_sums, axis=1) / attn_gain.astype(f32)
+
+    return (
+        result.reshape(tokens.shape),
+        input_grad.reshape(tokens.shape),
+        grad_query,
+        grad_key,
+        grad_value,
+        grad_out,
+        grad_attn_gain,
+        head_gains[0],
+        head_gains[1],
+        grad_gate,
+        grad_up,
+        grad_down,
+        grad_ffn_gain,
+    )
+
+
 def solution(mesh):
+    n_rep, n_shard, n_ctx = (mesh.shape[name] for name in ("rep", "shard", "ctx"))
+    if n_rep % 2 == 0 and KEY_VALUE_HEADS % (2 * n_shard) == 0:
+        mesh = Mesh(
+            mesh.devices.reshape(n_rep // 2, 2, n_shard, n_ctx), ("hi", "core", "shard", "ctx")
+        )
+        rep = ("hi", "core")
+        body = partial(grouped_shards, n_rep // 2, n_shard, n_ctx)
+    else:
+        rep = "rep"
+        body = shards_general
     in_specs = (
-        P(None, "rep", ("shard", "ctx"), None),
-        P(None, "rep"),
-        P(None, "rep", ("shard", "ctx"), None),
+        P(None, rep, ("shard", "ctx"), None),
+        P(None, rep),
+        P(None, rep, ("shard", "ctx"), None),
         P("shard", None),
         P("shard", None),
         P("shard", None),
@@ -403,8 +1393,8 @@
         P("shard"),
     )
     out_specs = (
-        P(None, "rep", ("shard", "ctx"), None),
-        P(None, "rep", ("shard", "ctx"), None),
+        P(None, rep, ("shard", "ctx"), None),
+        P(None, rep, ("shard", "ctx"), None),
         P("shard", None),
         P("shard", None),
         P("shard", None),
@@ -417,4 +1407,4 @@
         P("shard", None),
         P("shard"),
     )
-    return jax.shard_map(shards, mesh=mesh, in_specs=in_specs, out_specs=out_specs, check_vma=False)
+    return jax.shard_map(body, mesh=mesh, in_specs=in_specs, out_specs=out_specs, check_vma=False)

time: 4440 us -> 730 us (0.16)
  the two profiles are of different devices: /device:TPU:14 before, /device:TPU:0 now
where the time goes in v1:
time: 730 us; the launch traced here: 719 us
  waiting for transfers between devices  373 us (51%)
  Pallas kernels  115 us (16%)
  starting transfers between devices  66 us (9%)
  local copies, waits for them, and re-layouts  52.3 us (7%)
  matrix products  51.6 us (7%)
  other arithmetic  44.6 us (6%)
  between operations  16 us (2%)
    ppermute x15, waiting for transfers between devices, send_terms(): lax.ppermute(pieces[count - k].astype(jnp.bfloat16), axis, [(i, (i + k) %...  144 us
    ppermute x23, waiting for transfers between devices, from_ring(): lax.ppermute(block, axis, [(i, (i + k) % count) for i in range(count)])  112 us
    ppermute x9, waiting for transfers between devices, exchange_ring(): lax.ppermute(piece_for(k), 'shard', [(i, (i + k) % count) for i in range(...  42.9 us
    dot_general x12, matrix products, product(): return lax.dot_general(left, right, dims, preferred_element_type=f32)  34.2 us
    unnamed x170, local copies, waits for them, and re-layouts  28.4 us
    ppermute x23, starting transfers between devices, from_ring(): lax.ppermute(block, axis, [(i, (i + k) % count) for i in range(count)])  25.5 us
    all_to_all x1, waiting for transfers between devices, exchange(): return lax.all_to_all(pieces, 'shard', 0, 0, tiled=True)  24.2 us
    all_gather x1, waiting for transfers between devices, grouped_shards(): cot_all = lax.all_gather(after(own_cot, gathered), 'shard', axis=0)  20.5 us
  transfers between devices with their start and end apart: 70, of which 29 were waited for; matrix products, arithmetic and copies ran while one was open for 15% of the time, Pallas kernels for 14%

profile of v1, /device:TPU:0, one launch (start us, length us, event | category | flops | bytes accessed | tf_op | source)
XLA Modules:
  0.0 718.9 jit_solution(18021165293755050643)
XLA Ops:
  8.5 3.8 take_columns.2
  12.3 6.3 all-to-all-start
  18.7 4.5 take_columns.3
  23.3 24.2 %all-to-all-done.refs_4_.refs_0_ = bf16[4,128,512]{2,1,0:T(8,128)(2,1)S(1)} async-done(((bf16[4,128,512]{2,1,0:T(8,128)(2,1)}), bf16[4,128,512]{2,1,0:T(8,128)(2,1)S(1)}, u32[]{:S(2)}, u32[]{:S(2)}) %all-to-all-start) | async-done | bytes 524320 | tf_op jit(solution)/shard_map/all_to_all | solution.py:1161
  47.5 3.3 collective-permute-start.5
  57.4 7.5 %collective-permute-done.3.refs_7_.refs_3_ = bf16[4,128,512]{2,1,0:T(8,128)(2,1)S(1)} collective-permute-done((bf16[4,128,512]{2,1,0:T(8,128)(2,1)S(1)}, bf16[4,128,512]{2,1,0:T(8,128)(2,1)S(1)}, u32[]{:S(2)}, u32[]{:S(2)}) %collective-permute-start.3) | collective-permute-done | bytes 524320 | tf_op jit(solution)/shard_map/ppermute | solution.py:393
  65.0 15.3 %collective-permute-done.2.refs_6_.refs_2_ = bf16[4,128,512]{2,1,0:T(8,128)(2,1)} collective-permute-done((bf16[4,128,512]{2,1,0:T(8,128)(2,1)S(1)}, bf16[4,128,512]{2,1,0:T(8,128)(2,1)}, u32[]{:S(2)}, u32[]{:S(2)}) %collective-permute-start.2) | collective-permute-done | bytes 524320 | tf_op jit(solution)/shard_map/ppermute | solution.py:393
  80.3 4.2 norm_group.1.refs_0_.refs_1_.refs_2_.refs_3_
  95.7 7.6 %project.2 = (bf16[512,256]{1,0:T(8,128)(2,1)S(1)}, bf16[512,256]{1,0:T(8,128)(2,1)}, f32[512,384]{1,0:T(8,128)S(1)}) custom-call(s32[3]{0:T(128)S(1)} %copy-done.27, bf16[512,2048]{1,0:T(8,128)(2,1)S(1)} %copy-done.1, bf16[512,2048]{1,0:T(8,128)(2,1)S(1)} %copy-done.1, bf16[512,2048]{1,0:T(8,128)(2,1)S(1)} %copy-done.1, bf16[512,2048]{1,0:T(8,128)(2,1)S(1)} %copy-done.1, ...), custom_call_target="tpu_custom_call" | custom-call | tf_op jit(solution)/shard_map/project/pallas_call | solution.py:724
  104.3 7.0 project.3
  114.6 4.6 lay_order.1
  119.3 3.7 attend.2
  123.0 2.8 attend.3
  125.9 7.0 collective-permute-done.15
  140.4 20.5 %all-gather.13.cloned.1.call-done = bf16[512,2048]{1,0:T(8,128)(2,1)} async-done(((bf16[128,2048]{1,0:T(8,128)(2,1)}), bf16[512,2048]{1,0:T(8,128)(2,1)}) %all-gather.13.cloned.1.call-update) | async-done | bytes 2097168 | tf_op jit(solution)/shard_map/all_gather | solution.py:1217
  162.5 3.4 collective-permute-done.10
  165.9 3.8 fusion.50
  169.7 3.8 ring_order.1
  181.5 10.9 %collective-permute-done.13 = bf16[128,2048]{1,0:T(8,128)(2,1)} collective-permute-done((bf16[128,2048]{1,0:T(8,128)(2,1)}, bf16[128,2048]{1,0:T(8,128)(2,1)}, u32[]{:S(2)}, u32[]{:S(2)}) %collective-permute-start.13) | collective-permute-done | bytes 524320 | tf_op jit(solution)/shard_map/ppermute | solution.py:400
  192.4 30.4 %collective-permute-done.12 = bf16[128,2048]{1,0:T(8,128)(2,1)} collective-permute-done((bf16[128,2048]{1,0:T(8,128)(2,1)}, bf16[128,2048]{1,0:T(8,128)(2,1)}, u32[]{:S(2)}, u32[]{:S(2)}) %collective-permute-start.12) | collective-permute-done | bytes 524320 | tf_op jit(solution)/shard_map/ppermute | solution.py:400
  222.8 8.3 %all-gather.11.cloned.1.call-done = bf16[4,512,1536]{2,1,0:T(8,128)(2,1)} async-done(((bf16[4,128,1536]{2,1,0:T(8,128)(2,1)}), bf16[4,512,1536]{2,1,0:T(8,128)(2,1)}) %all-gather.11.cloned.1.call-update) | async-done | bytes 6291472 | tf_op jit(solution)/shard_map/all_gather | solution.py:1233
  233.8 3.4 collective-permute-start.19
  238.7 3.7 fusion.18.d_inner_ref
  242.5 3.5 fusion.16.d_inner_ref
  246.0 3.6 collective-permute-done.19
  249.6 32.6 %collective-permute-done.18 = bf16[128,2048]{1,0:T(8,128)(2,1)S(1)} collective-permute-done((bf16[128,2048]{1,0:T(8,128)(2,1)S(1)}, bf16[128,2048]{1,0:T(8,128)(2,1)S(1)}, u32[]{:S(2)}, u32[]{:S(2)}) %collective-permute-start.18) | collective-permute-done | bytes 524320 | tf_op jit(solution)/shard_map/ppermute | solution.py:393
  282.4 6.7 inner_parts.2
  289.2 7.0 inner_parts.3
  296.4 7.3 %convolution_convert_fusion.4 = bf16[512,2048]{1,0:T(8,128)(2,1)S(1)} fusion(bf16[512,1536]{1,0:T(8,128)(2,1)S(1)} %constant_dynamic-update-slice_fusion.6, bf16[2048,1536]{1,0:T(8,128)(2,1)} %bitcast.173), kind=kOutput, calls=%fused_computation.19 | convolution fusion | flops 3222274048 | bytes 9961472 | tf_op jit(solution)/shard_map/dot_general | solution.py:1158
  303.9 3.4 fusion.56
  307.9 3.8 fusion.49
  311.7 6.5 fusion.7
  320.0 2.8 collective-permute-start.24
  324.9 10.9 %convolution_convert_fusion = bf16[2048,1536]{1,0:T(8,128)(2,1)} fusion(bf16[512,2048]{1,0:T(8,128)(2,1)} %copy-done.16, bf16[512,2048]{1,0:T(8,128)(2,1)S(1)} %copy-done.11, bf16[512,1536]{1,0:T(8,128)(2,1)} %copy-done.59, bf16[512,1536]{1,0:T(8,128)(2,1)} %copy-done.58), kind=kOutput, calls=%fused_computation | convolution fusion | flops 6460276736 | bytes 13631488 | tf_op jit(solution)/shard_map/dot_general | solution.py:49
  338.2 30.5 %collective-permute-done.24 = bf16[128,2048]{1,0:T(8,128)(2,1)} collective-permute-done((bf16[128,2048]{1,0:T(8,128)(2,1)S(1)}, bf16[128,2048]{1,0:T(8,128)(2,1)}, u32[]{:S(2)}, u32[]{:S(2)}) %collective-permute-start.24) | collective-permute-done | bytes 524320 | tf_op jit(solution)/shard_map/ppermute | solution.py:400
  371.6 3.1 fusion.48
  377.1 12.7 %collective-permute-done.28 = bf16[128,2048]{1,0:T(8,128)(2,1)S(1)} collective-permute-done((bf16[128,2048]{1,0:T(8,128)(2,1)}, bf16[128,2048]{1,0:T(8,128)(2,1)S(1)}, u32[]{:S(2)}, u32[]{:S(2)}) %collective-permute-start.28) | collective-permute-done | bytes 524320 | tf_op jit(solution)/shard_map/ppermute | solution.py:393
  389.7 31.3 %collective-permute-done.27 = bf16[128,2048]{1,0:T(8,128)(2,1)S(1)} collective-permute-done((bf16[128,2048]{1,0:T(8,128)(2,1)}, bf16[128,2048]{1,0:T(8,128)(2,1)S(1)}, u32[]{:S(2)}, u32[]{:S(2)}) %collective-permute-start.27) | collective-permute-done | bytes 524320 | tf_op jit(solution)/shard_map/ppermute | solution.py:393
  424.6 5.2 attend_back.2
  431.6 4.4 attend_back.3
  438.3 4.0 reduce-scatter.5.cloned.1.call-done
  444.7 7.4 %collective-permute-done.30.refs_2_ = bf16[512,256]{1,0:T(8,128)(2,1)S(1)} collective-permute-done((bf16[512,256]{1,0:T(8,128)(2,1)}, bf16[512,256]{1,0:T(8,128)(2,1)S(1)}, u32[]{:S(2)}, u32[]{:S(2)}) %collective-permute-start.30) | collective-permute-done | bytes 262176 | tf_op jit(solution)/shard_map/ppermute | solution.py:1295
  455.5 4.2 collective-permute-done.31.refs_2_
  463.1 3.2 convolution_convert_fusion.3
  466.5 3.4 collective-permute-start.35
  475.0 4.4 collective-permute-done.35
  479.4 24.8 %collective-permute-done.34 = bf16[128,1536]{1,0:T(8,128)(2,1)S(1)} collective-permute-done((bf16[128,1536]{1,0:T(8,128)(2,1)S(1)}, bf16[128,1536]{1,0:T(8,128)(2,1)S(1)}, u32[]{:S(2)}, u32[]{:S(2)}) %collective-permute-start.34) | collective-permute-done | bytes 393248 | tf_op jit(solution)/shard_map/ppermute | solution.py:583
  506.7 8.1 %head_gradients.1 = (bf16[4,128,768]{2,1,0:T(8,128)(2,1)S(1)}, bf16[4,128,768]{2,1,0:T(8,128)(2,1)S(1)}, bf16[4,128,768]{2,1,0:T(8,128)(2,1)S(1)}, bf16[4,128,768]{2,1,0:T(8,128)(2,1)S(1)}) custom-call(s32[3]{0:T(128)S(1)} %copy-done.28, bf16[512,2048]{1,0:T(8,128)(2,1)} %norm_group.1.refs_0_.refs_1_.refs_2_.refs_3_, ...), custom_call_target="tpu_custom_call" | custom-call | tf_op jit(solution)/shard_map/head_gradients/pallas_call | solution.py:1035
  518.8 5.0 convolution_convert_fusion.2
  528.9 23.0 %collective-permute-done.36 = bf16[4,128,768]{2,1,0:T(8,128)(2,1)S(1)} collective-permute-done((bf16[4,128,768]{2,1,0:T(8,128)(2,1)S(1)}, bf16[4,128,768]{2,1,0:T(8,128)(2,1)S(1)}, u32[]{:S(2)}, u32[]{:S(2)}) %collective-permute-start.36) | collective-permute-done | bytes 786464 | tf_op jit(solution)/shard_map/ppermute | solution.py:400
  551.9 16.1 %collective-permute-done.37 = bf16[4,128,768]{2,1,0:T(8,128)(2,1)S(1)} collective-permute-done((bf16[4,128,768]{2,1,0:T(8,128)(2,1)S(1)}, bf16[4,128,768]{2,1,0:T(8,128)(2,1)S(1)}, u32[]{:S(2)}, u32[]{:S(2)}) %collective-permute-start.37) | collective-permute-done | bytes 786464 | tf_op jit(solution)/shard_map/ppermute | solution.py:400
  577.1 6.6 collective-permute-done.41
  590.2 3.8 fusion.13
  596.0 4.3 convert_add_fusion
  602.6 8.9 %lay_rows.1 = f32[1536,2048]{1,0:T(8,128)} custom-call(bf16[2,2,2,192,2048]{4,3,2,1,0:T(8,128)(2,1)} %bitcast.180), custom_call_target="tpu_custom_call" | custom-call | tf_op jit(solution)/shard_map/lay_rows/pallas_call | solution.py:491
  613.5 22.7 %collective-permute-done.46 = bf16[128,2048]{1,0:T(8,128)(2,1)} collective-permute-done((bf16[128,2048]{1,0:T(8,128)(2,1)}, bf16[128,2048]{1,0:T(8,128)(2,1)}, u32[]{:S(2)}, u32[]{:S(2)}) %collective-permute-start.46) | collective-permute-done | bytes 524320 | tf_op jit(solution)/shard_map/ppermute | solution.py:400
  639.1 2.9 fusion.28
  642.0 4.9 collective-permute-done.52.refs_2_
  663.7 9.4 %lay_heads.1 = (f32[512,2048]{1,0:T(8,128)}, f32[512,1024]{1,0:T(8,128)}, f32[512,1024]{1,0:T(8,128)}, f32[512,2048]{1,0:T(8,128)}, f32[512,128]{1,0:T(8,128)S(1)}) custom-call(s32[3]{0:T(128)S(1)} %copy-done.28, bf16[4,128,768]{2,1,0:T(8,128)(2,1)S(1)} %pad_maximum_fusion.1.refs_0_, bf16[4,128,768]{2,1,0:T(8,128)(2,1)} %collective-permute-done.51.refs_1_, ...), custom_call_target="tpu_custom_call" | custom-call | tf_op jit(solution)/shard_map/lay_heads/pallas_call | solution.py:552
  673.9 2.8 copy-done.2
  676.6 2.8 copy-done.3
  679.4 18.0 %lay_in.1 = (f32[512,6144]{1,0:T(8,128)}, f32[512,6144]{1,0:T(8,128)}, f32[512,128]{1,0:T(8,128)S(1)}) custom-call(s32[1]{0:T(128)} %bitcast.4.z_ref, bf16[2,2,2,4,128,1536]{5,4,3,2,1,0:T(8,128)(2,1)} %bitcast.178, bf16[512,6144]{1,0:T(8,128)(2,1)S(1)} %copy-done.2, bf16[512,6144]{1,0:T(8,128)(2,1)S(1)} %copy-done.3), custom_call_target="tpu_custom_call" | custom-call | tf_op jit(solution)/shard_map/lay_in/pallas_call | solution.py:463
  697.4 10.6 %collective-permute-done.49 = bf16[128,2048]{1,0:T(8,128)(2,1)} collective-permute-done((bf16[128,2048]{1,0:T(8,128)(2,1)}, bf16[128,2048]{1,0:T(8,128)(2,1)}, u32[]{:S(2)}, u32[]{:S(2)}) %collective-permute-start.49) | collective-permute-done | bytes 524320 | tf_op jit(solution)/shard_map/ppermute | solution.py:400
  708.8 2.9 add_convert_fusion.1
  (373 shorter events, 133.5 us)
Async XLA Ops:
  7.2 73.1 %all-gather.9.cloned.1.call-start = ((), (), s32[]{:S(2)}) async-start(), calls=%async_computation.3 | async-start | bytes 2621440 | tf_op jit(solution)/shard_map/all_gather | solution.py:1173
  12.3 35.2 %all-to-all-start = ((bf16[4,128,512]{2,1,0:T(8,128)(2,1)}), bf16[4,128,512]{2,1,0:T(8,128)(2,1)S(1)}, u32[]{:S(2)}, u32[]{:S(2)}) async-start(bf16[4,128,512]{2,1,0:T(8,128)(2,1)} %take_columns.2), calls=%async_computation | async-start | bytes 1048576 | tf_op jit(solution)/shard_map/all_to_all | solution.py:1161
  18.6 142.2 %all-gather.13.cloned.1.call-start = ((), (), s32[]{:S(2)}) async-start(), calls=%async_computation.7 | async-start | bytes 2621440 | tf_op jit(solution)/shard_map/all_gather | solution.py:1217
  47.5 8.0 %collective-permute-start.6 = (bf16[1088]{0:T(1024)(128)(2,1)S(1)}, bf16[1088]{0:T(1024)(128)(2,1)S(1)}, u32[]{:S(2)}, u32[]{:S(2)}) collective-permute-start(bf16[1088]{0:T(1024)(128)(2,1)S(1)} %concatenate.44), channel_id=1, source_target_pairs={{0,2},{2,4},{4,6},{6,0},{1,3},{3,5},{5,7},{7,1},{8,10},{10,12},{12... | collective-permute-start | bytes 6536 | tf_op jit(solution)/shard_map/ppermute | solution.py:393
  47.5 8.6 %collective-permute-start.5 = (bf16[1088]{0:T(1024)(128)(2,1)S(1)}, bf16[1088]{0:T(1024)(128)(2,1)S(1)}, u32[]{:S(2)}, u32[]{:S(2)}) collective-permute-start(bf16[1088]{0:T(1024)(128)(2,1)S(1)} %concatenate.44), channel_id=1, source_target_pairs={{0,4},{2,6},{4,0},{6,2},{1,5},{3,7},{5,1},{7,3},{8,12},{10,14},{12... | collective-permute-start | bytes 6536 | tf_op jit(solution)/shard_map/ppermute | solution.py:393
  51.3 13.6 %collective-permute-start.3 = (bf16[4,128,512]{2,1,0:T(8,128)(2,1)S(1)}, bf16[4,128,512]{2,1,0:T(8,128)(2,1)S(1)}, u32[]{:S(2)}, u32[]{:S(2)}) collective-permute-start(bf16[4,128,512]{2,1,0:T(8,128)(2,1)S(1)} %all-to-all-done.refs_4_.refs_0_), channel_id=1, source_target_pairs={{0,17},{1,0},{16,1},{17,16},{2,19},{3,2},{18,3},{19,18},{4,21},{5,... | collective-permute-start | bytes 1572872 | tf_op jit(solution)/shard_map/ppermute | solution.py:393
  54.9 25.4 %collective-permute-start.2 = (bf16[4,128,512]{2,1,0:T(8,128)(2,1)S(1)}, bf16[4,128,512]{2,1,0:T(8,128)(2,1)}, u32[]{:S(2)}, u32[]{:S(2)}) collective-permute-start(bf16[4,128,512]{2,1,0:T(8,128)(2,1)S(1)} %all-to-all-done.refs_4_.refs_0_), channel_id=1, source_target_pairs={{0,16},{1,17},{16,0},{17,1},{2,18},{3,19},{18,2},{19,3},{4,20},{5,... | collective-permute-start | bytes 1572872 | tf_op jit(solution)/shard_map/ppermute | solution.py:393
  55.4 24.9 %collective-permute-start.1 = (bf16[4,128,512]{2,1,0:T(8,128)(2,1)S(1)}, bf16[4,128,512]{2,1,0:T(8,128)(2,1)}, u32[]{:S(2)}, u32[]{:S(2)}) collective-permute-start(bf16[4,128,512]{2,1,0:T(8,128)(2,1)S(1)} %all-to-all-done.refs_4_.refs_0_), channel_id=1, source_target_pairs={{0,1},{1,16},{16,17},{17,0},{2,3},{3,18},{18,19},{19,2},{4,5},{5,2... | collective-permute-start | bytes 1572872 | tf_op jit(solution)/shard_map/ppermute | solution.py:393
  84.5 19.8 %collective-permute-start.8 = (bf16[512,2048]{1,0:T(8,128)(2,1)}, bf16[512,2048]{1,0:T(8,128)(2,1)}, u32[]{:S(2)}, u32[]{:S(2)}) collective-permute-start(bf16[512,2048]{1,0:T(8,128)(2,1)} %norm_group.1.refs_0_.refs_1_.refs_2_.refs_3_), channel_id=1, source_target_pairs={{0,8},{8,0},{1,9},{9,1},{2,10},{10,2},{3,11},{11,3},{4,12},{12,4},... | collective-permute-start | bytes 6291464 | tf_op jit(solution)/shard_map/ppermute | solution.py:414
  88.6 37.2 %collective-permute-start.16 = (bf16[128,1536]{1,0:T(8,128)(2,1)}, bf16[128,1536]{1,0:T(8,128)(2,1)}, u32[]{:S(2)}, u32[]{:S(2)}) collective-permute-start(bf16[128,1536]{1,0:T(8,128)(2,1)} %get-tuple-element.336), channel_id=1, source_target_pairs={{0,6},{2,0},{4,2},{6,4},{1,7},{3,1},{5,3},{7,5},{8,14},{10,8},{12,... | collective-permute-start | bytes 1179656 | tf_op jit(solution)/shard_map/ppermute | solution.py:583
  89.5 43.4 %collective-permute-start.15 = (bf16[128,1536]{1,0:T(8,128)(2,1)}, bf16[128,1536]{1,0:T(8,128)(2,1)}, u32[]{:S(2)}, u32[]{:S(2)}) collective-permute-start(bf16[128,1536]{1,0:T(8,128)(2,1)} %get-tuple-element.337), channel_id=1, source_target_pairs={{0,4},{2,6},{4,0},{6,2},{1,5},{3,7},{5,1},{7,3},{8,12},{10,14},{12... | collective-permute-start | bytes 1179656 | tf_op jit(solution)/shard_map/ppermute | solution.py:583
  91.5 41.4 %collective-permute-start.14 = (bf16[128,1536]{1,0:T(8,128)(2,1)}, bf16[128,1536]{1,0:T(8,128)(2,1)}, u32[]{:S(2)}, u32[]{:S(2)}) collective-permute-start(bf16[128,1536]{1,0:T(8,128)(2,1)} %get-tuple-element.338), channel_id=1, source_target_pairs={{0,2},{2,4},{4,6},{6,0},{1,3},{3,5},{5,7},{7,1},{8,10},{10,12},{12... | collective-permute-start | bytes 1179656 | tf_op jit(solution)/shard_map/ppermute | solution.py:583
  104.2 15.0 %collective-permute-start.7 = (bf16[512,256]{1,0:T(8,128)(2,1)}, bf16[512,256]{1,0:T(8,128)(2,1)}, u32[]{:S(2)}, u32[]{:S(2)}) collective-permute-start(bf16[512,256]{1,0:T(8,128)(2,1)} %get-tuple-element.147), channel_id=1, source_target_pairs={{0,1},{1,0},{2,3},{3,2},{4,5},{5,4},{6,7},{7,6},{8,9},{9,8},{10,11... | collective-permute-start | bytes 786440 | tf_op jit(solution)/shard_map/ppermute | solution.py:393
  112.2 10.8 %collective-permute-start.9 = (bf16[512,256]{1,0:T(8,128)(2,1)S(1)}, bf16[512,256]{1,0:T(8,128)(2,1)S(1)}, u32[]{:S(2)}, u32[]{:S(2)}) collective-permute-start(bf16[512,256]{1,0:T(8,128)(2,1)S(1)} %get-tuple-element.150), channel_id=1, source_target_pairs={{0,1},{1,0},{2,3},{3,2},{4,5},{5,4},{6,7},{7,6},{8,9},{9,8},{10,11... | collective-permute-start | bytes 786440 | tf_op jit(solution)/shard_map/ppermute | solution.py:393
  114.6 116.5 %all-gather.11.cloned.1.call-start = ((), (), s32[]{:S(2)}) async-start(), calls=%async_computation.4 | async-start | bytes 7864320 | tf_op jit(solution)/shard_map/all_gather | solution.py:1233
  160.9 213.8 %reduce-scatter.3.cloned.1.call-start = ((), (), s32[]{:S(2)}) async-start(), calls=%async_computation.5 | async-start | bytes 3932160 | tf_op jit(solution)/shard_map/reduce_scatter | solution.py:1268
  173.5 69.0 %collective-permute-start.20 = (bf16[512,2048]{1,0:T(8,128)(2,1)}, bf16[512,2048]{1,0:T(8,128)(2,1)}, u32[]{:S(2)}, u32[]{:S(2)}) collective-permute-start(bf16[512,2048]{1,0:T(8,128)(2,1)} %ring_order.1), channel_id=1, source_target_pairs={{0,8},{8,0},{1,9},{9,1},{2,10},{10,2},{3,11},{11,3},{4,12},{12,4},... | collective-permute-start | bytes 6291464 | tf_op jit(solution)/shard_map/ppermute | solution.py:414
  176.2 16.2 %collective-permute-start.13 = (bf16[128,2048]{1,0:T(8,128)(2,1)}, bf16[128,2048]{1,0:T(8,128)(2,1)}, u32[]{:S(2)}, u32[]{:S(2)}) collective-permute-start(bf16[128,2048]{1,0:T(8,128)(2,1)} %get-tuple-element.329), channel_id=1, source_target_pairs={{0,6},{2,0},{4,2},{6,4},{1,7},{3,1},{5,3},{7,5},{8,14},{10,8},{12,... | collective-permute-start | bytes 1572872 | tf_op jit(solution)/shard_map/ppermute | solution.py:400
  177.9 44.9 %collective-permute-start.12 = (bf16[128,2048]{1,0:T(8,128)(2,1)}, bf16[128,2048]{1,0:T(8,128)(2,1)}, u32[]{:S(2)}, u32[]{:S(2)}) collective-permute-start(bf16[128,2048]{1,0:T(8,128)(2,1)} %get-tuple-element.330), channel_id=1, source_target_pairs={{0,4},{2,6},{4,0},{6,2},{1,5},{3,7},{5,1},{7,3},{8,12},{10,14},{12... | collective-permute-start | bytes 1572872 | tf_op jit(solution)/shard_map/ppermute | solution.py:400
  177.9 44.9 %collective-permute-start.11 = (bf16[128,2048]{1,0:T(8,128)(2,1)}, bf16[128,2048]{1,0:T(8,128)(2,1)}, u32[]{:S(2)}, u32[]{:S(2)}) collective-permute-start(bf16[128,2048]{1,0:T(8,128)(2,1)} %get-tuple-element.331), channel_id=1, source_target_pairs={{0,2},{2,4},{4,6},{6,0},{1,3},{3,5},{5,7},{7,1},{8,10},{10,12},{12... | collective-permute-start | bytes 1572872 | tf_op jit(solution)/shard_map/ppermute | solution.py:400
  233.8 15.8 %collective-permute-start.19 = (bf16[128,2048]{1,0:T(8,128)(2,1)S(1)}, bf16[128,2048]{1,0:T(8,128)(2,1)S(1)}, u32[]{:S(2)}, u32[]{:S(2)}) collective-permute-start(bf16[128,2048]{1,0:T(8,128)(2,1)S(1)} %multiply_convert_fusion), channel_id=1, source_target_pairs={{0,6},{2,0},{4,2},{6,4},{1,7},{3,1},{5,3},{7,5},{8,14},{10,8},{12,... | collective-permute-start | bytes 1572872 | tf_op jit(solution)/shard_map/ppermute | solution.py:393
  237.2 45.0 %collective-permute-start.18 = (bf16[128,2048]{1,0:T(8,128)(2,1)S(1)}, bf16[128,2048]{1,0:T(8,128)(2,1)S(1)}, u32[]{:S(2)}, u32[]{:S(2)}) collective-permute-start(bf16[128,2048]{1,0:T(8,128)(2,1)S(1)} %multiply_convert_fusion), channel_id=1, source_target_pairs={{0,4},{2,6},{4,0},{6,2},{1,5},{3,7},{5,1},{7,3},{8,12},{10,14},{12... | collective-permute-start | bytes 1572872 | tf_op jit(solution)/shard_map/ppermute | solution.py:393
  237.2 45.0 %collective-permute-start.17 = (bf16[128,2048]{1,0:T(8,128)(2,1)S(1)}, bf16[128,2048]{1,0:T(8,128)(2,1)S(1)}, u32[]{:S(2)}, u32[]{:S(2)}) collective-permute-start(bf16[128,2048]{1,0:T(8,128)(2,1)S(1)} %multiply_convert_fusion), channel_id=1, source_target_pairs={{0,2},{2,4},{4,6},{6,0},{1,3},{3,5},{5,7},{7,1},{8,10},{10,12},{12... | collective-permute-start | bytes 1572872 | tf_op jit(solution)/shard_map/ppermute | solution.py:393
  282.4 6.8 collective-permute-start.21
  318.2 124.1 %reduce-scatter.5.cloned.1.call-start = ((), (), s32[]{:S(2)}) async-start(), calls=%async_computation.6 | async-start | bytes 7864320 | tf_op jit(solution)/shard_map/reduce_scatter | solution.py:1277
  320.0 18.3 %collective-permute-start.25 = (bf16[128,2048]{1,0:T(8,128)(2,1)S(1)}, bf16[128,2048]{1,0:T(8,128)(2,1)}, u32[]{:S(2)}, u32[]{:S(2)}) collective-permute-start(bf16[128,2048]{1,0:T(8,128)(2,1)S(1)} %get-tuple-element.326), channel_id=1, source_target_pairs={{0,6},{2,0},{4,2},{6,4},{1,7},{3,1},{5,3},{7,5},{8,14},{10,8},{12,... | collective-permute-start | bytes 1572872 | tf_op jit(solution)/shard_map/ppermute | solution.py:400
  320.0 48.7 %collective-permute-start.24 = (bf16[128,2048]{1,0:T(8,128)(2,1)S(1)}, bf16[128,2048]{1,0:T(8,128)(2,1)}, u32[]{:S(2)}, u32[]{:S(2)}) collective-permute-start(bf16[128,2048]{1,0:T(8,128)(2,1)S(1)} %get-tuple-element.327), channel_id=1, source_target_pairs={{0,4},{2,6},{4,0},{6,2},{1,5},{3,7},{5,1},{7,3},{8,12},{10,14},{12... | collective-permute-start | bytes 1572872 | tf_op jit(solution)/shard_map/ppermute | solution.py:400
  322.8 46.0 %collective-permute-start.23 = (bf16[128,2048]{1,0:T(8,128)(2,1)S(1)}, bf16[128,2048]{1,0:T(8,128)(2,1)}, u32[]{:S(2)}, u32[]{:S(2)}) collective-permute-start(bf16[128,2048]{1,0:T(8,128)(2,1)S(1)} %get-tuple-element.328), channel_id=1, source_target_pairs={{0,2},{2,4},{4,6},{6,0},{1,3},{3,5},{5,7},{7,1},{8,10},{10,12},{12... | collective-permute-start | bytes 1572872 | tf_op jit(solution)/shard_map/ppermute | solution.py:400
  374.7 130.9 %all-gather.15.cloned.1.call-start = ((), (), s32[]{:S(2)}) async-start(), calls=%async_computation.8 | async-start | bytes 7077888 | tf_op jit(solution)/shard_map/all_gather | solution.py:1164
  374.8 15.0 %collective-permute-start.28 = (bf16[128,2048]{1,0:T(8,128)(2,1)}, bf16[128,2048]{1,0:T(8,128)(2,1)S(1)}, u32[]{:S(2)}, u32[]{:S(2)}) collective-permute-start(bf16[128,2048]{1,0:T(8,128)(2,1)} %get-tuple-element.194), channel_id=1, source_target_pairs={{0,6},{2,0},{4,2},{6,4},{1,7},{3,1},{5,3},{7,5},{8,14},{10,8},{12,... | collective-permute-start | bytes 1572872 | tf_op jit(solution)/shard_map/ppermute | solution.py:393
  374.8 46.3 %collective-permute-start.27 = (bf16[128,2048]{1,0:T(8,128)(2,1)}, bf16[128,2048]{1,0:T(8,128)(2,1)S(1)}, u32[]{:S(2)}, u32[]{:S(2)}) collective-permute-start(bf16[128,2048]{1,0:T(8,128)(2,1)} %get-tuple-element.194), channel_id=1, source_target_pairs={{0,4},{2,6},{4,0},{6,2},{1,5},{3,7},{5,1},{7,3},{8,12},{10,14},{12... | collective-permute-start | bytes 1572872 | tf_op jit(solution)/shard_map/ppermute | solution.py:393
  375.1 45.9 %collective-permute-start.26 = (bf16[128,2048]{1,0:T(8,128)(2,1)}, bf16[128,2048]{1,0:T(8,128)(2,1)S(1)}, u32[]{:S(2)}, u32[]{:S(2)}) collective-permute-start(bf16[128,2048]{1,0:T(8,128)(2,1)} %get-tuple-element.194), channel_id=1, source_target_pairs={{0,2},{2,4},{4,6},{6,0},{1,3},{3,5},{5,7},{7,1},{8,10},{10,12},{12... | collective-permute-start | bytes 1572872 | tf_op jit(solution)/shard_map/ppermute | solution.py:393
  422.5 7.3 %collective-permute-start.29 = (bf16[512,2048]{1,0:T(8,128)(2,1)S(1)}, bf16[512,2048]{1,0:T(8,128)(2,1)S(1)}, u32[]{:S(2)}, u32[]{:S(2)}) collective-permute-start(bf16[512,2048]{1,0:T(8,128)(2,1)S(1)} %constant_dynamic-update-slice_fusion.8.refs_8_.refs_9_.refs_10_.refs_11_), channel_id=1, source_target_pairs={{0,8},{8,0},{1,9},{9,1},{2,10},{10,2},{3,11},{11,3},{4,12},{12,4},... | collective-permute-start | bytes 6291464 | tf_op jit(solution)/shard_map/ppermute | solution.py:414
  442.3 231.5 %all-gather.17.cloned.1.call-start = ((), (), s32[]{:S(2)}) async-start(), calls=%async_computation.9 | async-start | bytes 14155776 | tf_op jit(solution)/shard_map/all_gather | solution.py:1164
  442.6 9.5 %collective-permute-start.30 = (bf16[512,256]{1,0:T(8,128)(2,1)}, bf16[512,256]{1,0:T(8,128)(2,1)S(1)}, u32[]{:S(2)}, u32[]{:S(2)}) collective-permute-start(bf16[512,256]{1,0:T(8,128)(2,1)} %bitcast.167), channel_id=1, source_target_pairs={{0,1},{1,0},{2,3},{3,2},{4,5},{5,4},{6,7},{7,6},{8,9},{9,8},{10,11... | collective-permute-start | bytes 786440 | tf_op jit(solution)/shard_map/ppermute | solution.py:1295
  444.0 15.7 %collective-permute-start.31 = (bf16[512,256]{1,0:T(8,128)(2,1)}, bf16[512,256]{1,0:T(8,128)(2,1)S(1)}, u32[]{:S(2)}, u32[]{:S(2)}) collective-permute-start(bf16[512,256]{1,0:T(8,128)(2,1)} %bitcast.168), channel_id=1, source_target_pairs={{0,1},{1,0},{2,3},{3,2},{4,5},{5,4},{6,7},{7,6},{8,9},{9,8},{10,11... | collective-permute-start | bytes 786440 | tf_op jit(solution)/shard_map/ppermute | solution.py:1295
  466.3 6.0 collective-permute-start.32
  466.5 12.9 %collective-permute-start.35 = (bf16[128,1536]{1,0:T(8,128)(2,1)S(1)}, bf16[128,1536]{1,0:T(8,128)(2,1)S(1)}, u32[]{:S(2)}, u32[]{:S(2)}) collective-permute-start(bf16[128,1536]{1,0:T(8,128)(2,1)S(1)} %get-tuple-element.332), channel_id=1, source_target_pairs={{0,6},{2,0},{4,2},{6,4},{1,7},{3,1},{5,3},{7,5},{8,14},{10,8},{12,... | collective-permute-start | bytes 1179656 | tf_op jit(solution)/shard_map/ppermute | solution.py:583
  469.9 34.4 %collective-permute-start.34 = (bf16[128,1536]{1,0:T(8,128)(2,1)S(1)}, bf16[128,1536]{1,0:T(8,128)(2,1)S(1)}, u32[]{:S(2)}, u32[]{:S(2)}) collective-permute-start(bf16[128,1536]{1,0:T(8,128)(2,1)S(1)} %get-tuple-element.333), channel_id=1, source_target_pairs={{0,4},{2,6},{4,0},{6,2},{1,5},{3,7},{5,1},{7,3},{8,12},{10,14},{12... | collective-permute-start | bytes 1179656 | tf_op jit(solution)/shard_map/ppermute | solution.py:583
  469.9 34.4 %collective-permute-start.33 = (bf16[128,1536]{1,0:T(8,128)(2,1)S(1)}, bf16[128,1536]{1,0:T(8,128)(2,1)S(1)}, u32[]{:S(2)}, u32[]{:S(2)}) collective-permute-start(bf16[128,1536]{1,0:T(8,128)(2,1)S(1)} %get-tuple-element.334), channel_id=1, source_target_pairs={{0,2},{2,4},{4,6},{6,0},{1,3},{3,5},{5,7},{7,1},{8,10},{10,12},{12... | collective-permute-start | bytes 1179656 | tf_op jit(solution)/shard_map/ppermute | solution.py:583
  514.7 37.1 %collective-permute-start.36 = (bf16[4,128,768]{2,1,0:T(8,128)(2,1)S(1)}, bf16[4,128,768]{2,1,0:T(8,128)(2,1)S(1)}, u32[]{:S(2)}, u32[]{:S(2)}) collective-permute-start(bf16[4,128,768]{2,1,0:T(8,128)(2,1)S(1)} %get-tuple-element.222), channel_id=1, source_target_pairs={{0,1},{1,16},{16,17},{17,0},{2,3},{3,18},{18,19},{19,2},{4,5},{5,2... | collective-permute-start | bytes 2359304 | tf_op jit(solution)/shard_map/ppermute | solution.py:400
  516.9 51.1 %collective-permute-start.37 = (bf16[4,128,768]{2,1,0:T(8,128)(2,1)S(1)}, bf16[4,128,768]{2,1,0:T(8,128)(2,1)S(1)}, u32[]{:S(2)}, u32[]{:S(2)}) collective-permute-start(bf16[4,128,768]{2,1,0:T(8,128)(2,1)S(1)} %get-tuple-element.223), channel_id=1, source_target_pairs={{0,16},{1,17},{16,0},{17,1},{2,18},{3,19},{18,2},{19,3},{4,20},{5,... | collective-permute-start | bytes 2359304 | tf_op jit(solution)/shard_map/ppermute | solution.py:400
  516.9 51.0 %collective-permute-start.38 = (bf16[4,128,768]{2,1,0:T(8,128)(2,1)S(1)}, bf16[4,128,768]{2,1,0:T(8,128)(2,1)S(1)}, u32[]{:S(2)}, u32[]{:S(2)}) collective-permute-start(bf16[4,128,768]{2,1,0:T(8,128)(2,1)S(1)} %get-tuple-element.224), channel_id=1, source_target_pairs={{0,17},{1,0},{16,1},{17,16},{2,19},{3,2},{18,3},{19,18},{4,21},{5,... | collective-permute-start | bytes 2359304 | tf_op jit(solution)/shard_map/ppermute | solution.py:400
  523.8 70.3 %collective-permute-start.44 = (bf16[512,2048]{1,0:T(8,128)(2,1)}, bf16[512,2048]{1,0:T(8,128)(2,1)}, u32[]{:S(2)}, u32[]{:S(2)}) collective-permute-start(bf16[512,2048]{1,0:T(8,128)(2,1)} %convolution_convert_fusion.2), channel_id=1, source_target_pairs={{0,8},{8,0},{1,9},{9,1},{2,10},{10,2},{3,11},{11,3},{4,12},{12,4},... | collective-permute-start | bytes 6291464 | tf_op jit(solution)/shard_map/ppermute | solution.py:414
  527.9 47.0 %collective-permute-start.43 = (f32[2,128]{1,0:T(2,128)S(1)}, f32[2,128]{1,0:T(2,128)}, u32[]{:S(2)}, u32[]{:S(2)}) collective-permute-start(f32[2,128]{1,0:T(2,128)S(1)} %add.357), channel_id=1, source_target_pairs={{0,16},{16,0},{1,17},{17,1},{2,18},{18,2},{3,19},{19,3},{4,20},{20... | collective-permute-start | bytes 3080 | tf_op jit(solution)/shard_map/ppermute | solution.py:393
  569.2 7.9 %collective-permute-start.42 = (bf16[128,512]{1,0:T(8,128)(2,1)}, bf16[128,512]{1,0:T(8,128)(2,1)}, u32[]{:S(2)}, u32[]{:S(2)}) collective-permute-start(bf16[128,512]{1,0:T(8,128)(2,1)} %get-tuple-element.340), channel_id=1, source_target_pairs={{0,6},{2,0},{4,2},{6,4},{1,7},{3,1},{5,3},{7,5},{8,14},{10,8},{12,... | collective-permute-start | bytes 393224 | tf_op jit(solution)/shard_map/ppermute | solution.py:583
  569.2 14.5 %collective-permute-start.41 = (bf16[128,512]{1,0:T(8,128)(2,1)}, bf16[128,512]{1,0:T(8,128)(2,1)}, u32[]{:S(2)}, u32[]{:S(2)}) collective-permute-start(bf16[128,512]{1,0:T(8,128)(2,1)} %get-tuple-element.341), channel_id=1, source_target_pairs={{0,4},{2,6},{4,0},{6,2},{1,5},{3,7},{5,1},{7,3},{8,12},{10,14},{12... | collective-permute-start | bytes 393224 | tf_op jit(solution)/shard_map/ppermute | solution.py:583
  571.6 12.1 %collective-permute-start.40 = (bf16[128,512]{1,0:T(8,128)(2,1)}, bf16[128,512]{1,0:T(8,128)(2,1)}, u32[]{:S(2)}, u32[]{:S(2)}) collective-permute-start(bf16[128,512]{1,0:T(8,128)(2,1)} %get-tuple-element.342), channel_id=1, source_target_pairs={{0,2},{2,4},{4,6},{6,0},{1,3},{3,5},{5,7},{7,1},{8,10},{10,12},{12... | collective-permute-start | bytes 393224 | tf_op jit(solution)/shard_map/ppermute | solution.py:583
  575.6 35.8 %collective-permute-start.54 = (f32[2,128]{1,0:T(2,128)S(1)}, f32[2,128]{1,0:T(2,128)}, u32[]{:S(2)}, u32[]{:S(2)}) collective-permute-start(f32[2,128]{1,0:T(2,128)S(1)} %add.361), channel_id=1, source_target_pairs={{0,1},{1,0},{2,3},{3,2},{4,5},{5,4},{6,7},{7,6},{8,9},{9,8},{10,11... | collective-permute-start | bytes 3080 | tf_op jit(solution)/shard_map/ppermute | solution.py:393
  584.8 57.2 %collective-permute-start.53 = (bf16[4,128,768]{2,1,0:T(8,128)(2,1)S(1)}, bf16[4,128,768]{2,1,0:T(8,128)(2,1)}, u32[]{:S(2)}, u32[]{:S(2)}) collective-permute-start(bf16[4,128,768]{2,1,0:T(8,128)(2,1)S(1)} %pad_maximum_fusion.1.refs_0_), channel_id=1, source_target_pairs={{0,17},{1,0},{16,1},{17,16},{2,19},{3,2},{18,3},{19,18},{4,21},{5,... | collective-permute-start | bytes 2359304 | tf_op jit(solution)/shard_map/ppermute | solution.py:393
  589.5 23.3 %collective-permute-start.47 = (bf16[128,2048]{1,0:T(8,128)(2,1)}, bf16[128,2048]{1,0:T(8,128)(2,1)}, u32[]{:S(2)}, u32[]{:S(2)}) collective-permute-start(bf16[128,2048]{1,0:T(8,128)(2,1)} %get-tuple-element.323), channel_id=1, source_target_pairs={{0,6},{2,0},{4,2},{6,4},{1,7},{3,1},{5,3},{7,5},{8,14},{10,8},{12,... | collective-permute-start | bytes 1572872 | tf_op jit(solution)/shard_map/ppermute | solution.py:400
  589.5 46.7 %collective-permute-start.46 = (bf16[128,2048]{1,0:T(8,128)(2,1)}, bf16[128,2048]{1,0:T(8,128)(2,1)}, u32[]{:S(2)}, u32[]{:S(2)}) collective-permute-start(bf16[128,2048]{1,0:T(8,128)(2,1)} %get-tuple-element.324), channel_id=1, source_target_pairs={{0,4},{2,6},{4,0},{6,2},{1,5},{3,7},{5,1},{7,3},{8,12},{10,14},{12... | collective-permute-start | bytes 1572872 | tf_op jit(solution)/shard_map/ppermute | solution.py:400
  594.1 42.1 %collective-permute-start.45 = (bf16[128,2048]{1,0:T(8,128)(2,1)}, bf16[128,2048]{1,0:T(8,128)(2,1)}, u32[]{:S(2)}, u32[]{:S(2)}) collective-permute-start(bf16[128,2048]{1,0:T(8,128)(2,1)} %get-tuple-element.325), channel_id=1, source_target_pairs={{0,2},{2,4},{4,6},{6,0},{1,3},{3,5},{5,7},{7,1},{8,10},{10,12},{12... | collective-permute-start | bytes 1572872 | tf_op jit(solution)/shard_map/ppermute | solution.py:400
  611.5 35.5 %collective-permute-start.52 = (bf16[4,128,768]{2,1,0:T(8,128)(2,1)S(1)}, bf16[4,128,768]{2,1,0:T(8,128)(2,1)S(1)}, u32[]{:S(2)}, u32[]{:S(2)}) collective-permute-start(bf16[4,128,768]{2,1,0:T(8,128)(2,1)S(1)} %pad_maximum_fusion.1.refs_0_), channel_id=1, source_target_pairs={{0,16},{1,17},{16,0},{17,1},{2,18},{3,19},{18,2},{19,3},{4,20},{5,... | collective-permute-start | bytes 2359304 | tf_op jit(solution)/shard_map/ppermute | solution.py:393
  612.8 34.1 %collective-permute-start.51 = (bf16[4,128,768]{2,1,0:T(8,128)(2,1)S(1)}, bf16[4,128,768]{2,1,0:T(8,128)(2,1)}, u32[]{:S(2)}, u32[]{:S(2)}) collective-permute-start(bf16[4,128,768]{2,1,0:T(8,128)(2,1)S(1)} %pad_maximum_fusion.1.refs_0_), channel_id=1, source_target_pairs={{0,1},{1,16},{16,17},{17,0},{2,3},{3,18},{18,19},{19,2},{4,5},{5,2... | collective-permute-start | bytes 2359304 | tf_op jit(solution)/shard_map/ppermute | solution.py:393
  647.8 13.2 %collective-permute-start.55 = (bf16[4,128,768]{2,1,0:T(8,128)(2,1)S(1)}, bf16[4,128,768]{2,1,0:T(8,128)(2,1)}, u32[]{:S(2)}, u32[]{:S(2)}) collective-permute-start(bf16[4,128,768]{2,1,0:T(8,128)(2,1)S(1)} %pad_maximum_fusion.1.refs_0_), channel_id=1, source_target_pairs={{0,8},{8,0},{1,9},{9,1},{2,10},{10,2},{3,11},{11,3},{4,12},{12,4},... | collective-permute-start | bytes 2359304 | tf_op jit(solution)/shard_map/ppermute | solution.py:414
  647.8 14.4 %collective-permute-start.56 = (bf16[4,128,768]{2,1,0:T(8,128)(2,1)}, bf16[4,128,768]{2,1,0:T(8,128)(2,1)}, u32[]{:S(2)}, u32[]{:S(2)}) collective-permute-start(bf16[4,128,768]{2,1,0:T(8,128)(2,1)} %collective-permute-done.51.refs_1_), channel_id=1, source_target_pairs={{0,8},{8,0},{1,9},{9,1},{2,10},{10,2},{3,11},{11,3},{4,12},{12,4},... | collective-permute-start | bytes 2359304 | tf_op jit(solution)/shard_map/ppermute | solution.py:414
  648.3 5.3 collective-permute-start.61
  650.5 8.0 %collective-permute-start.59 = (f32[2,128]{1,0:T(2,128)S(1)}, f32[2,128]{1,0:T(2,128)S(1)}, u32[]{:S(2)}, u32[]{:S(2)}) collective-permute-start(f32[2,128]{1,0:T(2,128)S(1)} %add.368), channel_id=1, source_target_pairs={{0,2},{2,4},{4,6},{6,0},{1,3},{3,5},{5,7},{7,1},{8,10},{10,12},{12... | collective-permute-start | bytes 3080 | tf_op jit(solution)/shard_map/ppermute | solution.py:393
  653.6 9.2 %collective-permute-start.57 = (bf16[4,128,768]{2,1,0:T(8,128)(2,1)S(1)}, bf16[4,128,768]{2,1,0:T(8,128)(2,1)S(1)}, u32[]{:S(2)}, u32[]{:S(2)}) collective-permute-start(bf16[4,128,768]{2,1,0:T(8,128)(2,1)S(1)} %copy-done.21), channel_id=1, source_target_pairs={{0,8},{8,0},{1,9},{9,1},{2,10},{10,2},{3,11},{11,3},{4,12},{12,4},... | collective-permute-start | bytes 2359304 | tf_op jit(solution)/shard_map/ppermute | solution.py:414
  655.0 7.8 %collective-permute-start.58 = (bf16[4,128,768]{2,1,0:T(8,128)(2,1)}, bf16[4,128,768]{2,1,0:T(8,128)(2,1)S(1)}, u32[]{:S(2)}, u32[]{:S(2)}) collective-permute-start(bf16[4,128,768]{2,1,0:T(8,128)(2,1)} %collective-permute-done.53.refs_3_), channel_id=1, source_target_pairs={{0,8},{8,0},{1,9},{9,1},{2,10},{10,2},{3,11},{11,3},{4,12},{12,4},... | collective-permute-start | bytes 2359304 | tf_op jit(solution)/shard_map/ppermute | solution.py:414
  658.5 38.9 %collective-permute-start.50 = (bf16[128,2048]{1,0:T(8,128)(2,1)}, bf16[128,2048]{1,0:T(8,128)(2,1)}, u32[]{:S(2)}, u32[]{:S(2)}) collective-permute-start(bf16[128,2048]{1,0:T(8,128)(2,1)} %get-tuple-element.320), channel_id=1, source_target_pairs={{0,6},{2,0},{4,2},{6,4},{1,7},{3,1},{5,3},{7,5},{8,14},{10,8},{12,... | collective-permute-start | bytes 1572872 | tf_op jit(solution)/shard_map/ppermute | solution.py:400
  661.0 47.0 %collective-permute-start.49 = (bf16[128,2048]{1,0:T(8,128)(2,1)}, bf16[128,2048]{1,0:T(8,128)(2,1)}, u32[]{:S(2)}, u32[]{:S(2)}) collective-permute-start(bf16[128,2048]{1,0:T(8,128)(2,1)} %get-tuple-element.321), channel_id=1, source_target_pairs={{0,4},{2,6},{4,0},{6,2},{1,5},{3,7},{5,1},{7,3},{8,12},{10,14},{12... | collective-permute-start | bytes 1572872 | tf_op jit(solution)/shard_map/ppermute | solution.py:400
  662.2 45.8 %collective-permute-start.48 = (bf16[128,2048]{1,0:T(8,128)(2,1)}, bf16[128,2048]{1,0:T(8,128)(2,1)}, u32[]{:S(2)}, u32[]{:S(2)}) collective-permute-start(bf16[128,2048]{1,0:T(8,128)(2,1)} %get-tuple-element.322), channel_id=1, source_target_pairs={{0,2},{2,4},{4,6},{6,0},{1,3},{3,5},{5,7},{7,1},{8,10},{10,12},{12... | collective-permute-start | bytes 1572872 | tf_op jit(solution)/shard_map/ppermute | solution.py:400
  (82 other events, 806.7 us)
Sparse Core Ops, SparseCore 0:
  9.6 58.0 all-gather.8
  114.7 46.1 all-gather.12
  163.3 67.7 all-gather.10
  318.4 43.3 reduce-scatter.2
  374.8 67.4 reduce-scatter.4
  444.0 47.2 all-gather.14
  505.7 122.1 all-gather.16

commit v2 on v1

--- a/solution.py
+++ b/solution.py
@@ -440,7 +440,7 @@
         sums_ref[...] += values
 
 
-def lay_in_kernel(z_ref, full_ref, gate_ref, up_ref, d_gate_ref, d_up_ref, sums_ref):
+def lay_in_kernel(full_ref, gate_ref, up_ref, d_gate_ref, d_up_ref, sums_ref):
     columns = gate_ref.shape[1] // 2
     total = None
     for core in range(2):
@@ -456,58 +456,64 @@
     add_sums(pl.program_id(1), sums_ref, total)
 
 
-def lay_in(rank, full, w_gate, w_up):
+def lay_in(full, w_gate, w_up):
     n_hi, _, n_ctx, n_shard, rows, both = full.shape
     shape = jax.ShapeDtypeStruct(w_gate.shape, jnp.float32)
-    block = pl.BlockSpec((rows, both), lambda i, j, z: (i, (z[0] - j + n_shard) % n_shard))
+    block = pl.BlockSpec((rows, both), lambda i, j: (i, j))
     return pl.pallas_call(
         lay_in_kernel,
-        grid_spec=pltpu.PrefetchScalarGridSpec(
-            num_scalar_prefetch=1,
-            grid=(n_hi * n_ctx, n_shard),
-            in_specs=[
-                pl.BlockSpec(
-                    (1, 2, 1, 1, rows, both),
-                    lambda i, j, z: (i // n_ctx, 0, i % n_ctx, j, 0, 0),
-                ),
-                block,
-                block,
-            ],
-            out_specs=[block, block, pl.BlockSpec((rows, 128), lambda i, j, z: (i, 0))],
-        ),
+        grid=(n_hi * n_ctx, n_shard),
+        in_specs=[
+            pl.BlockSpec(
+                (1, 2, 1, 1, rows, both), lambda i, j: (i // n_ctx, 0, i % n_ctx, j, 0, 0)
+            ),
+            block,
+            block,
+        ],
+        out_specs=[block, block, pl.BlockSpec((rows, 128), lambda i, j: (i, 0))],
         out_shape=[shape, shape, jax.ShapeDtypeStruct((w_gate.shape[0], 128), jnp.float32)],
-        compiler_params=pltpu.CompilerParams(vmem_limit_bytes=40 << 20),
+        compiler_params=pltpu.CompilerParams(vmem_limit_bytes=60 << 20),
         name="lay_in",
-    )(rank.reshape(1), full, w_gate, w_up)
+    )(full, w_gate, w_up)
 
 
 def lay_rows_kernel(full_ref, out_ref):
-    out_ref[...] = full_ref[...].reshape(out_ref.shape).astype(jnp.float32)
+    n_hi, _, n_ctx, _, rows, columns = full_ref.shape
+    for hi in range(n_hi):
+        for core in range(2):
+            for ctx in range(n_ctx):
+                start = (hi * n_ctx + ctx) * rows
+                out_ref[core * columns : (core + 1) * columns, start : start + rows] = full_ref[
+                    hi, core, ctx, 0
+                ].astype(jnp.float32).T
 
 
 def lay_rows(full):
-    n_hi, _, n_ctx, rows, columns = full.shape
+    n_hi, _, n_ctx, n_shard, rows, columns = full.shape
     n_part = n_hi * n_ctx
     return pl.pallas_call(
         lay_rows_kernel,
-        grid=(2, n_part),
+        grid=(n_shard,),
         in_specs=[
-            pl.BlockSpec(
-                (1, 1, 1, rows, columns), lambda i, j: (j // n_ctx, i, j % n_ctx, 0, 0)
-            )
+            pl.BlockSpec((n_hi, 2, n_ctx, 1, rows, columns), lambda j: (0, 0, 0, j, 0, 0))
         ],
-        out_specs=pl.BlockSpec((rows, columns), lambda i, j: (i * n_part + j, 0)),
-        out_shape=jax.ShapeDtypeStruct((2 * n_part * rows, columns), jnp.float32),
+        out_specs=pl.BlockSpec((2 * columns, n_part * rows), lambda j: (0, j)),
+        out_shape=jax.ShapeDtypeStruct((2 * columns, n_shard * n_part * rows), jnp.float32),
+        compiler_params=pltpu.CompilerParams(vmem_limit_bytes=48 << 20),
         name="lay_rows",
     )(full)
 
 
 def lay_heads_kernel(count, at_ref, *refs):
     mine, theirs = refs[:count], refs[count : 2 * count]
-    wq_ref, wk_ref, wv_ref, dq_ref, dk_ref, dv_ref, d_out_ref, sums_ref = refs[2 * count :]
+    wq_ref, wk_ref, wv_ref, dq_ref, dk_ref, dv_ref, d_out_ref, sums_ref, gains_ref = refs[
+        2 * count :
+    ]
     q_cols, kv_cols = wq_ref.shape[1] // 2, wk_ref.shape[1] // 2
     out_rows = d_out_ref.shape[0] // 2
-    rows = mine[0].shape[1]
+    rows = wq_ref.shape[0] // count
+    gains = mine[0][0, rows:, :].astype(jnp.float32) + theirs[0][0, rows:, :].astype(jnp.float32)
+    add_sums(pl.program_id(0), gains_ref, gains)
 
     @pl.when(pl.program_id(0) == 0)
     def _():
@@ -518,7 +524,7 @@
         here = pl.ds(pl.multiple_of(part * rows, rows), rows)
         total = sums_ref[here, :]
         for core, full_ref in ((at_ref[1], mine[k]), (1 - at_ref[1], theirs[k])):
-            full = full_ref[0].astype(jnp.float32)
+            full = full_ref[0, :rows].astype(jnp.float32)
             start = 0
             for weight_ref, grad_ref, columns in (
                 (wq_ref, dq_ref, q_cols),
@@ -538,15 +544,16 @@
 
 def lay_heads(at, mine, theirs, w_query, key_weight, value_weight):
     n_part = len(mine)
-    n_shard, rows, columns = mine[0].shape
+    n_shard, all_rows, columns = mine[0].shape
+    rows = w_query.shape[0] // n_part
     q_cols = w_query.shape[1] // n_shard
     kv_cols = key_weight.shape[1] // n_shard
     out_rows = 2 * columns - q_cols - 2 * kv_cols
-    block = pl.BlockSpec((1, rows, columns), lambda j, at: (j, 0, 0))
+    block = pl.BlockSpec((1, all_rows, columns), lambda j, at: (j, 0, 0))
 
     def spec(width):
         return pl.BlockSpec(
-            (n_part * rows, width), lambda j, at: (0, lax.rem(at[2] - j + n_shard, n_shard))
+            (n_part * rows, width), lambda j, at: (0, j)
         )
 
     return pl.pallas_call(
@@ -561,6 +568,7 @@
                 spec(kv_cols),
                 pl.BlockSpec((out_rows, n_part * rows), lambda j, at: (0, j)),
                 pl.BlockSpec((n_part * rows, 128), lambda j, at: (0, 0)),
+                pl.BlockSpec((all_rows - rows, columns), lambda j, at: (0, 0)),
             ],
         ),
         out_shape=[
@@ -569,6 +577,7 @@
             jax.ShapeDtypeStruct(value_weight.shape, jnp.float32),
             jax.ShapeDtypeStruct((out_rows, n_shard * n_part * rows), jnp.float32),
             jax.ShapeDtypeStruct((n_part * rows, 128), jnp.float32),
+            jax.ShapeDtypeStruct((all_rows - rows, columns), jnp.float32),
         ],
         compiler_params=pltpu.CompilerParams(vmem_limit_bytes=48 << 20),
         name="lay_heads",
@@ -636,6 +645,28 @@
         out_shape=jax.ShapeDtypeStruct((n_shard * block, columns), pieces[0].dtype),
         name="lay_order",
     )(at, *pieces)
+
+
+def place_kernel(z_ref, *refs):
+    out_ref = refs[-1]
+    count = len(refs) - 1
+    for k, ref in enumerate(refs[:-1]):
+        out_ref[lax.rem(z_ref[0] - k + count, count)] = ref[...]
+
+
+def place(rank, pieces):
+    return pl.pallas_call(
+        place_kernel,
+        grid_spec=pltpu.PrefetchScalarGridSpec(
+            num_scalar_prefetch=1,
+            grid=(1,),
+            in_specs=[pl.BlockSpec(pieces[0].shape, lambda i, z: (0, 0))] * len(pieces),
+            out_specs=pl.BlockSpec((len(pieces),) + pieces[0].shape, lambda i, z: (0, 0, 0)),
+        ),
+        out_shape=jax.ShapeDtypeStruct((len(pieces),) + pieces[0].shape, pieces[0].dtype),
+        compiler_params=pltpu.CompilerParams(vmem_limit_bytes=48 << 20),
+        name="place",
+    )(rank.reshape(1), *pieces)
 
 
 def norm_kernel(z_ref, tokens_ref, gain_ref, out_ref):
@@ -998,14 +1029,17 @@
 def head_gradients_kernel(count, at_ref, *refs):
     normed, branch = refs[: 2 * count], refs[2 * count : 4 * count]
     d_qkv, mixed = refs[4 * count : 4 * count + 2], refs[4 * count + 2 : 4 * count + 4]
+    gains_ref = refs[4 * count + 4]
     down = (((0,), (0,)), ((), ()))
-    for k, out_ref in enumerate(refs[4 * count + 4 :]):
+    slice_rows = normed[0].shape[1]
+    for k, out_ref in enumerate(refs[4 * count + 5 :]):
         split = d_qkv[0].shape[1]
+        out_ref[0, slice_rows:, :] = gains_ref[...]
         for columns, left, right in (
             (slice(0, split), normed, d_qkv),
             (slice(split, out_ref.shape[2]), branch, mixed),
         ):
-            out_ref[0, :, columns] = sum(
+            out_ref[0, :slice_rows, columns] = sum(
                 lax.dot_general(
                     left[core * count + k][...],
                     right[core][...],
@@ -1016,7 +1050,7 @@
             ).astype(jnp.bfloat16)
 
 
-def head_gradients(at, n_part, n_shard, normed, d_branch, d_qkv, mixed):
+def head_gradients(at, n_part, n_shard, normed, d_branch, d_qkv, mixed, gains):
     rows, width = normed[0].shape
     slice_rows = width // (n_part * n_shard)
     columns = d_qkv[0].shape[1] + mixed[0].shape[1]
@@ -1031,16 +1065,17 @@
         return pl.BlockSpec(values.shape, lambda j, at: (0, 0))
 
     specs = [spec(k) for k in range(n_part)] * 2
-    out = pl.BlockSpec((1, slice_rows, columns), lambda j, at: (j, 0, 0))
+    out_rows = slice_rows + gains.shape[0]
+    out = pl.BlockSpec((1, out_rows, columns), lambda j, at: (j, 0, 0))
     return pl.pallas_call(
         partial(head_gradients_kernel, n_part),
         grid_spec=pltpu.PrefetchScalarGridSpec(
             num_scalar_prefetch=1,
             grid=(n_shard,),
-            in_specs=specs + specs + [whole(values) for values in d_qkv + mixed],
+            in_specs=specs + specs + [whole(values) for values in d_qkv + mixed + (gains,)],
             out_specs=[out] * n_part,
         ),
-        out_shape=[jax.ShapeDtypeStruct((n_shard, slice_rows, columns), jnp.bfloat16)] * n_part,
+        out_shape=[jax.ShapeDtypeStruct((n_shard, out_rows, columns), jnp.bfloat16)] * n_part,
         compiler_params=pltpu.CompilerParams(vmem_limit_bytes=48 << 20),
         name="head_gradients",
     )(
@@ -1051,7 +1086,106 @@
         *[d_branch[1]] * n_part,
         *d_qkv,
         *mixed,
-    )
+        gains,
+    )
+
+
+def product_kernel(groups, has_got, *refs):
+    count = sum(n for n, _ in groups)
+    lefts, rights, rest = refs[:count], refs[count : 2 * count], refs[2 * count :]
+    if has_got:
+        got_ref, rest = rest[0], rest[1:]
+    rows = rest[0].shape[1]
+    at = 0
+    for group, (n, contract) in enumerate(groups):
+        total = sum(
+            lax.dot_general(
+                left[...],
+                right[...],
+                (((1,), (contract,)), ((), ())),
+                preferred_element_type=jnp.float32,
+            )
+            for left, right in zip(lefts[at : at + n], rights[at : at + n])
+        )
+        at += n
+        if has_got:
+            total = total + got_ref[group].astype(jnp.float32)
+        for k, ref in enumerate(rest):
+            ref[group] = total[k * rows : (k + 1) * rows].astype(ref.dtype)
+
+
+def product(groups, dtype=jnp.bfloat16, got=None, split=1):
+    rows = groups[0][0][0].shape[0]
+    columns = groups[0][1].shape[1 - groups[0][2]]
+    block = 512 if columns % 512 == 0 else 256
+    left_specs, right_specs, lefts, rights = [], [], [], []
+
+    def right_spec(contract, depth, k):
+        if contract:
+            return pl.BlockSpec((block, depth), lambda j: (j, k))
+        return pl.BlockSpec((depth, block), lambda j: (k, j))
+
+    for terms, right, contract in groups:
+        for k, term in enumerate(terms):
+            depth = term.shape[1]
+            left_specs.append(pl.BlockSpec((rows, depth), lambda j: (0, 0)))
+            right_specs.append(right_spec(contract, depth, k))
+            lefts.append(term)
+            rights.append(right)
+    n = len(groups)
+    in_specs, args = left_specs + right_specs, lefts + rights
+    if got is not None:
+        in_specs = in_specs + [pl.BlockSpec((n, rows, block), lambda j: (0, 0, j))]
+        args = args + [got]
+    dtypes = [dtype] if got is None else [jnp.float32] + [jnp.bfloat16] * (split - 1)
+    outs = pl.pallas_call(
+        partial(
+            product_kernel,
+            [(len(terms), contract) for terms, _, contract in groups],
+            got is not None,
+        ),
+        grid=(columns // block,),
+        in_specs=in_specs,
+        out_specs=[pl.BlockSpec((n, rows // split, block), lambda j: (0, 0, j))] * split,
+        out_shape=[jax.ShapeDtypeStruct((n, rows // split, columns), kind) for kind in dtypes],
+        compiler_params=pltpu.CompilerParams(vmem_limit_bytes=48 << 20),
+        name="product",
+    )(*args)
+    return outs if got is not None else outs[0]
+
+
+def ffn_gradients_kernel(*refs):
+    ffn, cot, d_gate, d_up, inner = (refs[2 * i : 2 * i + 2] for i in range(5))
+    out_ref = refs[10]
+    down = (((0,), (0,)), ((), ()))
+    start = 0
+    for left, right in ((ffn, d_gate), (ffn, d_up), (cot, inner)):
+        stop = start + right[0].shape[1]
+        out_ref[0, :, start:stop] = sum(
+            lax.dot_general(
+                left[core][...], right[core][...], down, preferred_element_type=jnp.float32
+            )
+            for core in range(2)
+        ).astype(jnp.bfloat16)
+        start = stop
+
+
+def ffn_gradients(n_shard, ffn_in, cot, d_gate, d_up, inner):
+    rows, width = ffn_in[0].shape
+    ff = inner[0].shape[1]
+    block = 256
+    per = width // (n_shard * block)
+    left = pl.BlockSpec((rows, block), lambda j: (0, j))
+    right = pl.BlockSpec((rows, ff), lambda j: (0, 0))
+    return pl.pallas_call(
+        ffn_gradients_kernel,
+        grid=(width // block,),
+        in_specs=[left] * 4 + [right] * 6,
+        out_specs=pl.BlockSpec((1, block, 3 * ff), lambda j: (j // per, j % per, 0)),
+        out_shape=jax.ShapeDtypeStruct((n_shard, width // n_shard, 3 * ff), jnp.bfloat16),
+        compiler_params=pltpu.CompilerParams(vmem_limit_bytes=56 << 20),
+        name="ffn_gradients",
+    )(*ffn_in, *cot, *d_gate, *d_up, *inner)
 
 
 def reorder_kernel(z_ref, in_ref, out_ref):
@@ -1151,21 +1285,12 @@
     ff = w_down.shape[0] // 2
 
     slice_rows = w_query.shape[0] // n_part
-    plain = (((1,), (0,)), ((), ()))
-    turned = (((1,), (1,)), ((), ()))
-
-    def product(left, right, dims):
-        return lax.dot_general(left, right, dims, preferred_element_type=f32)
-
     def exchange(pieces):
         return lax.all_to_all(pieces, "shard", 0, 0, tiled=True)
 
     def gather_plane(values):
         full = lax.all_gather(values, ("hi", "core", "ctx"), axis=0)
         return full.reshape((n_hi, 2, n_ctx) + values.shape)
-
-    def send_blocks(mine):
-        return [mine[k * own : (k + 1) * own] for k in range(n_shard)]
 
     own_tokens = tokens.reshape(own, width)
     own_cot = cotangent.reshape(own, width)
@@ -1173,14 +1298,15 @@
     gathered = lax.all_gather(own_tokens, "shard", axis=0)
     pieces_qkv = take_columns(at, n_part, n_shard, (w_query, key_weight, value_weight))
     pieces_in = take_columns(at, n_part, n_shard, (w_gate, w_up))
-    got_qkv = after(exchange(pieces_qkv), pieces_in)
+    gain_sizes = (attn_gain.shape[0], query_gain.shape[0], key_gain.shape[0], ffn_gain.shape[0])
+    gains = after(jnp.concatenate([attn_gain, query_gain, key_gain, ffn_gain]), pieces_qkv)
+    gains = from_ring(gains, "shard", n_shard)
+    starts = after(span_starts.reshape(micro), pieces_qkv)
+    starts = jnp.stack([starts, swap(starts, "core")])
+    got_qkv = after(exchange(pieces_qkv), pieces_in, gains, starts)
+    gains = in_order(gains, z).astype(f32)
     w_out_rows = lax.dynamic_slice_in_dim(w_out, c * q_cols, q_cols, axis=0)
     w_down_rows = lax.dynamic_slice_in_dim(w_down, c * ff, ff, axis=0)
-    gain_sizes = (attn_gain.shape[0], query_gain.shape[0], key_gain.shape[0], ffn_gain.shape[0])
-    gains = after(jnp.concatenate([attn_gain, query_gain, key_gain, ffn_gain]), got_qkv)
-    gains = in_order(from_ring(gains, "shard", n_shard), z).astype(f32)
-    starts = after(span_starts.reshape(micro), got_qkv)
-    starts = jnp.stack([starts, swap(starts, "core")])
     ring_qkv = from_ring(got_qkv, ("hi", "ctx"), n_part)
     gathered = after(gathered, ring_qkv, gains, starts)
     ends = [0]
@@ -1217,11 +1343,12 @@
     cot_all = lax.all_gather(after(own_cot, gathered), "shard", axis=0)
     turns = (cosine, sine, gain_query, gain_key)
     q_mine, kv_mine, pre_mine = project(at, q_cols, normed_mine, ring_qkv, *turns)
-    kv_mine_parts = from_ring(kv_mine, "ctx", n_ctx)
     q_theirs, kv_theirs, pre_theirs = project(
         at, q_cols, after(normed_theirs, kv_mine), ring_qkv, *turns
     )
-    kv_theirs_parts = from_ring(kv_theirs, "ctx", n_ctx)
+    kv_parts = from_ring(jnp.concatenate([kv_mine, kv_theirs], axis=0), "ctx", n_ctx)
+    kv_mine_parts = [values[:group] for values in kv_parts]
+    kv_theirs_parts = [values[group:] for values in kv_parts]
     w_qkv = lay_order(at, after(ring_qkv, kv_theirs))
     mixed_mine = attend(
         0, starts, *order, after(q_mine, w_qkv), kv_mine_parts, query_pos, key_pos
@@ -1229,66 +1356,65 @@
     mixed_theirs = attend(
         1, starts, *order, after(q_theirs, mixed_mine), kv_theirs_parts, query_pos, key_pos
     )
-    got_in = in_order(after(got_in, mixed_theirs), z)
+    def core_sum(mine, theirs, right, contract):
+        got = swap(product([(theirs, right, contract)]), "core")
+        pieces = product([(mine, right, contract)], got=got, split=n_shard)
+        return [piece[0] for piece in pieces]
+
+    branch_sent = core_sum([mixed_mine], [mixed_theirs], w_out_rows, 0)
+    hidden_in = own_tokens.astype(f32)
+    got_in = place(z, after(got_in, branch_sent))
+    cot_all = after(cot_all, got_in)
     w_in = lax.all_gather(after(got_in, cot_all), ("hi", "ctx"), axis=1, tiled=True)
     w_in = w_in.reshape(width, -1)
-
-    def core_sum(mine, theirs, right, dims):
-        sent = product(theirs, right, dims).astype(bf16)
-        kept = product(after(mine, sent), right, dims)
-        return kept + after(swap(sent, "core"), kept).astype(f32)
-
-    branch = core_sum(mixed_mine, mixed_theirs, w_out_rows, plain)
-    hidden_in = own_tokens.astype(f32)
-    branch_sent = send_blocks(branch)
-    cot_mine = ring_order(z, after(cot_all, branch))
+    cot_mine = ring_order(z, cot_all)
     cot_theirs = swap(cot_mine, "core")
     branch_terms = send_terms(branch_sent, "shard", n_shard)
-    middle = hidden_in + sum_terms(after(branch_terms, w_in, cot_mine))
+    middle = hidden_in + sum_terms(after(branch_terms, cot_mine))
 
     recip_m = recip_rms(middle)
     unit_m = middle * recip_m
     ffn_own = (unit_m * gain_ffn).astype(bf16)
     ffn_ring = from_ring(ffn_own, "shard", n_shard)
-    d_inner_mine = product(after(cot_mine, ffn_own), w_down_rows, turned)
-    d_inner_theirs = product(after(cot_theirs, d_inner_mine), w_down_rows, turned)
-    ffn_mine = jnp.concatenate(after(ffn_ring, d_inner_theirs), axis=0)
+    d_inner_mine = product([([after(cot_mine, ffn_own)], w_down_rows, 1)], f32)[0]
+    d_inner_theirs = product([([after(cot_theirs, d_inner_mine)], w_down_rows, 1)], f32)[0]
+    ffn_mine = jnp.concatenate(after(ffn_ring, d_inner_theirs, w_in), axis=0)
     ffn_theirs = swap(ffn_mine, "core")
     inner_mine, d_gate_mine, d_up_mine = inner_parts(ffn_mine, w_in, d_inner_mine)
     inner_theirs, d_gate_theirs, d_up_theirs = inner_parts(
         after(ffn_theirs, inner_mine), w_in, d_inner_theirs
     )
-    d_pre_mine = jnp.concatenate([d_gate_mine, d_up_mine], axis=1)
-    d_pre_theirs = jnp.concatenate([d_gate_theirs, d_up_theirs], axis=1)
-    d_ffn = core_sum(d_pre_mine, d_pre_theirs, w_in, turned)
-    d_ffn_sent = send_blocks(d_ffn)
-    inner_act = jnp.concatenate([after(inner_mine, d_ffn), inner_theirs], axis=0)
-    cot_rows = jnp.concatenate([cot_mine, cot_theirs], axis=0)
-    grad_rows = over_rows(inner_act, cot_rows).astype(bf16)
-    part_down = lax.psum_scatter(grad_rows, ("hi", "ctx"), scatter_dimension=0, tiled=True)
-    ffn_in = jnp.concatenate([after(ffn_mine, grad_rows), ffn_theirs], axis=0)
-    d_pre = jnp.concatenate([after(d_pre_mine, grad_rows), d_pre_theirs], axis=0)
-    grad_in = over_rows(ffn_in, d_pre).astype(bf16).reshape(n_shard, n_part * slice_rows, -1)
-    d_ffn_in = sum_terms(after(send_terms(d_ffn_sent, "shard", n_shard), grad_in))
+    grad_in = ffn_gradients(
+        n_shard,
+        (ffn_mine, ffn_theirs),
+        (cot_mine, cot_theirs),
+        (d_gate_mine, d_gate_theirs),
+        (d_up_mine, d_up_theirs),
+        (inner_mine, inner_theirs),
+    )
+    part_in = lax.psum_scatter(grad_in, ("hi", "ctx"), scatter_dimension=1, tiled=True)
+    d_ffn_sent = core_sum(
+        [d_gate_mine, d_up_mine], [after(d_gate_theirs, grad_in), d_up_theirs], w_in, 1
+    )
+    d_ffn_in = sum_terms(send_terms(d_ffn_sent, "shard", n_shard))
     d_middle = own_cot.astype(f32) + norm_back(unit_m, recip_m, gain_ffn, d_ffn_in)
 
     d_branch_own = d_middle.astype(bf16)
     branch_ring = from_ring(d_branch_own, "shard", n_shard)
-    part_in = lax.psum_scatter(
-        after(grad_in, part_down, d_branch_own), ("hi", "ctx"), scatter_dimension=1, tiled=True
-    )
-    branch_mine = jnp.concatenate(after(branch_ring, part_down), axis=0)
+    branch_mine, part_in = lax.optimization_barrier((jnp.concatenate(branch_ring, axis=0), part_in))
     branch_theirs = swap(branch_mine, "core")
-    d_mixed_mine = product(branch_mine, w_out_rows, turned).astype(bf16)
+    d_mixed_mine = product([([branch_mine], w_out_rows, 1)])[0]
     tables = (query_pos, key_pos, cosine, sine, gain_query)
     d_q_mine, gain_q_mine, d_kv_mine = attend_back(
         0, starts, *order, q_mine, pre_mine, kv_mine_parts, d_mixed_mine, *tables
     )
-    d_mixed_theirs = product(after(branch_theirs, d_q_mine), w_out_rows, turned).astype(bf16)
+    d_mixed_theirs = product([([after(branch_theirs, d_q_mine)], w_out_rows, 1)])[0]
     d_q_theirs, gain_q_theirs, d_kv_theirs = attend_back(
         1, starts, *order, q_theirs, pre_theirs, kv_theirs_parts, d_mixed_theirs, *tables
     )
-    part_in = after(part_in, d_q_theirs)
+
+    sent_in = exchange_ring(part_in[..., : 2 * ff], z, n_shard)
+    full_down = gather_plane(part_in[..., 2 * ff :])
 
     def keys_gradient(d_queries, d_kv, pre, *others):
         got = [
@@ -1302,49 +1428,50 @@
     d_qkv_theirs, gain_k_theirs = keys_gradient(
         d_q_theirs, d_kv_theirs, pre_theirs, d_qkv_mine
     )
-    sent_in = exchange_ring(part_in, z, n_shard)
-    full_rows = gather_plane(after(part_down, part_in))
-    d_in = core_sum(d_qkv_mine, after(d_qkv_theirs, part_in), w_qkv, turned)
-    sent_in = jnp.stack(after(sent_in, d_in))
+    sent_in = place(z, after(sent_in, d_qkv_theirs))
+    qkv_cols = q_cols + 2 * kv_cols
+    head_columns = qkv_cols + q_cols
+    full_in = gather_plane(after(sent_in, full_down))
+    head_gains = jnp.concatenate([gain_q_mine + gain_q_theirs, gain_k_mine + gain_k_theirs])
+    head_gains = jnp.zeros((16, head_columns), f32).at[0, : 2 * HEAD_SIZE].set(head_gains)
     sent = head_gradients(
         at,
         n_part,
         n_shard,
         (normed_mine, normed_theirs),
         (branch_mine, branch_theirs),
-        (after(d_qkv_mine, d_in, sent_in), d_qkv_theirs),
+        (after(d_qkv_mine, sent_in), d_qkv_theirs),
         (mixed_mine, mixed_theirs),
+        head_gains.astype(bf16),
     )
     part_heads = send_terms(sent, ("hi", "ctx"), n_part)
-    full_in = gather_plane(after(sent_in, full_rows))
-    head_gains = jnp.stack([gain_q_mine + gain_q_theirs, gain_k_mine + gain_k_theirs])
-    head_gains = sum(after(from_ring(head_gains, "core", 2), sent))
-    part_heads = sum_terms(after(part_heads, head_gains)).astype(bf16)
-    qkv_cols = q_cols + 2 * kv_cols
-    ring_heads = exchange_ring(part_heads[..., :qkv_cols], z, n_shard)
-    head_gains = sum(after(from_ring(head_gains, "hi", n_hi), part_heads))
-    d_normed = send_terms(send_blocks(after(d_in, ring_heads)), "shard", n_shard)
-    ring_heads = after(ring_heads, head_gains)
-    part_heads = jnp.concatenate([jnp.stack(ring_heads), part_heads[..., qkv_cols:]], axis=-1)
+    got = product([([after(d_qkv_theirs, sent)], w_qkv, 1), ([inner_theirs], w_down_rows, 0)])
+    part_heads = sum_terms(after(part_heads, got)).astype(bf16)
+    last = product(
+        [([after(d_qkv_mine, part_heads)], w_qkv, 1), ([inner_mine], w_down_rows, 0)],
+        got=swap(got, "core"),
+        split=n_shard,
+    )
+    ring_heads = exchange(part_heads[..., :qkv_cols])
+    ring_heads = after(ring_heads, last)
+    last = send_terms(last, "shard", n_shard)
+    part_heads = jnp.concatenate([ring_heads, part_heads[..., qkv_cols:]], axis=-1)
     mine_heads = from_ring(part_heads, ("hi", "ctx"), n_part)
-    result = core_sum(after(inner_mine, part_heads), inner_theirs, w_down_rows, plain)
-    grad_down = lay_rows(after(full_rows, result))
-    head_gains = sum(after(from_ring(head_gains, "ctx", n_ctx), grad_down))
-    d_normed = sum_terms(after(d_normed, grad_down))
+    grad_down = lay_rows(after(full_down, part_heads))
+    grad_gate, grad_up, ffn_sums = lay_in(after(full_in, grad_down), w_gate, w_up)
+    mine_heads = after(mine_heads, grad_gate)
+    theirs_heads = [swap(values, "core") for values in mine_heads]
+    last = sum_terms(after(last, mine_heads))
     recip_h = recip_rms(hidden_in)
     unit_h = hidden_in * recip_h
-    input_grad = d_middle + norm_back(unit_h, recip_h, gain_attn, d_normed)
-    result = send_terms(send_blocks(after(result, input_grad)), "shard", n_shard)
-    mine_heads = after(mine_heads, head_gains, input_grad)
-    theirs_heads = [swap(values, "core") for values in mine_heads]
-    head_gains = sum(from_ring(after(head_gains, mine_heads), "shard", n_shard))
+    input_grad = d_middle + norm_back(unit_h, recip_h, gain_attn, last[0])
+    result = (middle + last[1]).astype(bf16)
+    grad_query, grad_key, grad_value, grad_out, attn_sums, gain_sums = lay_heads(
+        at, mine_heads, theirs_heads, w_query, key_weight, value_weight
+    )
+    head_gains = gain_sums[0, : 2 * HEAD_SIZE].reshape(2, HEAD_SIZE)
     head_size = query_gain.shape[0]
     head_gains = lax.dynamic_slice_in_dim(head_gains, z * head_size, head_size, axis=1)
-    grad_query, grad_key, grad_value, grad_out, attn_sums = lay_heads(
-        at, mine_heads, theirs_heads, w_query, key_weight, value_weight
-    )
-    grad_gate, grad_up, ffn_sums = lay_in(z, after(full_in, grad_query), w_gate, w_up)
-    result = (middle + sum_terms(after(result, grad_gate))).astype(bf16)
     grad_ffn_gain = jnp.sum(ffn_sums, axis=1) / ffn_gain.astype(f32)
     grad_attn_gain = jnp.sum(attn_sums, axis=1) / attn_gain.astype(f32)
 

time: 730 us -> 689 us (0.944)
  the two profiles are of different devices: /device:TPU:0 before, /device:TPU:14 now
where the time goes in v2:
time: 689 us; the launch traced here: 686 us
  waiting for transfers between devices  354 us (51%)
  Pallas kernels  181 us (26%)
  starting transfers between devices  60.8 us (9%)
  local copies, waits for them, and re-layouts  53.3 us (8%)
  other arithmetic  22.5 us (3%)
  between operations  15.4 us (2%)
    ppermute x12, waiting for transfers between devices, send_terms(): lax.ppermute(pieces[count - k].astype(jnp.bfloat16), axis, [(i, (i + k) %...  169 us
    ppermute x16, waiting for transfers between devices, from_ring(): lax.ppermute(block, axis, [(i, (i + k) % count) for i in range(count)])  134 us
    pallas_call x10, Pallas kernels, product(): pl.pallas_call(partial(product_kernel, [(len(terms), contract) for terms,...  43 us
    unnamed x217, local copies, waits for them, and re-layouts  37 us
    ppermute x6, waiting for transfers between devices, exchange_ring(): lax.ppermute(piece_for(k), 'shard', [(i, (i + k) % count) for i in range(...  32.3 us
    ppermute x16, starting transfers between devices, from_ring(): lax.ppermute(block, axis, [(i, (i + k) % count) for i in range(count)])  23.2 us
    pallas_call x1, Pallas kernels, lay_in(): pl.pallas_call(lay_in_kernel, grid=(n_hi * n_ctx, n_shard), in_specs=[pl....  22.8 us
    pallas_call x1, Pallas kernels, ffn_gradients(): pl.pallas_call(ffn_gradients_kernel, grid=(width // block,), in_specs=[le...  15.9 us
  transfers between devices with their start and end apart: 56, of which 31 were waited for; matrix products, arithmetic and copies ran while one was open for 5% of the time, Pallas kernels for 21%

profile of v2, /device:TPU:14, one launch (start us, length us, event | category | flops | bytes accessed | tf_op | source)
XLA Modules:
  0.0 686.0 jit_solution(2168340980087495517)
XLA Ops:
  8.6 3.9 take_columns.2
  12.5 5.3 all-to-all-start
  22.3 4.3 take_columns.3
  26.6 18.2 %collective-permute-done.1 = bf16[1088]{0:T(1024)(128)(2,1)S(1)} collective-permute-done((bf16[1088]{0:T(1024)(128)(2,1)S(1)}, bf16[1088]{0:T(1024)(128)(2,1)S(1)}, u32[]{:S(2)}, u32[]{:S(2)}) %collective-permute-start.1) | collective-permute-done | bytes 2208 | tf_op jit(solution)/shard_map/ppermute | solution.py:393
  49.4 9.5 %collective-permute-done.4.refs_5_.refs_1_ = bf16[4,128,512]{2,1,0:T(8,128)(2,1)S(1)} collective-permute-done((bf16[4,128,512]{2,1,0:T(8,128)(2,1)S(1)}, bf16[4,128,512]{2,1,0:T(8,128)(2,1)S(1)}, u32[]{:S(2)}, u32[]{:S(2)}) %collective-permute-start.4) | collective-permute-done | bytes 524320 | tf_op jit(solution)/shard_map/ppermute | solution.py:393
  58.8 5.9 collective-permute-done.5.refs_6_.refs_2_
  64.8 4.2 norm_group.1.refs_0_.refs_1_.refs_2_.refs_3_
  76.2 6.9 %project.2 = (bf16[512,256]{1,0:T(8,128)(2,1)S(1)}, bf16[512,256]{1,0:T(8,128)(2,1)S(1)}, f32[512,384]{1,0:T(8,128)S(1)}) custom-call(s32[3]{0:T(128)S(1)} %copy-done.68, bf16[512,2048]{1,0:T(8,128)(2,1)S(1)} %copy-done.2, bf16[512,2048]{1,0:T(8,128)(2,1)S(1)} %copy-done.2, bf16[512,2048]{1,0:T(8,128)(2,1)S(1)} %copy-done.2, ...), custom_call_target="tpu_custom_call" | custom-call | tf_op jit(solution)/shard_map/project/pallas_call | solution.py:755
  84.9 7.0 %project.3 = (bf16[512,256]{1,0:T(8,128)(2,1)S(1)}, bf16[512,256]{1,0:T(8,128)(2,1)S(1)}, f32[512,384]{1,0:T(8,128)S(1)}) custom-call(s32[3]{0:T(128)S(1)} %copy-done.68, bf16[512,2048]{1,0:T(8,128)(2,1)} %collective-permute-done.7.refs_0_.refs_1_.refs_2_.refs_3_.refs_4_.refs_5_.refs_6_.refs_7_, ...), custom_call_target="tpu_custom_call" | custom-call | tf_op jit(solution)/shard_map/project/pallas_call | solution.py:755
  95.7 4.6 lay_order.1.refs_2_
  100.3 7.8 %collective-permute-done.8 = bf16[1024,256]{1,0:T(8,128)(2,1)} collective-permute-done((bf16[1024,256]{1,0:T(8,128)(2,1)}, bf16[1024,256]{1,0:T(8,128)(2,1)}, u32[]{:S(2)}, u32[]{:S(2)}) %collective-permute-start.8) | collective-permute-done | bytes 524320 | tf_op jit(solution)/shard_map/ppermute | solution.py:393
  109.2 2.8 attend.2
  112.1 2.8 attend.3
  115.0 2.6 product.10
  119.8 4.4 collective-permute-start.14
  128.4 3.4 collective-permute-done.13.refs_1_
  131.8 22.6 %collective-permute-done.14.refs_2_ = bf16[128,1536]{1,0:T(8,128)(2,1)S(1)} collective-permute-done((bf16[128,1536]{1,0:T(8,128)(2,1)S(1)}, bf16[128,1536]{1,0:T(8,128)(2,1)S(1)}, u32[]{:S(2)}, u32[]{:S(2)}) %collective-permute-start.14) | collective-permute-done | bytes 393248 | tf_op jit(solution)/shard_map/ppermute | solution.py:592
  154.4 3.8 collective-permute-done.15.refs_3_
  159.6 3.9 ring_order.1.refs_0_.refs_2_
  165.6 12.8 %collective-permute-done.10 = bf16[128,2048]{1,0:T(8,128)(2,1)S(1)} collective-permute-done((bf16[128,2048]{1,0:T(8,128)(2,1)}, bf16[128,2048]{1,0:T(8,128)(2,1)S(1)}, u32[]{:S(2)}, u32[]{:S(2)}) %collective-permute-start.10) | collective-permute-done | bytes 524320 | tf_op jit(solution)/shard_map/ppermute | solution.py:400
  178.4 31.1 %collective-permute-done.11 = bf16[128,2048]{1,0:T(8,128)(2,1)S(1)} collective-permute-done((bf16[128,2048]{1,0:T(8,128)(2,1)S(1)}, bf16[128,2048]{1,0:T(8,128)(2,1)S(1)}, u32[]{:S(2)}, u32[]{:S(2)}) %collective-permute-start.11) | collective-permute-done | bytes 524320 | tf_op jit(solution)/shard_map/ppermute | solution.py:400
  212.3 3.3 collective-permute-start.17
  217.6 4.1 constant_dynamic-slice_fusion.1.refs_1_.refs_3_
  221.8 4.0 product.12
  226.9 4.7 product.13
  232.8 25.3 %collective-permute-done.17 = bf16[128,2048]{1,0:T(8,128)(2,1)} collective-permute-done((bf16[128,2048]{1,0:T(8,128)(2,1)}, bf16[128,2048]{1,0:T(8,128)(2,1)}, u32[]{:S(2)}, u32[]{:S(2)}) %collective-permute-start.17) | collective-permute-done | bytes 524320 | tf_op jit(solution)/shard_map/ppermute | solution.py:393
  258.1 3.6 collective-permute-done.18
  266.3 6.8 inner_parts.2
  275.0 7.0 %inner_parts.3 = (bf16[512,768]{1,0:T(8,128)(2,1)S(1)}, bf16[512,768]{1,0:T(8,128)(2,1)S(1)}, bf16[512,768]{1,0:T(8,128)(2,1)S(1)}) custom-call(bf16[512,2048]{1,0:T(8,128)(2,1)S(1)} %collective-permute-done.20.ffn_ref.refs_1_, bf16[2048,1536]{1,0:T(8,128)(2,1)} %bitcast.181, bf16[2048,1536]{1,0:T(8,128)(2,1)} %bitcast.182, f32[512,768]{1,0:T(8,128)S(1)} %bitcast.140), custom_call_target="tpu_custom_call" | custom-call | tf_op jit(solution)/shard_map/inner_parts/pallas_call | solution.py:1234
  284.7 15.9 %ffn_gradients.1 = bf16[4,512,2304]{2,1,0:T(8,128)(2,1)} custom-call(bf16[512,2048]{1,0:T(8,128)(2,1)} %copy-done.6, bf16[512,2048]{1,0:T(8,128)(2,1)} %copy-done.9, bf16[512,2048]{1,0:T(8,128)(2,1)} %ring_order.1.refs_0_.refs_2_, bf16[512,2048]{1,0:T(8,128)(2,1)} %collective-permute-done.19.refs_0_.refs_3_, bf16[512,768]{1,0:T(8,128)(2,1)} %copy-done.20, ...), custom_call_target="tpu_custom_call" | custom-call | tf_op jit(solution)/shard_map/ffn_gradients/pallas_call | solution.py:1180
  302.9 6.3 product.14
  309.6 3.9 collective-permute-done.21.refs_4_
  314.8 6.7 product.15
  324.1 34.8 %collective-permute-done.24 = bf16[128,2048]{1,0:T(8,128)(2,1)S(1)} collective-permute-done((bf16[128,2048]{1,0:T(8,128)(2,1)S(1)}, bf16[128,2048]{1,0:T(8,128)(2,1)S(1)}, u32[]{:S(2)}, u32[]{:S(2)}) %collective-permute-start.24) | collective-permute-done | bytes 524320 | tf_op jit(solution)/shard_map/ppermute | solution.py:400
  358.9 8.2 %collective-permute-done.22 = bf16[128,2048]{1,0:T(8,128)(2,1)S(1)} collective-permute-done((bf16[128,2048]{1,0:T(8,128)(2,1)S(1)}, bf16[128,2048]{1,0:T(8,128)(2,1)S(1)}, u32[]{:S(2)}, u32[]{:S(2)}) %collective-permute-start.22) | collective-permute-done | bytes 524320 | tf_op jit(solution)/shard_map/ppermute | solution.py:400
  369.0 3.7 collective-permute-start.27
  374.2 10.2 %collective-permute-done.27 = bf16[128,2048]{1,0:T(8,128)(2,1)S(1)} collective-permute-done((bf16[128,2048]{1,0:T(8,128)(2,1)S(1)}, bf16[128,2048]{1,0:T(8,128)(2,1)S(1)}, u32[]{:S(2)}, u32[]{:S(2)}) %collective-permute-start.27) | collective-permute-done | bytes 524320 | tf_op jit(solution)/shard_map/ppermute | solution.py:393
  384.3 21.3 %collective-permute-done.26 = bf16[128,2048]{1,0:T(8,128)(2,1)S(1)} collective-permute-done((bf16[128,2048]{1,0:T(8,128)(2,1)S(1)}, bf16[128,2048]{1,0:T(8,128)(2,1)S(1)}, u32[]{:S(2)}, u32[]{:S(2)}) %collective-permute-start.26) | collective-permute-done | bytes 524320 | tf_op jit(solution)/shard_map/ppermute | solution.py:393
  405.6 11.1 %collective-permute-done.25 = bf16[128,2048]{1,0:T(8,128)(2,1)S(1)} collective-permute-done((bf16[128,2048]{1,0:T(8,128)(2,1)S(1)}, bf16[128,2048]{1,0:T(8,128)(2,1)S(1)}, u32[]{:S(2)}, u32[]{:S(2)}) %collective-permute-start.25) | collective-permute-done | bytes 524320 | tf_op jit(solution)/shard_map/ppermute | solution.py:393
  428.1 2.9 product.16
  431.1 4.5 attend_back.2
  438.3 4.4 attend_back.3
  445.8 2.7 keys_back.2
  448.6 7.5 %collective-permute-done.33.refs_2_ = bf16[512,256]{1,0:T(8,128)(2,1)S(1)} collective-permute-done((bf16[512,256]{1,0:T(8,128)(2,1)S(1)}, bf16[512,256]{1,0:T(8,128)(2,1)S(1)}, u32[]{:S(2)}, u32[]{:S(2)}) %collective-permute-start.33) | collective-permute-done | bytes 262176 | tf_op jit(solution)/shard_map/ppermute | solution.py:1421
  456.8 2.7 keys_back.3
  464.6 6.0 all-gather.15.cloned.1.call-done
  475.1 8.1 %head_gradients.1 = (bf16[4,144,768]{2,1,0:T(8,128)(2,1)S(1)}, bf16[4,144,768]{2,1,0:T(8,128)(2,1)S(1)}, bf16[4,144,768]{2,1,0:T(8,128)(2,1)S(1)}, bf16[4,144,768]{2,1,0:T(8,128)(2,1)S(1)}) custom-call(s32[3]{0:T(128)S(1)} %copy-done.69, bf16[512,2048]{1,0:T(8,128)(2,1)} %norm_group.1.refs_0_.refs_1_.refs_2_.refs_3_, ...), custom_call_target="tpu_custom_call" | custom-call | tf_op jit(solution)/shard_map/head_gradients/pallas_call | solution.py:1070
  483.3 6.5 product.18
  493.8 25.7 %collective-permute-done.34 = bf16[4,144,768]{2,1,0:T(8,128)(2,1)S(1)} collective-permute-done((bf16[4,144,768]{2,1,0:T(8,128)(2,1)S(1)}, bf16[4,144,768]{2,1,0:T(8,128)(2,1)S(1)}, u32[]{:S(2)}, u32[]{:S(2)}) %collective-permute-start.34) | collective-permute-done | bytes 884768 | tf_op jit(solution)/shard_map/ppermute | solution.py:400
  519.5 18.0 %collective-permute-done.35 = bf16[4,144,768]{2,1,0:T(8,128)(2,1)S(1)} collective-permute-done((bf16[4,144,768]{2,1,0:T(8,128)(2,1)S(1)}, bf16[4,144,768]{2,1,0:T(8,128)(2,1)S(1)}, u32[]{:S(2)}, u32[]{:S(2)}) %collective-permute-start.35) | collective-permute-done | bytes 884768 | tf_op jit(solution)/shard_map/ppermute | solution.py:400
  537.5 4.0 collective-permute-done.36
  542.8 5.1 all-to-all-start.1
  550.9 6.9 %product.19 = (f32[2,128,2048]{2,1,0:T(8,128)}, bf16[2,128,2048]{2,1,0:T(8,128)(2,1)S(1)}, bf16[2,128,2048]{2,1,0:T(8,128)(2,1)S(1)}, bf16[2,128,2048]{2,1,0:T(8,128)(2,1)S(1)}) custom-call(bf16[512,512]{1,0:T(8,128)(2,1)S(1)} %copy-done.51, bf16[512,768]{1,0:T(8,128)(2,1)S(1)} %copy-done.29, bf16[2048,512]{1,0:T(8,128)(2,1)} %lay_order.1.refs_2_, ...), custom_call_target="tpu_custom_call" | custom-call | tf_op jit(solution)/shard_map/product/pallas_call | solution.py:1141
  561.5 2.6 collective-permute-start.41
  565.6 4.3 collective-permute-start.39
  570.4 20.6 %collective-permute-done.41.refs_1_ = bf16[4,144,768]{2,1,0:T(8,128)(2,1)S(1)} collective-permute-done((bf16[4,144,768]{2,1,0:T(8,128)(2,1)S(1)}, bf16[4,144,768]{2,1,0:T(8,128)(2,1)S(1)}, u32[]{:S(2)}, u32[]{:S(2)}) %collective-permute-start.41) | collective-permute-done | bytes 884768 | tf_op jit(solution)/shard_map/ppermute | solution.py:393
  592.8 8.5 %lay_rows.1 = f32[1536,2048]{1,0:T(8,128)} custom-call(bf16[2,2,2,4,128,768]{5,4,3,2,1,0:T(8,128)(2,1)} %bitcast.189), custom_call_target="tpu_custom_call" | custom-call | tf_op jit(solution)/shard_map/lay_rows/pallas_call | solution.py:494
  601.2 22.8 %lay_in.1 = (f32[512,6144]{1,0:T(8,128)}, f32[512,6144]{1,0:T(8,128)}, f32[512,128]{1,0:T(8,128)}) custom-call(bf16[2,2,2,4,128,1536]{5,4,3,2,1,0:T(8,128)(2,1)} %bitcast.188, bf16[512,6144]{1,0:T(8,128)(2,1)} %gate_ref.1, bf16[512,6144]{1,0:T(8,128)(2,1)} %up_ref.1), custom_call_target="tpu_custom_call" | custom-call | tf_op jit(solution)/shard_map/lay_in/pallas_call | solution.py:463
  624.7 9.4 %collective-permute-done.38 = bf16[2,128,2048]{2,1,0:T(8,128)(2,1)} collective-permute-done((bf16[2,128,2048]{2,1,0:T(8,128)(2,1)S(1)}, bf16[2,128,2048]{2,1,0:T(8,128)(2,1)}, u32[]{:S(2)}, u32[]{:S(2)}) %collective-permute-start.38) | collective-permute-done | bytes 1048608 | tf_op jit(solution)/shard_map/ppermute | solution.py:400
  634.0 20.5 %collective-permute-done.39 = bf16[2,128,2048]{2,1,0:T(8,128)(2,1)} collective-permute-done((bf16[2,128,2048]{2,1,0:T(8,128)(2,1)}, bf16[2,128,2048]{2,1,0:T(8,128)(2,1)}, u32[]{:S(2)}, u32[]{:S(2)}) %collective-permute-start.39) | collective-permute-done | bytes 1048608 | tf_op jit(solution)/shard_map/ppermute | solution.py:400
  654.5 4.0 collective-permute-done.40
  658.6 3.1 convert_add_fusion
  664.1 4.0 fusion.11
  668.1 9.7 %lay_heads.1 = (f32[512,2048]{1,0:T(8,128)}, f32[512,1024]{1,0:T(8,128)}, f32[512,1024]{1,0:T(8,128)}, f32[512,2048]{1,0:T(8,128)}, f32[512,128]{1,0:T(8,128)S(1)}, /*index=5*/f32[16,768]{1,0:T(8,128)S(1)}) custom-call(s32[3]{0:T(128)S(1)} %copy-done.69, bf16[4,144,768]{2,1,0:T(8,128)(2,1)S(1)} %copy-done.19, bf16[4,144,768]{2,1,0:T(8,128)(2,1)S(1)} %copy-done.63, ...), custom_call_target="tpu_custom_call" | custom-call | tf_op jit(solution)/shard_map/lay_heads/pallas_call | solution.py:559
  (373 shorter events, 107.2 us)
Async XLA Ops:
  7.2 88.4 %copy-start = (bf16[512,2048]{1,0:T(8,128)(2,1)S(1)}, bf16[512,2048]{1,0:T(8,128)(2,1)}, u32[]{:S(2)}) copy-start(bf16[512,2048]{1,0:T(8,128)(2,1)} %param.22) | copy-start | bytes 6291460
  7.2 57.6 %all-gather.9.cloned.1.call-start = ((), (), s32[]{:S(2)}) async-start(), calls=%async_computation.3 | async-start | bytes 2621440 | tf_op jit(solution)/shard_map/all_gather | solution.py:1298
  12.5 33.0 %all-to-all-start = ((bf16[4,128,512]{2,1,0:T(8,128)(2,1)}), bf16[4,128,512]{2,1,0:T(8,128)(2,1)S(1)}, u32[]{:S(2)}, u32[]{:S(2)}) async-start(bf16[4,128,512]{2,1,0:T(8,128)(2,1)} %take_columns.2), calls=%async_computation | async-start | bytes 1048576 | tf_op jit(solution)/shard_map/all_to_all | solution.py:1289
  17.8 141.7 %all-gather.13.cloned.1.call-start = ((), (), s32[]{:S(2)}) async-start(), calls=%async_computation.6 | async-start | bytes 2621440 | tf_op jit(solution)/shard_map/all_gather | solution.py:1343
  17.9 26.9 %collective-permute-start.1 = (bf16[1088]{0:T(1024)(128)(2,1)S(1)}, bf16[1088]{0:T(1024)(128)(2,1)S(1)}, u32[]{:S(2)}, u32[]{:S(2)}) collective-permute-start(bf16[1088]{0:T(1024)(128)(2,1)S(1)} %concatenate.35), channel_id=1, source_target_pairs={{0,2},{2,4},{4,6},{6,0},{1,3},{3,5},{5,7},{7,1},{8,10},{10,12},{12... | collective-permute-start | bytes 6536 | tf_op jit(solution)/shard_map/ppermute | solution.py:393
  19.4 25.5 %collective-permute-start.2 = (bf16[1088]{0:T(1024)(128)(2,1)S(1)}, bf16[1088]{0:T(1024)(128)(2,1)S(1)}, u32[]{:S(2)}, u32[]{:S(2)}) collective-permute-start(bf16[1088]{0:T(1024)(128)(2,1)S(1)} %concatenate.35), channel_id=1, source_target_pairs={{0,4},{2,6},{4,0},{6,2},{1,5},{3,7},{5,1},{7,3},{8,12},{10,14},{12... | collective-permute-start | bytes 6536 | tf_op jit(solution)/shard_map/ppermute | solution.py:393
  20.3 25.1 %collective-permute-start.3 = (bf16[1088]{0:T(1024)(128)(2,1)S(1)}, bf16[1088]{0:T(1024)(128)(2,1)S(1)}, u32[]{:S(2)}, u32[]{:S(2)}) collective-permute-start(bf16[1088]{0:T(1024)(128)(2,1)S(1)} %concatenate.35), channel_id=1, source_target_pairs={{0,6},{2,0},{4,2},{6,4},{1,7},{3,1},{5,3},{7,5},{8,14},{10,8},{12,... | collective-permute-start | bytes 6536 | tf_op jit(solution)/shard_map/ppermute | solution.py:393
  22.3 4.3 collective-permute-start
  45.4 13.4 %collective-permute-start.4 = (bf16[4,128,512]{2,1,0:T(8,128)(2,1)S(1)}, bf16[4,128,512]{2,1,0:T(8,128)(2,1)S(1)}, u32[]{:S(2)}, u32[]{:S(2)}) collective-permute-start(bf16[4,128,512]{2,1,0:T(8,128)(2,1)S(1)} %all-to-all-done.refs_4_.refs_0_), channel_id=1, source_target_pairs={{0,1},{1,16},{16,17},{17,0},{2,3},{3,18},{18,19},{19,2},{4,5},{5,2... | collective-permute-start | bytes 1572872 | tf_op jit(solution)/shard_map/ppermute | solution.py:393
  45.9 18.9 %collective-permute-start.5 = (bf16[4,128,512]{2,1,0:T(8,128)(2,1)S(1)}, bf16[4,128,512]{2,1,0:T(8,128)(2,1)}, u32[]{:S(2)}, u32[]{:S(2)}) collective-permute-start(bf16[4,128,512]{2,1,0:T(8,128)(2,1)S(1)} %all-to-all-done.refs_4_.refs_0_), channel_id=1, source_target_pairs={{0,16},{1,17},{16,0},{17,1},{2,18},{3,19},{18,2},{19,3},{4,20},{5,... | collective-permute-start | bytes 1572872 | tf_op jit(solution)/shard_map/ppermute | solution.py:393
  47.4 17.3 %collective-permute-start.6 = (bf16[4,128,512]{2,1,0:T(8,128)(2,1)S(1)}, bf16[4,128,512]{2,1,0:T(8,128)(2,1)}, u32[]{:S(2)}, u32[]{:S(2)}) collective-permute-start(bf16[4,128,512]{2,1,0:T(8,128)(2,1)S(1)} %all-to-all-done.refs_4_.refs_0_), channel_id=1, source_target_pairs={{0,17},{1,0},{16,1},{17,16},{2,19},{3,2},{18,3},{19,18},{4,21},{5,... | collective-permute-start | bytes 1572872 | tf_op jit(solution)/shard_map/ppermute | solution.py:393
  68.9 15.9 %collective-permute-start.7 = (bf16[512,2048]{1,0:T(8,128)(2,1)}, bf16[512,2048]{1,0:T(8,128)(2,1)}, u32[]{:S(2)}, u32[]{:S(2)}) collective-permute-start(bf16[512,2048]{1,0:T(8,128)(2,1)} %norm_group.1.refs_0_.refs_1_.refs_2_.refs_3_), channel_id=1, source_target_pairs={{0,8},{8,0},{1,9},{9,1},{2,10},{10,2},{3,11},{11,3},{4,12},{12,4},... | collective-permute-start | bytes 6291464 | tf_op jit(solution)/shard_map/ppermute | solution.py:414
  71.8 189.9 %all-gather.11.cloned.1.call-start = ((), (), s32[]{:S(2)}) async-start(), calls=%async_computation.4 | async-start | bytes 7864320 | tf_op jit(solution)/shard_map/all_gather | solution.py:1368
  93.5 14.6 %collective-permute-start.8 = (bf16[1024,256]{1,0:T(8,128)(2,1)}, bf16[1024,256]{1,0:T(8,128)(2,1)}, u32[]{:S(2)}, u32[]{:S(2)}) collective-permute-start(bf16[1024,256]{1,0:T(8,128)(2,1)} %pad_maximum_fusion.2), channel_id=1, source_target_pairs={{0,1},{1,0},{2,3},{3,2},{4,5},{5,4},{6,7},{7,6},{8,9},{9,8},{10,11... | collective-permute-start | bytes 1572872 | tf_op jit(solution)/shard_map/ppermute | solution.py:393
  118.2 6.0 collective-permute-start.9
  119.7 12.1 %collective-permute-start.13 = (bf16[128,1536]{1,0:T(8,128)(2,1)S(1)}, bf16[128,1536]{1,0:T(8,128)(2,1)S(1)}, u32[]{:S(2)}, u32[]{:S(2)}) collective-permute-start(bf16[128,1536]{1,0:T(8,128)(2,1)S(1)} %get-tuple-element.292), channel_id=1, source_target_pairs={{0,2},{2,4},{4,6},{6,0},{1,3},{3,5},{5,7},{7,1},{8,10},{10,12},{12... | collective-permute-start | bytes 1179656 | tf_op jit(solution)/shard_map/ppermute | solution.py:592
  119.8 34.6 %collective-permute-start.14 = (bf16[128,1536]{1,0:T(8,128)(2,1)S(1)}, bf16[128,1536]{1,0:T(8,128)(2,1)S(1)}, u32[]{:S(2)}, u32[]{:S(2)}) collective-permute-start(bf16[128,1536]{1,0:T(8,128)(2,1)S(1)} %get-tuple-element.291), channel_id=1, source_target_pairs={{0,4},{2,6},{4,0},{6,2},{1,5},{3,7},{5,1},{7,3},{8,12},{10,14},{12... | collective-permute-start | bytes 1179656 | tf_op jit(solution)/shard_map/ppermute | solution.py:592
  124.2 34.0 %collective-permute-start.15 = (bf16[128,1536]{1,0:T(8,128)(2,1)S(1)}, bf16[128,1536]{1,0:T(8,128)(2,1)S(1)}, u32[]{:S(2)}, u32[]{:S(2)}) collective-permute-start(bf16[128,1536]{1,0:T(8,128)(2,1)S(1)} %get-tuple-element.290), channel_id=1, source_target_pairs={{0,6},{2,0},{4,2},{6,4},{1,7},{3,1},{5,3},{7,5},{8,14},{10,8},{12,... | collective-permute-start | bytes 1179656 | tf_op jit(solution)/shard_map/ppermute | solution.py:592
  159.5 50.1 %copy-start.55 = (f32[1,128,2048]{2,1,0:T(8,128)S(1)}, f32[1,128,2048]{2,1,0:T(8,128)}, u32[]{:S(2)}) copy-start(f32[1,128,2048]{2,1,0:T(8,128)} %copy-done.54) | copy-start | bytes 3145732
  159.5 258.8 %reduce-scatter.2.cloned.1.call-start = ((), (), s32[]{:S(2)}) async-start(), calls=%async_computation.5 | async-start | bytes 11796480 | tf_op jit(solution)/shard_map/reduce_scatter | solution.py:1395
  163.5 63.4 %collective-permute-start.19 = (bf16[512,2048]{1,0:T(8,128)(2,1)}, bf16[512,2048]{1,0:T(8,128)(2,1)}, u32[]{:S(2)}, u32[]{:S(2)}) collective-permute-start(bf16[512,2048]{1,0:T(8,128)(2,1)} %ring_order.1.refs_0_.refs_2_), channel_id=1, source_target_pairs={{0,8},{8,0},{1,9},{9,1},{2,10},{10,2},{3,11},{11,3},{4,12},{12,4},... | collective-permute-start | bytes 6291464 | tf_op jit(solution)/shard_map/ppermute | solution.py:414
  163.5 14.9 %collective-permute-start.10 = (bf16[128,2048]{1,0:T(8,128)(2,1)}, bf16[128,2048]{1,0:T(8,128)(2,1)S(1)}, u32[]{:S(2)}, u32[]{:S(2)}) collective-permute-start(bf16[128,2048]{1,0:T(8,128)(2,1)} %bitcast.173), channel_id=1, source_target_pairs={{0,2},{2,4},{4,6},{6,0},{1,3},{3,5},{5,7},{7,1},{8,10},{10,12},{12... | collective-permute-start | bytes 1572872 | tf_op jit(solution)/shard_map/ppermute | solution.py:400
  163.5 46.0 %collective-permute-start.11 = (bf16[128,2048]{1,0:T(8,128)(2,1)S(1)}, bf16[128,2048]{1,0:T(8,128)(2,1)S(1)}, u32[]{:S(2)}, u32[]{:S(2)}) collective-permute-start(bf16[128,2048]{1,0:T(8,128)(2,1)S(1)} %bitcast.172), channel_id=1, source_target_pairs={{0,4},{2,6},{4,0},{6,2},{1,5},{3,7},{5,1},{7,3},{8,12},{10,14},{12... | collective-permute-start | bytes 1572872 | tf_op jit(solution)/shard_map/ppermute | solution.py:400
  163.6 46.0 %collective-permute-start.12 = (bf16[128,2048]{1,0:T(8,128)(2,1)S(1)}, bf16[128,2048]{1,0:T(8,128)(2,1)S(1)}, u32[]{:S(2)}, u32[]{:S(2)}) collective-permute-start(bf16[128,2048]{1,0:T(8,128)(2,1)S(1)} %bitcast.171), channel_id=1, source_target_pairs={{0,6},{2,0},{4,2},{6,4},{1,7},{3,1},{5,3},{7,5},{8,14},{10,8},{12,... | collective-permute-start | bytes 1572872 | tf_op jit(solution)/shard_map/ppermute | solution.py:400
  212.3 20.5 %collective-permute-start.16 = (bf16[128,2048]{1,0:T(8,128)(2,1)}, bf16[128,2048]{1,0:T(8,128)(2,1)}, u32[]{:S(2)}, u32[]{:S(2)}) collective-permute-start(bf16[128,2048]{1,0:T(8,128)(2,1)} %multiply_convert_fusion), channel_id=1, source_target_pairs={{0,2},{2,4},{4,6},{6,0},{1,3},{3,5},{5,7},{7,1},{8,10},{10,12},{12... | collective-permute-start | bytes 1572872 | tf_op jit(solution)/shard_map/ppermute | solution.py:393
  212.3 45.8 %collective-permute-start.17 = (bf16[128,2048]{1,0:T(8,128)(2,1)}, bf16[128,2048]{1,0:T(8,128)(2,1)}, u32[]{:S(2)}, u32[]{:S(2)}) collective-permute-start(bf16[128,2048]{1,0:T(8,128)(2,1)} %multiply_convert_fusion), channel_id=1, source_target_pairs={{0,4},{2,6},{4,0},{6,2},{1,5},{3,7},{5,1},{7,3},{8,12},{10,14},{12... | collective-permute-start | bytes 1572872 | tf_op jit(solution)/shard_map/ppermute | solution.py:393
  215.6 46.1 %collective-permute-start.18 = (bf16[128,2048]{1,0:T(8,128)(2,1)}, bf16[128,2048]{1,0:T(8,128)(2,1)}, u32[]{:S(2)}, u32[]{:S(2)}) collective-permute-start(bf16[128,2048]{1,0:T(8,128)(2,1)} %multiply_convert_fusion), channel_id=1, source_target_pairs={{0,6},{2,0},{4,2},{6,4},{1,7},{3,1},{5,3},{7,5},{8,14},{10,8},{12,... | collective-permute-start | bytes 1572872 | tf_op jit(solution)/shard_map/ppermute | solution.py:393
  266.2 8.8 %collective-permute-start.20 = (bf16[512,2048]{1,0:T(8,128)(2,1)S(1)}, bf16[512,2048]{1,0:T(8,128)(2,1)S(1)}, u32[]{:S(2)}, u32[]{:S(2)}) collective-permute-start(bf16[512,2048]{1,0:T(8,128)(2,1)S(1)} %constant_dynamic-update-slice_fusion.ffn_ref.refs_0_), channel_id=1, source_target_pairs={{0,8},{8,0},{1,9},{9,1},{2,10},{10,2},{3,11},{11,3},{4,12},{12,4},... | collective-permute-start | bytes 6291464 | tf_op jit(solution)/shard_map/ppermute | solution.py:414
  300.6 170.0 %all-gather.15.cloned.1.call-start = ((), (), s32[]{:S(2)}) async-start(), calls=%async_computation.7 | async-start | bytes 7077888 | tf_op jit(solution)/shard_map/all_gather | solution.py:1292
  309.3 57.8 %copy-start.82 = (f32[128,2048]{1,0:T(8,128)S(1)}, f32[128,2048]{1,0:T(8,128)}, u32[]{:S(2)}) copy-start(f32[128,2048]{1,0:T(8,128)} %copy-done.81) | copy-start | bytes 3145732
  309.3 4.2 collective-permute-start.21
  321.6 45.9 %copy-start.86 = (bf16[2,1,64,2048]{3,2,1,0:T(8,128)(2,1)S(1)}, bf16[2,1,64,2048]{3,2,1,0:T(8,128)(2,1)}, u32[]{:S(2)}) copy-start(bf16[2,1,64,2048]{3,2,1,0:T(8,128)(2,1)} %param.18) | copy-start | bytes 1572868
  321.6 37.3 %collective-permute-start.24 = (bf16[128,2048]{1,0:T(8,128)(2,1)S(1)}, bf16[128,2048]{1,0:T(8,128)(2,1)S(1)}, u32[]{:S(2)}, u32[]{:S(2)}) collective-permute-start(bf16[128,2048]{1,0:T(8,128)(2,1)S(1)} %bitcast.176), channel_id=1, source_target_pairs={{0,6},{2,0},{4,2},{6,4},{1,7},{3,1},{5,3},{7,5},{8,14},{10,8},{12,... | collective-permute-start | bytes 1572872 | tf_op jit(solution)/shard_map/ppermute | solution.py:400
  321.7 37.2 %collective-permute-start.23 = (bf16[128,2048]{1,0:T(8,128)(2,1)S(1)}, bf16[128,2048]{1,0:T(8,128)(2,1)S(1)}, u32[]{:S(2)}, u32[]{:S(2)}) collective-permute-start(bf16[128,2048]{1,0:T(8,128)(2,1)S(1)} %bitcast.175), channel_id=1, source_target_pairs={{0,4},{2,6},{4,0},{6,2},{1,5},{3,7},{5,1},{7,3},{8,12},{10,14},{12... | collective-permute-start | bytes 1572872 | tf_op jit(solution)/shard_map/ppermute | solution.py:400
  322.1 45.0 %collective-permute-start.22 = (bf16[128,2048]{1,0:T(8,128)(2,1)S(1)}, bf16[128,2048]{1,0:T(8,128)(2,1)S(1)}, u32[]{:S(2)}, u32[]{:S(2)}) collective-permute-start(bf16[128,2048]{1,0:T(8,128)(2,1)S(1)} %bitcast.174), channel_id=1, source_target_pairs={{0,2},{2,4},{4,6},{6,0},{1,3},{3,5},{5,7},{7,1},{8,10},{10,12},{12... | collective-permute-start | bytes 1572872 | tf_op jit(solution)/shard_map/ppermute | solution.py:400
  369.0 15.3 %collective-permute-start.27 = (bf16[128,2048]{1,0:T(8,128)(2,1)S(1)}, bf16[128,2048]{1,0:T(8,128)(2,1)S(1)}, u32[]{:S(2)}, u32[]{:S(2)}) collective-permute-start(bf16[128,2048]{1,0:T(8,128)(2,1)S(1)} %get-tuple-element.280), channel_id=1, source_target_pairs={{0,6},{2,0},{4,2},{6,4},{1,7},{3,1},{5,3},{7,5},{8,14},{10,8},{12,... | collective-permute-start | bytes 1572872 | tf_op jit(solution)/shard_map/ppermute | solution.py:393
  372.7 32.9 %collective-permute-start.26 = (bf16[128,2048]{1,0:T(8,128)(2,1)S(1)}, bf16[128,2048]{1,0:T(8,128)(2,1)S(1)}, u32[]{:S(2)}, u32[]{:S(2)}) collective-permute-start(bf16[128,2048]{1,0:T(8,128)(2,1)S(1)} %get-tuple-element.280), channel_id=1, source_target_pairs={{0,4},{2,6},{4,0},{6,2},{1,5},{3,7},{5,1},{7,3},{8,12},{10,14},{12... | collective-permute-start | bytes 1572872 | tf_op jit(solution)/shard_map/ppermute | solution.py:393
  373.0 43.8 %collective-permute-start.25 = (bf16[128,2048]{1,0:T(8,128)(2,1)S(1)}, bf16[128,2048]{1,0:T(8,128)(2,1)S(1)}, u32[]{:S(2)}, u32[]{:S(2)}) collective-permute-start(bf16[128,2048]{1,0:T(8,128)(2,1)S(1)} %get-tuple-element.280), channel_id=1, source_target_pairs={{0,2},{2,4},{4,6},{6,0},{1,3},{3,5},{5,7},{7,1},{8,10},{10,12},{12... | collective-permute-start | bytes 1572872 | tf_op jit(solution)/shard_map/ppermute | solution.py:393
  420.4 180.8 %all-gather.17.cloned.1.call-start = ((), (), s32[]{:S(2)}) async-start(), calls=%async_computation.8 | async-start | bytes 14155776 | tf_op jit(solution)/shard_map/all_gather | solution.py:1292
  420.5 17.0 %collective-permute-start.29 = (bf16[512,2048]{1,0:T(8,128)(2,1)}, bf16[512,2048]{1,0:T(8,128)(2,1)S(1)}, u32[]{:S(2)}, u32[]{:S(2)}) collective-permute-start(bf16[512,2048]{1,0:T(8,128)(2,1)} %pad_maximum_fusion.refs_0_.refs_8_.refs_9_.refs_10_.refs_11_), channel_id=1, source_target_pairs={{0,8},{8,0},{1,9},{9,1},{2,10},{10,2},{3,11},{11,3},{4,12},{12,4},... | collective-permute-start | bytes 6291464 | tf_op jit(solution)/shard_map/ppermute | solution.py:414
  423.3 36.2 %collective-permute-start.30 = (bf16[128,1536]{1,0:T(8,128)(2,1)}, bf16[128,1536]{1,0:T(8,128)(2,1)}, u32[]{:S(2)}, u32[]{:S(2)}) collective-permute-start(bf16[128,1536]{1,0:T(8,128)(2,1)} %get-tuple-element.288), channel_id=1, source_target_pairs={{0,2},{2,4},{4,6},{6,0},{1,3},{3,5},{5,7},{7,1},{8,10},{10,12},{12... | collective-permute-start | bytes 1179656 | tf_op jit(solution)/shard_map/ppermute | solution.py:592
  425.8 34.6 %collective-permute-start.31 = (bf16[128,1536]{1,0:T(8,128)(2,1)}, bf16[128,1536]{1,0:T(8,128)(2,1)}, u32[]{:S(2)}, u32[]{:S(2)}) collective-permute-start(bf16[128,1536]{1,0:T(8,128)(2,1)} %get-tuple-element.287), channel_id=1, source_target_pairs={{0,4},{2,6},{4,0},{6,2},{1,5},{3,7},{5,1},{7,3},{8,12},{10,14},{12... | collective-permute-start | bytes 1179656 | tf_op jit(solution)/shard_map/ppermute | solution.py:592
  427.8 34.3 %collective-permute-start.32 = (bf16[128,1536]{1,0:T(8,128)(2,1)}, bf16[128,1536]{1,0:T(8,128)(2,1)}, u32[]{:S(2)}, u32[]{:S(2)}) collective-permute-start(bf16[128,1536]{1,0:T(8,128)(2,1)} %get-tuple-element.286), channel_id=1, source_target_pairs={{0,6},{2,0},{4,2},{6,4},{1,7},{3,1},{5,3},{7,5},{8,14},{10,8},{12,... | collective-permute-start | bytes 1179656 | tf_op jit(solution)/shard_map/ppermute | solution.py:592
  436.3 8.9 %collective-permute-start.28 = (bf16[512,256]{1,0:T(8,128)(2,1)S(1)}, bf16[512,256]{1,0:T(8,128)(2,1)S(1)}, u32[]{:S(2)}, u32[]{:S(2)}) collective-permute-start(bf16[512,256]{1,0:T(8,128)(2,1)S(1)} %bitcast.177), channel_id=1, source_target_pairs={{0,1},{1,0},{2,3},{3,2},{4,5},{5,4},{6,7},{7,6},{8,9},{9,8},{10,11... | collective-permute-start | bytes 786440 | tf_op jit(solution)/shard_map/ppermute | solution.py:1421
  444.2 11.8 %collective-permute-start.33 = (bf16[512,256]{1,0:T(8,128)(2,1)S(1)}, bf16[512,256]{1,0:T(8,128)(2,1)S(1)}, u32[]{:S(2)}, u32[]{:S(2)}) collective-permute-start(bf16[512,256]{1,0:T(8,128)(2,1)S(1)} %bitcast.178), channel_id=1, source_target_pairs={{0,1},{1,0},{2,3},{3,2},{4,5},{5,4},{6,7},{7,6},{8,9},{9,8},{10,11... | collective-permute-start | bytes 786440 | tf_op jit(solution)/shard_map/ppermute | solution.py:1421
  489.8 58.9 %collective-permute-start.37 = (bf16[2,512,2048]{2,1,0:T(8,128)(2,1)}, bf16[2,512,2048]{2,1,0:T(8,128)(2,1)}, u32[]{:S(2)}, u32[]{:S(2)}) collective-permute-start(bf16[2,512,2048]{2,1,0:T(8,128)(2,1)} %product.18), channel_id=1, source_target_pairs={{0,8},{8,0},{1,9},{9,1},{2,10},{10,2},{3,11},{11,3},{4,12},{12,4},... | collective-permute-start | bytes 12582920 | tf_op jit(solution)/shard_map/ppermute | solution.py:414
  490.0 29.5 %collective-permute-start.34 = (bf16[4,144,768]{2,1,0:T(8,128)(2,1)S(1)}, bf16[4,144,768]{2,1,0:T(8,128)(2,1)S(1)}, u32[]{:S(2)}, u32[]{:S(2)}) collective-permute-start(bf16[4,144,768]{2,1,0:T(8,128)(2,1)S(1)} %get-tuple-element.207), channel_id=1, source_target_pairs={{0,1},{1,16},{16,17},{17,0},{2,3},{3,18},{18,19},{19,2},{4,5},{5,2... | collective-permute-start | bytes 2654216 | tf_op jit(solution)/shard_map/ppermute | solution.py:400
  491.6 45.9 %collective-permute-start.35 = (bf16[4,144,768]{2,1,0:T(8,128)(2,1)S(1)}, bf16[4,144,768]{2,1,0:T(8,128)(2,1)S(1)}, u32[]{:S(2)}, u32[]{:S(2)}) collective-permute-start(bf16[4,144,768]{2,1,0:T(8,128)(2,1)S(1)} %get-tuple-element.208), channel_id=1, source_target_pairs={{0,16},{1,17},{16,0},{17,1},{2,18},{3,19},{18,2},{19,3},{4,20},{5,... | collective-permute-start | bytes 2654216 | tf_op jit(solution)/shard_map/ppermute | solution.py:400
  492.4 49.1 %collective-permute-start.36 = (bf16[4,144,768]{2,1,0:T(8,128)(2,1)S(1)}, bf16[4,144,768]{2,1,0:T(8,128)(2,1)S(1)}, u32[]{:S(2)}, u32[]{:S(2)}) collective-permute-start(bf16[4,144,768]{2,1,0:T(8,128)(2,1)S(1)} %get-tuple-element.209), channel_id=1, source_target_pairs={{0,17},{1,0},{16,1},{17,16},{2,19},{3,2},{18,3},{19,18},{4,21},{5,... | collective-permute-start | bytes 2654216 | tf_op jit(solution)/shard_map/ppermute | solution.py:400
  542.8 17.3 %all-to-all-start.1 = ((bf16[4,144,512]{2,1,0:T(8,128)(2,1)}), bf16[4,144,512]{2,1,0:T(8,128)(2,1)}, u32[]{:S(2)}, u32[]{:S(2)}) async-start(bf16[4,144,512]{2,1,0:T(8,128)(2,1)} %slice.98), calls=%async_computation.2 | async-start | bytes 1179648 | tf_op jit(solution)/shard_map/all_to_all | solution.py:1289
  561.5 62.5 %copy-start.18 = (bf16[4,144,768]{2,1,0:T(8,128)(2,1)}, bf16[4,144,768]{2,1,0:T(8,128)(2,1)S(1)}, u32[]{:S(2)}) copy-start(bf16[4,144,768]{2,1,0:T(8,128)(2,1)S(1)} %pad_maximum_fusion.1.refs_0_) | copy-start | bytes 2654212
  561.5 29.5 %collective-permute-start.41 = (bf16[4,144,768]{2,1,0:T(8,128)(2,1)S(1)}, bf16[4,144,768]{2,1,0:T(8,128)(2,1)S(1)}, u32[]{:S(2)}, u32[]{:S(2)}) collective-permute-start(bf16[4,144,768]{2,1,0:T(8,128)(2,1)S(1)} %pad_maximum_fusion.1.refs_0_), channel_id=1, source_target_pairs={{0,1},{1,16},{16,17},{17,0},{2,3},{3,18},{18,19},{19,2},{4,5},{5,2... | collective-permute-start | bytes 2654216 | tf_op jit(solution)/shard_map/ppermute | solution.py:393
  564.2 69.9 %collective-permute-start.38 = (bf16[2,128,2048]{2,1,0:T(8,128)(2,1)S(1)}, bf16[2,128,2048]{2,1,0:T(8,128)(2,1)}, u32[]{:S(2)}, u32[]{:S(2)}) collective-permute-start(bf16[2,128,2048]{2,1,0:T(8,128)(2,1)S(1)} %get-tuple-element.217), channel_id=1, source_target_pairs={{0,2},{2,4},{4,6},{6,0},{1,3},{3,5},{5,7},{7,1},{8,10},{10,12},{12... | collective-permute-start | bytes 3145736 | tf_op jit(solution)/shard_map/ppermute | solution.py:400
  565.6 88.9 %collective-permute-start.39 = (bf16[2,128,2048]{2,1,0:T(8,128)(2,1)}, bf16[2,128,2048]{2,1,0:T(8,128)(2,1)}, u32[]{:S(2)}, u32[]{:S(2)}) collective-permute-start(bf16[2,128,2048]{2,1,0:T(8,128)(2,1)} %copy-done.74), channel_id=1, source_target_pairs={{0,4},{2,6},{4,0},{6,2},{1,5},{3,7},{5,1},{7,3},{8,12},{10,14},{12... | collective-permute-start | bytes 3145736 | tf_op jit(solution)/shard_map/ppermute | solution.py:400
  569.9 88.7 %collective-permute-start.40 = (bf16[2,128,2048]{2,1,0:T(8,128)(2,1)}, bf16[2,128,2048]{2,1,0:T(8,128)(2,1)}, u32[]{:S(2)}, u32[]{:S(2)}) collective-permute-start(bf16[2,128,2048]{2,1,0:T(8,128)(2,1)} %copy-done.73), channel_id=1, source_target_pairs={{0,6},{2,0},{4,2},{6,4},{1,7},{3,1},{5,3},{7,5},{8,14},{10,8},{12,... | collective-permute-start | bytes 3145736 | tf_op jit(solution)/shard_map/ppermute | solution.py:400
  569.9 54.1 %collective-permute-start.42 = (bf16[4,144,768]{2,1,0:T(8,128)(2,1)S(1)}, bf16[4,144,768]{2,1,0:T(8,128)(2,1)}, u32[]{:S(2)}, u32[]{:S(2)}) collective-permute-start(bf16[4,144,768]{2,1,0:T(8,128)(2,1)S(1)} %pad_maximum_fusion.1.refs_0_), channel_id=1, source_target_pairs={{0,16},{1,17},{16,0},{17,1},{2,18},{3,19},{18,2},{19,3},{4,20},{5,... | collective-permute-start | bytes 2654216 | tf_op jit(solution)/shard_map/ppermute | solution.py:393
  591.0 33.1 %collective-permute-start.43 = (bf16[4,144,768]{2,1,0:T(8,128)(2,1)S(1)}, bf16[4,144,768]{2,1,0:T(8,128)(2,1)}, u32[]{:S(2)}, u32[]{:S(2)}) collective-permute-start(bf16[4,144,768]{2,1,0:T(8,128)(2,1)S(1)} %pad_maximum_fusion.1.refs_0_), channel_id=1, source_target_pairs={{0,17},{1,0},{16,1},{17,16},{2,19},{3,2},{18,3},{19,18},{4,21},{5,... | collective-permute-start | bytes 2654216 | tf_op jit(solution)/shard_map/ppermute | solution.py:393
  624.1 39.0 %copy-start.85 = (bf16[2,1,64,2048]{3,2,1,0:T(8,128)(2,1)S(1)}, bf16[2,1,64,2048]{3,2,1,0:T(8,128)(2,1)}, u32[]{:S(2)}) copy-start(bf16[2,1,64,2048]{3,2,1,0:T(8,128)(2,1)} %param.16) | copy-start | bytes 1572868
  624.1 39.3 %copy-start.94 = (f32[512,128]{1,0:T(8,128)S(1)}, f32[512,128]{1,0:T(8,128)}, u32[]{:S(2)}) copy-start(f32[512,128]{1,0:T(8,128)} %get-tuple-element.240) | copy-start | bytes 786436
  624.1 39.4 %copy-start.98 = (bf16[512]{0:T(512)(128)(2,1)S(1)}, bf16[512]{0:T(512)(128)(2,1)}, u32[]{:S(2)}) copy-start(bf16[512]{0:T(512)(128)(2,1)} %param.29) | copy-start | bytes 3076
  624.1 44.0 %collective-permute-start.44 = (bf16[4,144,768]{2,1,0:T(8,128)(2,1)S(1)}, bf16[4,144,768]{2,1,0:T(8,128)(2,1)}, u32[]{:S(2)}, u32[]{:S(2)}) collective-permute-start(bf16[4,144,768]{2,1,0:T(8,128)(2,1)S(1)} %pad_maximum_fusion.1.refs_0_), channel_id=1, source_target_pairs={{0,8},{8,0},{1,9},{9,1},{2,10},{10,2},{3,11},{11,3},{4,12},{12,4},... | collective-permute-start | bytes 2654216 | tf_op jit(solution)/shard_map/ppermute | solution.py:414
  624.2 43.9 %collective-permute-start.45 = (bf16[4,144,768]{2,1,0:T(8,128)(2,1)S(1)}, bf16[4,144,768]{2,1,0:T(8,128)(2,1)}, u32[]{:S(2)}, u32[]{:S(2)}) collective-permute-start(bf16[4,144,768]{2,1,0:T(8,128)(2,1)S(1)} %collective-permute-done.41.refs_1_), channel_id=1, source_target_pairs={{0,8},{8,0},{1,9},{9,1},{2,10},{10,2},{3,11},{11,3},{4,12},{12,4},... | collective-permute-start | bytes 2654216 | tf_op jit(solution)/shard_map/ppermute | solution.py:414
  634.0 34.0 %collective-permute-start.46 = (bf16[4,144,768]{2,1,0:T(8,128)(2,1)}, bf16[4,144,768]{2,1,0:T(8,128)(2,1)}, u32[]{:S(2)}, u32[]{:S(2)}) collective-permute-start(bf16[4,144,768]{2,1,0:T(8,128)(2,1)} %collective-permute-done.42.refs_2_), channel_id=1, source_target_pairs={{0,8},{8,0},{1,9},{9,1},{2,10},{10,2},{3,11},{11,3},{4,12},{12,4},... | collective-permute-start | bytes 2654216 | tf_op jit(solution)/shard_map/ppermute | solution.py:414
  654.5 13.5 %collective-permute-start.47 = (bf16[4,144,768]{2,1,0:T(8,128)(2,1)}, bf16[4,144,768]{2,1,0:T(8,128)(2,1)}, u32[]{:S(2)}, u32[]{:S(2)}) collective-permute-start(bf16[4,144,768]{2,1,0:T(8,128)(2,1)} %collective-permute-done.43.refs_3_), channel_id=1, source_target_pairs={{0,8},{8,0},{1,9},{9,1},{2,10},{10,2},{3,11},{11,3},{4,12},{12,4},... | collective-permute-start | bytes 2654216 | tf_op jit(solution)/shard_map/ppermute | solution.py:414
  (97 other events, 607.8 us)
Sparse Core Ops, SparseCore 0:
  9.6 53.5 all-gather.8
  71.9 45.0 all-gather.12
  159.6 68.2 all-gather.10
  300.7 93.1 reduce-scatter.1
  420.5 50.0 all-gather.14
  472.9 109.3 all-gather.16

commit v3 on v2

--- a/solution.py
+++ b/solution.py
@@ -16,6 +16,7 @@
 
 EPSILON = 1e-06
 THETA = 1000000.0
+FF_BLOCK = 256
 
 
 def apply_rotation(values):
@@ -444,15 +445,16 @@
     columns = gate_ref.shape[1] // 2
     total = None
     for core in range(2):
-        full = full_ref[0, core, 0, 0].astype(jnp.float32)
-        span = slice(core * columns, (core + 1) * columns)
-        d_gate = full[:, :columns]
-        d_up = full[:, columns:]
-        d_gate_ref[:, span] = d_gate
-        d_up_ref[:, span] = d_up
-        both = d_gate * gate_ref[:, span].astype(jnp.float32)
-        both = lane_sums(both + d_up * up_ref[:, span].astype(jnp.float32))
-        total = both if total is None else total + both
+        for at in range(0, columns, FF_BLOCK):
+            full = full_ref[0, core, 0, 0, :, 2 * at : 2 * (at + FF_BLOCK)].astype(jnp.float32)
+            span = slice(core * columns + at, core * columns + at + FF_BLOCK)
+            d_gate = full[:, :FF_BLOCK]
+            d_up = full[:, FF_BLOCK:]
+            d_gate_ref[:, span] = d_gate
+            d_up_ref[:, span] = d_up
+            both = d_gate * gate_ref[:, span].astype(jnp.float32)
+            both = lane_sums(both + d_up * up_ref[:, span].astype(jnp.float32))
+            total = both if total is None else total + both
     add_sums(pl.program_id(1), sums_ref, total)
 
 
@@ -499,7 +501,7 @@
         ],
         out_specs=pl.BlockSpec((2 * columns, n_part * rows), lambda j: (0, j)),
         out_shape=jax.ShapeDtypeStruct((2 * columns, n_shard * n_part * rows), jnp.float32),
-        compiler_params=pltpu.CompilerParams(vmem_limit_bytes=48 << 20),
+        compiler_params=pltpu.CompilerParams(vmem_limit_bytes=60 << 20),
         name="lay_rows",
     )(full)
 
@@ -594,20 +596,21 @@
     ]
 
 
-def take_columns_kernel(at_ref, *refs):
+def take_columns_kernel(block, at_ref, *refs):
     out_ref = refs[-1]
-    start = 0
-    for ref in refs[:-1]:
-        columns = ref.shape[1]
-        out_ref[0, :, start : start + columns] = ref[...]
-        start += columns
-
-
-def take_columns(at, n_part, n_shard, weights):
+    at = 0
+    for first in range(0, refs[0].shape[1], block or refs[0].shape[1]):
+        for ref in refs[:-1]:
+            columns = block or ref.shape[1]
+            out_ref[0, :, at : at + columns] = ref[:, first : first + columns]
+            at += columns
+
+
+def take_columns(at, n_part, n_shard, weights, block=0):
     rows = weights[0].shape[0] // n_part
     widths = [weight.shape[1] // (2 * n_shard) for weight in weights]
     return pl.pallas_call(
-        take_columns_kernel,
+        partial(take_columns_kernel, block),
         grid_spec=pltpu.PrefetchScalarGridSpec(
             num_scalar_prefetch=1,
             grid=(n_shard,),
@@ -664,7 +667,7 @@
             out_specs=pl.BlockSpec((len(pieces),) + pieces[0].shape, lambda i, z: (0, 0, 0)),
         ),
         out_shape=jax.ShapeDtypeStruct((len(pieces),) + pieces[0].shape, pieces[0].dtype),
-        compiler_params=pltpu.CompilerParams(vmem_limit_bytes=48 << 20),
+        compiler_params=pltpu.CompilerParams(vmem_limit_bytes=8 << 20),
         name="place",
     )(rank.reshape(1), *pieces)
 
@@ -772,7 +775,7 @@
             jax.ShapeDtypeStruct((group, 2 * kv_cols), jnp.bfloat16),
             jax.ShapeDtypeStruct((group, q_cols + kv_cols), jnp.float32),
         ],
-        compiler_params=pltpu.CompilerParams(vmem_limit_bytes=48 << 20),
+        compiler_params=pltpu.CompilerParams(vmem_limit_bytes=20 << 20),
         name="project",
     )(
         at,
@@ -857,7 +860,7 @@
             out_specs=spec(columns),
         ),
         out_shape=jax.ShapeDtypeStruct(view(queries).shape, jnp.bfloat16),
-        compiler_params=pltpu.CompilerParams(vmem_limit_bytes=48 << 20),
+        compiler_params=pltpu.CompilerParams(vmem_limit_bytes=16 << 20),
         name="attend",
     )(starts, *[view(part) for part in kv_parts], view(queries), q_pos, k_pos)
     return mixed.reshape(queries.shape)
@@ -973,7 +976,7 @@
             )
             for i in range(n_ctx)
         ],
-        compiler_params=pltpu.CompilerParams(vmem_limit_bytes=48 << 20),
+        compiler_params=pltpu.CompilerParams(vmem_limit_bytes=24 << 20),
         name="attend_back",
     )(
         starts,
@@ -1076,7 +1079,7 @@
             out_specs=[out] * n_part,
         ),
         out_shape=[jax.ShapeDtypeStruct((n_shard, out_rows, columns), jnp.bfloat16)] * n_part,
-        compiler_params=pltpu.CompilerParams(vmem_limit_bytes=48 << 20),
+        compiler_params=pltpu.CompilerParams(vmem_limit_bytes=24 << 20),
         name="head_gradients",
     )(
         at,
@@ -1148,18 +1151,18 @@
         in_specs=in_specs,
         out_specs=[pl.BlockSpec((n, rows // split, block), lambda j: (0, 0, j))] * split,
         out_shape=[jax.ShapeDtypeStruct((n, rows // split, columns), kind) for kind in dtypes],
-        compiler_params=pltpu.CompilerParams(vmem_limit_bytes=48 << 20),
+        compiler_params=pltpu.CompilerParams(vmem_limit_bytes=24 << 20),
         name="product",
     )(*args)
     return outs if got is not None else outs[0]
 
 
 def ffn_gradients_kernel(*refs):
-    ffn, cot, d_gate, d_up, inner = (refs[2 * i : 2 * i + 2] for i in range(5))
-    out_ref = refs[10]
+    ffn, cot, d_pre, inner = (refs[2 * i : 2 * i + 2] for i in range(4))
+    out_ref = refs[8]
     down = (((0,), (0,)), ((), ()))
     start = 0
-    for left, right in ((ffn, d_gate), (ffn, d_up), (cot, inner)):
+    for left, right in ((ffn, d_pre), (cot, inner)):
         stop = start + right[0].shape[1]
         out_ref[0, :, start:stop] = sum(
             lax.dot_general(
@@ -1170,22 +1173,23 @@
         start = stop
 
 
-def ffn_gradients(n_shard, ffn_in, cot, d_gate, d_up, inner):
+def ffn_gradients(n_shard, ffn_in, cot, d_pre, inner):
     rows, width = ffn_in[0].shape
     ff = inner[0].shape[1]
     block = 256
     per = width // (n_shard * block)
     left = pl.BlockSpec((rows, block), lambda j: (0, j))
-    right = pl.BlockSpec((rows, ff), lambda j: (0, 0))
+    wide = pl.BlockSpec((rows, 2 * ff), lambda j: (0, 0))
+    narrow = pl.BlockSpec((rows, ff), lambda j: (0, 0))
     return pl.pallas_call(
         ffn_gradients_kernel,
         grid=(width // block,),
-        in_specs=[left] * 4 + [right] * 6,
+        in_specs=[left] * 4 + [wide] * 2 + [narrow] * 2,
         out_specs=pl.BlockSpec((1, block, 3 * ff), lambda j: (j // per, j % per, 0)),
         out_shape=jax.ShapeDtypeStruct((n_shard, width // n_shard, 3 * ff), jnp.bfloat16),
-        compiler_params=pltpu.CompilerParams(vmem_limit_bytes=56 << 20),
+        compiler_params=pltpu.CompilerParams(vmem_limit_bytes=50 << 20),
         name="ffn_gradients",
-    )(*ffn_in, *cot, *d_gate, *d_up, *inner)
+    )(*ffn_in, *cot, *d_pre, *inner)
 
 
 def reorder_kernel(z_ref, in_ref, out_ref):
@@ -1211,40 +1215,39 @@
     )(rank.reshape(1), gathered)
 
 
-def inner_kernel(ffn_ref, gate_ref, up_ref, d_inner_ref, inner_ref, d_gate_ref, d_up_ref):
-    ffn = ffn_ref[...]
-    gate_pre = jnp.dot(ffn, gate_ref[...], preferred_element_type=jnp.float32)
-    up_pre = jnp.dot(ffn, up_ref[...], preferred_element_type=jnp.float32)
+def inner_kernel(ffn_ref, weight_ref, d_inner_ref, inner_ref, d_pre_ref):
+    pre = jnp.dot(ffn_ref[...], weight_ref[...], preferred_element_type=jnp.float32)
+    gate_pre, up_pre = pre[:, :FF_BLOCK], pre[:, FF_BLOCK:]
     d_inner = d_inner_ref[...]
     sigma = jax.nn.sigmoid(gate_pre)
     act_gate = gate_pre * sigma
     inner_ref[...] = (act_gate * up_pre).astype(jnp.bfloat16)
     d_gate = d_inner * up_pre * sigma * (1.0 + gate_pre * (1.0 - sigma))
-    d_gate_ref[...] = d_gate.astype(jnp.bfloat16)
-    d_up_ref[...] = (d_inner * act_gate).astype(jnp.bfloat16)
+    d_pre_ref[:, :FF_BLOCK] = d_gate.astype(jnp.bfloat16)
+    d_pre_ref[:, FF_BLOCK:] = (d_inner * act_gate).astype(jnp.bfloat16)
 
 
 def inner_parts(ffn_in, w_in, d_inner):
     rows, width = ffn_in.shape
     ff = w_in.shape[1] // 2
-    block = 256 if ff % 256 == 0 else 128
-    steps = ff // block
-    out = pl.BlockSpec((rows, block), lambda j: (0, j))
-    shape = jax.ShapeDtypeStruct((rows, ff), jnp.bfloat16)
+    narrow = pl.BlockSpec((rows, FF_BLOCK), lambda j: (0, j))
+    wide = pl.BlockSpec((rows, 2 * FF_BLOCK), lambda j: (0, j))
     return pl.pallas_call(
         inner_kernel,
-        grid=(steps,),
+        grid=(ff // FF_BLOCK,),
         in_specs=[
             pl.BlockSpec((rows, width), lambda j: (0, 0)),
-            pl.BlockSpec((width, block), lambda j: (0, j)),
-            pl.BlockSpec((width, block), lambda j: (0, steps + j)),
-            out,
+            pl.BlockSpec((width, 2 * FF_BLOCK), lambda j: (0, j)),
+            narrow,
         ],
-        out_specs=[out, out, out],
-        out_shape=[shape, shape, shape],
-        compiler_params=pltpu.CompilerParams(vmem_limit_bytes=48 << 20),
+        out_specs=[narrow, wide],
+        out_shape=[
+            jax.ShapeDtypeStruct((rows, ff), jnp.bfloat16),
+            jax.ShapeDtypeStruct((rows, 2 * ff), jnp.bfloat16),
+        ],
+        compiler_params=pltpu.CompilerParams(vmem_limit_bytes=20 << 20),
         name="inner_parts",
-    )(ffn_in, w_in, w_in, d_inner)
+    )(ffn_in, w_in, d_inner)
 
 
 def grouped_shards(
@@ -1297,7 +1300,7 @@
     at = jnp.stack([part, c, z])
     gathered = lax.all_gather(own_tokens, "shard", axis=0)
     pieces_qkv = take_columns(at, n_part, n_shard, (w_query, key_weight, value_weight))
-    pieces_in = take_columns(at, n_part, n_shard, (w_gate, w_up))
+    pieces_in = take_columns(at, n_part, n_shard, (w_gate, w_up), FF_BLOCK)
     gain_sizes = (attn_gain.shape[0], query_gain.shape[0], key_gain.shape[0], ffn_gain.shape[0])
     gains = after(jnp.concatenate([attn_gain, query_gain, key_gain, ffn_gain]), pieces_qkv)
     gains = from_ring(gains, "shard", n_shard)
@@ -1380,22 +1383,19 @@
     d_inner_theirs = product([([after(cot_theirs, d_inner_mine)], w_down_rows, 1)], f32)[0]
     ffn_mine = jnp.concatenate(after(ffn_ring, d_inner_theirs, w_in), axis=0)
     ffn_theirs = swap(ffn_mine, "core")
-    inner_mine, d_gate_mine, d_up_mine = inner_parts(ffn_mine, w_in, d_inner_mine)
-    inner_theirs, d_gate_theirs, d_up_theirs = inner_parts(
+    inner_mine, d_pre_mine = inner_parts(ffn_mine, w_in, d_inner_mine)
+    inner_theirs, d_pre_theirs = inner_parts(
         after(ffn_theirs, inner_mine), w_in, d_inner_theirs
     )
     grad_in = ffn_gradients(
         n_shard,
         (ffn_mine, ffn_theirs),
         (cot_mine, cot_theirs),
-        (d_gate_mine, d_gate_theirs),
-        (d_up_mine, d_up_theirs),
+        (d_pre_mine, d_pre_theirs),
         (inner_mine, inner_theirs),
     )
     part_in = lax.psum_scatter(grad_in, ("hi", "ctx"), scatter_dimension=1, tiled=True)
-    d_ffn_sent = core_sum(
-        [d_gate_mine, d_up_mine], [after(d_gate_theirs, grad_in), d_up_theirs], w_in, 1
-    )
+    d_ffn_sent = core_sum([d_pre_mine], [after(d_pre_theirs, grad_in)], w_in, 1)
     d_ffn_in = sum_terms(send_terms(d_ffn_sent, "shard", n_shard))
     d_middle = own_cot.astype(f32) + norm_back(unit_m, recip_m, gain_ffn, d_ffn_in)
 
@@ -1429,9 +1429,9 @@
         d_q_theirs, d_kv_theirs, pre_theirs, d_qkv_mine
     )
     sent_in = place(z, after(sent_in, d_qkv_theirs))
+    full_in = gather_plane(after(sent_in, full_down))
     qkv_cols = q_cols + 2 * kv_cols
     head_columns = qkv_cols + q_cols
-    full_in = gather_plane(after(sent_in, full_down))
     head_gains = jnp.concatenate([gain_q_mine + gain_q_theirs, gain_k_mine + gain_k_theirs])
     head_gains = jnp.zeros((16, head_columns), f32).at[0, : 2 * HEAD_SIZE].set(head_gains)
     sent = head_gradients(
@@ -1446,29 +1446,28 @@
     )
     part_heads = send_terms(sent, ("hi", "ctx"), n_part)
     got = product([([after(d_qkv_theirs, sent)], w_qkv, 1), ([inner_theirs], w_down_rows, 0)])
-    part_heads = sum_terms(after(part_heads, got)).astype(bf16)
     last = product(
-        [([after(d_qkv_mine, part_heads)], w_qkv, 1), ([inner_mine], w_down_rows, 0)],
+        [([after(d_qkv_mine, got)], w_qkv, 1), ([inner_mine], w_down_rows, 0)],
         got=swap(got, "core"),
         split=n_shard,
     )
+    part_heads = sum_terms(after(part_heads, last)).astype(bf16)
     ring_heads = exchange(part_heads[..., :qkv_cols])
-    ring_heads = after(ring_heads, last)
-    last = send_terms(last, "shard", n_shard)
+    last = send_terms(after(last, part_heads), "shard", n_shard)
     part_heads = jnp.concatenate([ring_heads, part_heads[..., qkv_cols:]], axis=-1)
     mine_heads = from_ring(part_heads, ("hi", "ctx"), n_part)
     grad_down = lay_rows(after(full_down, part_heads))
     grad_gate, grad_up, ffn_sums = lay_in(after(full_in, grad_down), w_gate, w_up)
     mine_heads = after(mine_heads, grad_gate)
     theirs_heads = [swap(values, "core") for values in mine_heads]
+    grad_query, grad_key, grad_value, grad_out, attn_sums, gain_sums = lay_heads(
+        at, mine_heads, theirs_heads, w_query, key_weight, value_weight
+    )
     last = sum_terms(after(last, mine_heads))
     recip_h = recip_rms(hidden_in)
     unit_h = hidden_in * recip_h
     input_grad = d_middle + norm_back(unit_h, recip_h, gain_attn, last[0])
     result = (middle + last[1]).astype(bf16)
-    grad_query, grad_key, grad_value, grad_out, attn_sums, gain_sums = lay_heads(
-        at, mine_heads, theirs_heads, w_query, key_weight, value_weight
-    )
     head_gains = gain_sums[0, : 2 * HEAD_SIZE].reshape(2, HEAD_SIZE)
     head_size = query_gain.shape[0]
     head_gains = lax.dynamic_slice_in_dim(head_gains, z * head_size, head_size, axis=1)

time: 689 us -> 681 us (0.988)
  Pallas kernels: 181 us -> 165 us
  waiting for transfers between devices: 354 us -> 364 us
    all_to_all x2, waiting for transfers between devices: 0.42 us -> 12.2 us  [exchange(): return lax.all_to_all(pieces, 'shard', 0, 0, tiled=True)]
    ppermute x12, waiting for transfers between devices: 169 us -> 157 us  [send_terms(): lax.ppermute(pieces[count - k].astype(jnp.bfloat16), axis, [(i, (i + k) %...]
    pallas_call x10, Pallas kernels: 43 us -> 31.9 us  [product(): pl.pallas_call(partial(product_kernel, [(len(terms), contract) for terms,...]
    unnamed x217 -> x213, local copies, waits for them, and re-layouts: 37 us -> 37.7 us
  transfers between devices with their start and end apart: 56 -> 56, of which waited for: 31 -> 32; matrix products, arithmetic and copies ran while one was open for 5% -> 5% of each run, Pallas kernels for 21% -> 19%
where the time goes in v3:
time: 681 us; the launch traced here: 678 us
  waiting for transfers between devices  364 us (53%)
  Pallas kernels  165 us (24%)
  starting transfers between devices  59.2 us (9%)
  local copies, waits for them, and re-layouts  51.6 us (8%)
  other arithmetic  22.9 us (3%)
  between operations  15.4 us (2%)
    ppermute x12, waiting for transfers between devices, send_terms(): lax.ppermute(pieces[count - k].astype(jnp.bfloat16), axis, [(i, (i + k) %...  157 us
    ppermute x16, waiting for transfers between devices, from_ring(): lax.ppermute(block, axis, [(i, (i + k) % count) for i in range(count)])  139 us
    unnamed x213, local copies, waits for them, and re-layouts  37.7 us
    ppermute x6, waiting for transfers between devices, exchange_ring(): lax.ppermute(piece_for(k), 'shard', [(i, (i + k) % count) for i in range(...  32.4 us
    pallas_call x10, Pallas kernels, product(): pl.pallas_call(partial(product_kernel, [(len(terms), contract) for terms,...  31.9 us
    pallas_call x1, Pallas kernels, lay_in(): pl.pallas_call(lay_in_kernel, grid=(n_hi * n_ctx, n_shard), in_specs=[pl....  22.9 us
    ppermute x16, starting transfers between devices, from_ring(): lax.ppermute(block, axis, [(i, (i + k) % count) for i in range(count)])  22.6 us
    pallas_call x1, Pallas kernels, ffn_gradients(): pl.pallas_call(ffn_gradients_kernel, grid=(width // block,), in_specs=[le...  15 us
  transfers between devices with their start and end apart: 56, of which 32 were waited for; matrix products, arithmetic and copies ran while one was open for 5% of the time, Pallas kernels for 19%

profile of v3, /device:TPU:14, one launch (start us, length us, event | category | flops | bytes accessed | tf_op | source)
XLA Modules:
  0.0 678.2 jit_solution(10143503668195973720)
XLA Ops:
  8.6 3.9 take_columns.2
  12.5 5.3 all-to-all-start
  22.3 4.3 take_columns.3
  26.6 18.2 %collective-permute-done.1 = bf16[1088]{0:T(1024)(128)(2,1)S(1)} collective-permute-done((bf16[1088]{0:T(1024)(128)(2,1)S(1)}, bf16[1088]{0:T(1024)(128)(2,1)S(1)}, u32[]{:S(2)}, u32[]{:S(2)}) %collective-permute-start.1) | collective-permute-done | bytes 2208 | tf_op jit(solution)/shard_map/ppermute | solution.py:394
  49.4 9.5 %collective-permute-done.4.refs_5_.refs_1_ = bf16[4,128,512]{2,1,0:T(8,128)(2,1)S(1)} collective-permute-done((bf16[4,128,512]{2,1,0:T(8,128)(2,1)S(1)}, bf16[4,128,512]{2,1,0:T(8,128)(2,1)S(1)}, u32[]{:S(2)}, u32[]{:S(2)}) %collective-permute-start.4) | collective-permute-done | bytes 524320 | tf_op jit(solution)/shard_map/ppermute | solution.py:394
  58.8 5.9 collective-permute-done.5.refs_6_.refs_2_
  64.8 4.2 norm_group.1.refs_0_.refs_1_.refs_2_.refs_3_
  76.2 7.0 %project.2 = (bf16[512,256]{1,0:T(8,128)(2,1)S(1)}, bf16[512,256]{1,0:T(8,128)(2,1)S(1)}, f32[512,384]{1,0:T(8,128)S(1)}) custom-call(s32[3]{0:T(128)S(1)} %copy-done.68, bf16[512,2048]{1,0:T(8,128)(2,1)S(1)} %copy-done.2, bf16[512,2048]{1,0:T(8,128)(2,1)S(1)} %copy-done.2, bf16[512,2048]{1,0:T(8,128)(2,1)S(1)} %copy-done.2, ...), custom_call_target="tpu_custom_call" | custom-call | tf_op jit(solution)/shard_map/project/pallas_call | solution.py:758
  84.9 7.0 %project.3 = (bf16[512,256]{1,0:T(8,128)(2,1)S(1)}, bf16[512,256]{1,0:T(8,128)(2,1)S(1)}, f32[512,384]{1,0:T(8,128)S(1)}) custom-call(s32[3]{0:T(128)S(1)} %copy-done.68, bf16[512,2048]{1,0:T(8,128)(2,1)} %collective-permute-done.7.refs_0_.refs_1_.refs_2_.refs_3_.refs_4_.refs_5_.refs_6_.refs_7_, ...), custom_call_target="tpu_custom_call" | custom-call | tf_op jit(solution)/shard_map/project/pallas_call | solution.py:758
  95.7 4.6 lay_order.1.refs_2_
  100.4 7.8 %collective-permute-done.8 = bf16[1024,256]{1,0:T(8,128)(2,1)} collective-permute-done((bf16[1024,256]{1,0:T(8,128)(2,1)}, bf16[1024,256]{1,0:T(8,128)(2,1)}, u32[]{:S(2)}, u32[]{:S(2)}) %collective-permute-start.8) | collective-permute-done | bytes 524320 | tf_op jit(solution)/shard_map/ppermute | solution.py:394
  109.3 2.8 attend.2
  112.1 2.8 attend.3
  119.8 4.4 collective-permute-start.14
  128.5 3.4 collective-permute-done.13.refs_1_
  131.8 22.6 %collective-permute-done.14.refs_2_ = bf16[128,1536]{1,0:T(8,128)(2,1)S(1)} collective-permute-done((bf16[128,1536]{1,0:T(8,128)(2,1)S(1)}, bf16[128,1536]{1,0:T(8,128)(2,1)S(1)}, u32[]{:S(2)}, u32[]{:S(2)}) %collective-permute-start.14) | collective-permute-done | bytes 393248 | tf_op jit(solution)/shard_map/ppermute | solution.py:594
  154.4 3.8 collective-permute-done.15.refs_3_
  159.6 3.9 ring_order.1.refs_0_.refs_2_
  166.3 12.1 %collective-permute-done.10 = bf16[128,2048]{1,0:T(8,128)(2,1)S(1)} collective-permute-done((bf16[128,2048]{1,0:T(8,128)(2,1)}, bf16[128,2048]{1,0:T(8,128)(2,1)S(1)}, u32[]{:S(2)}, u32[]{:S(2)}) %collective-permute-start.10) | collective-permute-done | bytes 524320 | tf_op jit(solution)/shard_map/ppermute | solution.py:401
  178.5 31.1 %collective-permute-done.11 = bf16[128,2048]{1,0:T(8,128)(2,1)S(1)} collective-permute-done((bf16[128,2048]{1,0:T(8,128)(2,1)S(1)}, bf16[128,2048]{1,0:T(8,128)(2,1)S(1)}, u32[]{:S(2)}, u32[]{:S(2)}) %collective-permute-start.11) | collective-permute-done | bytes 524320 | tf_op jit(solution)/shard_map/ppermute | solution.py:401
  212.3 3.3 collective-permute-start.17
  223.7 3.9 product.13
  228.7 29.4 %collective-permute-done.17 = bf16[128,2048]{1,0:T(8,128)(2,1)} collective-permute-done((bf16[128,2048]{1,0:T(8,128)(2,1)}, bf16[128,2048]{1,0:T(8,128)(2,1)}, u32[]{:S(2)}, u32[]{:S(2)}) %collective-permute-start.17) | collective-permute-done | bytes 524320 | tf_op jit(solution)/shard_map/ppermute | solution.py:394
  258.1 3.6 collective-permute-done.18
  266.3 3.4 copy-done.4
  269.7 4.7 inner_parts.2
  274.6 4.8 inner_parts.3
  280.5 15.0 %ffn_gradients.1 = bf16[4,512,2304]{2,1,0:T(8,128)(2,1)} custom-call(bf16[512,2048]{1,0:T(8,128)(2,1)} %copy-done.12, bf16[512,2048]{1,0:T(8,128)(2,1)} %copy-done.15, bf16[512,2048]{1,0:T(8,128)(2,1)} %ring_order.1.refs_0_.refs_2_, bf16[512,2048]{1,0:T(8,128)(2,1)} %collective-permute-done.19.refs_0_.refs_3_, ...), custom_call_target="tpu_custom_call" | custom-call | tf_op jit(solution)/shard_map/ffn_gradients/pallas_call | solution.py:1184
  296.4 2.8 copy-done.5
  300.6 4.2 product.14
  304.9 4.1 collective-permute-done.21.refs_2_
  309.0 4.4 product.15
  316.3 34.5 %collective-permute-done.24 = bf16[128,2048]{1,0:T(8,128)(2,1)S(1)} collective-permute-done((bf16[128,2048]{1,0:T(8,128)(2,1)S(1)}, bf16[128,2048]{1,0:T(8,128)(2,1)S(1)}, u32[]{:S(2)}, u32[]{:S(2)}) %collective-permute-start.24) | collective-permute-done | bytes 524320 | tf_op jit(solution)/shard_map/ppermute | solution.py:401
  350.7 8.7 %collective-permute-done.22 = bf16[128,2048]{1,0:T(8,128)(2,1)S(1)} collective-permute-done((bf16[128,2048]{1,0:T(8,128)(2,1)S(1)}, bf16[128,2048]{1,0:T(8,128)(2,1)S(1)}, u32[]{:S(2)}, u32[]{:S(2)}) %collective-permute-start.22) | collective-permute-done | bytes 524320 | tf_op jit(solution)/shard_map/ppermute | solution.py:401
  361.4 3.2 collective-permute-start.27
  366.1 10.9 %collective-permute-done.27 = bf16[128,2048]{1,0:T(8,128)(2,1)S(1)} collective-permute-done((bf16[128,2048]{1,0:T(8,128)(2,1)S(1)}, bf16[128,2048]{1,0:T(8,128)(2,1)S(1)}, u32[]{:S(2)}, u32[]{:S(2)}) %collective-permute-start.27) | collective-permute-done | bytes 524320 | tf_op jit(solution)/shard_map/ppermute | solution.py:394
  377.0 20.6 %collective-permute-done.26 = bf16[128,2048]{1,0:T(8,128)(2,1)S(1)} collective-permute-done((bf16[128,2048]{1,0:T(8,128)(2,1)S(1)}, bf16[128,2048]{1,0:T(8,128)(2,1)S(1)}, u32[]{:S(2)}, u32[]{:S(2)}) %collective-permute-start.26) | collective-permute-done | bytes 524320 | tf_op jit(solution)/shard_map/ppermute | solution.py:394
  397.6 11.1 %collective-permute-done.25 = bf16[128,2048]{1,0:T(8,128)(2,1)S(1)} collective-permute-done((bf16[128,2048]{1,0:T(8,128)(2,1)S(1)}, bf16[128,2048]{1,0:T(8,128)(2,1)S(1)}, u32[]{:S(2)}, u32[]{:S(2)}) %collective-permute-start.25) | collective-permute-done | bytes 524320 | tf_op jit(solution)/shard_map/ppermute | solution.py:394
  420.4 2.8 product.16
  423.4 4.4 attend_back.2
  430.4 4.4 attend_back.3
  438.2 2.8 keys_back.2
  440.9 7.4 %collective-permute-done.30.refs_2_ = bf16[512,256]{1,0:T(8,128)(2,1)S(1)} collective-permute-done((bf16[512,256]{1,0:T(8,128)(2,1)S(1)}, bf16[512,256]{1,0:T(8,128)(2,1)S(1)}, u32[]{:S(2)}, u32[]{:S(2)}) %collective-permute-start.30) | collective-permute-done | bytes 262176 | tf_op jit(solution)/shard_map/ppermute | solution.py:1421
  449.1 2.8 keys_back.3
  456.9 6.5 all-gather.15.cloned.1.call-done
  471.1 8.6 %head_gradients.1 = (bf16[4,144,768]{2,1,0:T(8,128)(2,1)S(1)}, bf16[4,144,768]{2,1,0:T(8,128)(2,1)S(1)}, bf16[4,144,768]{2,1,0:T(8,128)(2,1)S(1)}, bf16[4,144,768]{2,1,0:T(8,128)(2,1)S(1)}) custom-call(s32[3]{0:T(128)S(1)} %copy-done.69, bf16[512,2048]{1,0:T(8,128)(2,1)S(1)} %copy-done.3, bf16[512,2048]{1,0:T(8,128)(2,1)S(1)} %copy-done.3, ...), custom_call_target="tpu_custom_call" | custom-call | tf_op jit(solution)/shard_map/head_gradients/pallas_call | solution.py:1073
  479.8 4.1 product.18
  487.1 4.0 collective-permute-done.34.refs_4_
  491.1 5.2 product.19
  496.3 15.7 %collective-permute-done.35 = bf16[4,144,768]{2,1,0:T(8,128)(2,1)S(1)} collective-permute-done((bf16[4,144,768]{2,1,0:T(8,128)(2,1)S(1)}, bf16[4,144,768]{2,1,0:T(8,128)(2,1)S(1)}, u32[]{:S(2)}, u32[]{:S(2)}) %collective-permute-start.35) | collective-permute-done | bytes 884768 | tf_op jit(solution)/shard_map/ppermute | solution.py:401
  512.0 17.7 %collective-permute-done.36 = bf16[4,144,768]{2,1,0:T(8,128)(2,1)S(1)} collective-permute-done((bf16[4,144,768]{2,1,0:T(8,128)(2,1)S(1)}, bf16[4,144,768]{2,1,0:T(8,128)(2,1)S(1)}, u32[]{:S(2)}, u32[]{:S(2)}) %collective-permute-start.36) | collective-permute-done | bytes 884768 | tf_op jit(solution)/shard_map/ppermute | solution.py:401
  529.7 4.6 collective-permute-done.37
  535.6 5.3 all-to-all-start.1
  540.9 12.2 %all-to-all-done.1 = bf16[4,144,512]{2,1,0:T(8,128)(2,1)S(1)} async-done(((bf16[4,144,512]{2,1,0:T(8,128)(2,1)}), bf16[4,144,512]{2,1,0:T(8,128)(2,1)S(1)}, u32[]{:S(2)}, u32[]{:S(2)}) %all-to-all-start.1) | async-done | bytes 589856 | tf_op jit(solution)/shard_map/all_to_all | solution.py:1292
  557.3 4.2 collective-permute-start.39
  561.8 21.7 %collective-permute-done.41.refs_1_ = bf16[4,144,768]{2,1,0:T(8,128)(2,1)} collective-permute-done((bf16[4,144,768]{2,1,0:T(8,128)(2,1)S(1)}, bf16[4,144,768]{2,1,0:T(8,128)(2,1)}, u32[]{:S(2)}, u32[]{:S(2)}) %collective-permute-start.41) | collective-permute-done | bytes 884768 | tf_op jit(solution)/shard_map/ppermute | solution.py:394
  585.3 8.5 %lay_rows.1 = f32[1536,2048]{1,0:T(8,128)} custom-call(bf16[2,2,2,4,128,768]{5,4,3,2,1,0:T(8,128)(2,1)} %bitcast.185), custom_call_target="tpu_custom_call" | custom-call | tf_op jit(solution)/shard_map/lay_rows/pallas_call | solution.py:496
  593.8 22.9 %lay_in.1 = (f32[512,6144]{1,0:T(8,128)}, f32[512,6144]{1,0:T(8,128)}, f32[512,128]{1,0:T(8,128)}) custom-call(bf16[2,2,2,4,128,1536]{5,4,3,2,1,0:T(8,128)(2,1)} %bitcast.184, bf16[512,6144]{1,0:T(8,128)(2,1)} %gate_ref.1, bf16[512,6144]{1,0:T(8,128)(2,1)} %up_ref.1), custom_call_target="tpu_custom_call" | custom-call | tf_op jit(solution)/shard_map/lay_in/pallas_call | solution.py:465
  617.3 8.8 %collective-permute-done.38 = bf16[2,128,2048]{2,1,0:T(8,128)(2,1)} collective-permute-done((bf16[2,128,2048]{2,1,0:T(8,128)(2,1)}, bf16[2,128,2048]{2,1,0:T(8,128)(2,1)}, u32[]{:S(2)}, u32[]{:S(2)}) %collective-permute-start.38) | collective-permute-done | bytes 1048608 | tf_op jit(solution)/shard_map/ppermute | solution.py:401
  626.0 20.3 %collective-permute-done.39 = bf16[2,128,2048]{2,1,0:T(8,128)(2,1)} collective-permute-done((bf16[2,128,2048]{2,1,0:T(8,128)(2,1)}, bf16[2,128,2048]{2,1,0:T(8,128)(2,1)}, u32[]{:S(2)}, u32[]{:S(2)}) %collective-permute-start.39) | collective-permute-done | bytes 1048608 | tf_op jit(solution)/shard_map/ppermute | solution.py:401
  646.4 3.8 collective-permute-done.40
  650.2 3.8 convert_add_fusion
  656.4 3.6 fusion.11
  660.1 9.9 %lay_heads.1 = (f32[512,2048]{1,0:T(8,128)}, f32[512,1024]{1,0:T(8,128)}, f32[512,1024]{1,0:T(8,128)}, f32[512,2048]{1,0:T(8,128)}, f32[512,128]{1,0:T(8,128)S(1)}, /*index=5*/f32[16,768]{1,0:T(8,128)S(1)}) custom-call(s32[3]{0:T(128)S(1)} %copy-done.69, bf16[4,144,768]{2,1,0:T(8,128)(2,1)S(1)} %copy-done.29, ...), custom_call_target="tpu_custom_call" | custom-call | tf_op jit(solution)/shard_map/lay_heads/pallas_call | solution.py:561
  (369 shorter events, 109.5 us)
Async XLA Ops:
  7.2 88.4 %copy-start = (bf16[512,2048]{1,0:T(8,128)(2,1)S(1)}, bf16[512,2048]{1,0:T(8,128)(2,1)}, u32[]{:S(2)}) copy-start(bf16[512,2048]{1,0:T(8,128)(2,1)} %param.22) | copy-start | bytes 6291460
  7.2 57.6 %all-gather.9.cloned.1.call-start = ((), (), s32[]{:S(2)}) async-start(), calls=%async_computation.3 | async-start | bytes 2621440 | tf_op jit(solution)/shard_map/all_gather | solution.py:1301
  12.5 33.0 %all-to-all-start = ((bf16[4,128,512]{2,1,0:T(8,128)(2,1)}), bf16[4,128,512]{2,1,0:T(8,128)(2,1)S(1)}, u32[]{:S(2)}, u32[]{:S(2)}) async-start(bf16[4,128,512]{2,1,0:T(8,128)(2,1)} %take_columns.2), calls=%async_computation | async-start | bytes 1048576 | tf_op jit(solution)/shard_map/all_to_all | solution.py:1292
  17.8 141.7 %all-gather.13.cloned.1.call-start = ((), (), s32[]{:S(2)}) async-start(), calls=%async_computation.6 | async-start | bytes 2621440 | tf_op jit(solution)/shard_map/all_gather | solution.py:1346
  17.9 26.9 %collective-permute-start.1 = (bf16[1088]{0:T(1024)(128)(2,1)S(1)}, bf16[1088]{0:T(1024)(128)(2,1)S(1)}, u32[]{:S(2)}, u32[]{:S(2)}) collective-permute-start(bf16[1088]{0:T(1024)(128)(2,1)S(1)} %concatenate.35), channel_id=1, source_target_pairs={{0,2},{2,4},{4,6},{6,0},{1,3},{3,5},{5,7},{7,1},{8,10},{10,12},{12... | collective-permute-start | bytes 6536 | tf_op jit(solution)/shard_map/ppermute | solution.py:394
  19.4 25.5 %collective-permute-start.2 = (bf16[1088]{0:T(1024)(128)(2,1)S(1)}, bf16[1088]{0:T(1024)(128)(2,1)S(1)}, u32[]{:S(2)}, u32[]{:S(2)}) collective-permute-start(bf16[1088]{0:T(1024)(128)(2,1)S(1)} %concatenate.35), channel_id=1, source_target_pairs={{0,4},{2,6},{4,0},{6,2},{1,5},{3,7},{5,1},{7,3},{8,12},{10,14},{12... | collective-permute-start | bytes 6536 | tf_op jit(solution)/shard_map/ppermute | solution.py:394
  20.3 25.1 %collective-permute-start.3 = (bf16[1088]{0:T(1024)(128)(2,1)S(1)}, bf16[1088]{0:T(1024)(128)(2,1)S(1)}, u32[]{:S(2)}, u32[]{:S(2)}) collective-permute-start(bf16[1088]{0:T(1024)(128)(2,1)S(1)} %concatenate.35), channel_id=1, source_target_pairs={{0,6},{2,0},{4,2},{6,4},{1,7},{3,1},{5,3},{7,5},{8,14},{10,8},{12,... | collective-permute-start | bytes 6536 | tf_op jit(solution)/shard_map/ppermute | solution.py:394
  22.3 4.3 collective-permute-start
  45.4 13.4 %collective-permute-start.4 = (bf16[4,128,512]{2,1,0:T(8,128)(2,1)S(1)}, bf16[4,128,512]{2,1,0:T(8,128)(2,1)S(1)}, u32[]{:S(2)}, u32[]{:S(2)}) collective-permute-start(bf16[4,128,512]{2,1,0:T(8,128)(2,1)S(1)} %all-to-all-done.refs_4_.refs_0_), channel_id=1, source_target_pairs={{0,1},{1,16},{16,17},{17,0},{2,3},{3,18},{18,19},{19,2},{4,5},{5,2... | collective-permute-start | bytes 1572872 | tf_op jit(solution)/shard_map/ppermute | solution.py:394
  45.9 18.9 %collective-permute-start.5 = (bf16[4,128,512]{2,1,0:T(8,128)(2,1)S(1)}, bf16[4,128,512]{2,1,0:T(8,128)(2,1)}, u32[]{:S(2)}, u32[]{:S(2)}) collective-permute-start(bf16[4,128,512]{2,1,0:T(8,128)(2,1)S(1)} %all-to-all-done.refs_4_.refs_0_), channel_id=1, source_target_pairs={{0,16},{1,17},{16,0},{17,1},{2,18},{3,19},{18,2},{19,3},{4,20},{5,... | collective-permute-start | bytes 1572872 | tf_op jit(solution)/shard_map/ppermute | solution.py:394
  47.4 17.3 %collective-permute-start.6 = (bf16[4,128,512]{2,1,0:T(8,128)(2,1)S(1)}, bf16[4,128,512]{2,1,0:T(8,128)(2,1)}, u32[]{:S(2)}, u32[]{:S(2)}) collective-permute-start(bf16[4,128,512]{2,1,0:T(8,128)(2,1)S(1)} %all-to-all-done.refs_4_.refs_0_), channel_id=1, source_target_pairs={{0,17},{1,0},{16,1},{17,16},{2,19},{3,2},{18,3},{19,18},{4,21},{5,... | collective-permute-start | bytes 1572872 | tf_op jit(solution)/shard_map/ppermute | solution.py:394
  68.9 15.9 %collective-permute-start.7 = (bf16[512,2048]{1,0:T(8,128)(2,1)}, bf16[512,2048]{1,0:T(8,128)(2,1)}, u32[]{:S(2)}, u32[]{:S(2)}) collective-permute-start(bf16[512,2048]{1,0:T(8,128)(2,1)} %norm_group.1.refs_0_.refs_1_.refs_2_.refs_3_), channel_id=1, source_target_pairs={{0,8},{8,0},{1,9},{9,1},{2,10},{10,2},{3,11},{11,3},{4,12},{12,4},... | collective-permute-start | bytes 6291464 | tf_op jit(solution)/shard_map/ppermute | solution.py:415
  71.8 189.9 %all-gather.11.cloned.1.call-start = ((), (), s32[]{:S(2)}) async-start(), calls=%async_computation.4 | async-start | bytes 7864320 | tf_op jit(solution)/shard_map/all_gather | solution.py:1371
  93.5 14.6 %collective-permute-start.8 = (bf16[1024,256]{1,0:T(8,128)(2,1)}, bf16[1024,256]{1,0:T(8,128)(2,1)}, u32[]{:S(2)}, u32[]{:S(2)}) collective-permute-start(bf16[1024,256]{1,0:T(8,128)(2,1)} %pad_maximum_fusion.2), channel_id=1, source_target_pairs={{0,1},{1,0},{2,3},{3,2},{4,5},{5,4},{6,7},{7,6},{8,9},{9,8},{10,11... | collective-permute-start | bytes 1572872 | tf_op jit(solution)/shard_map/ppermute | solution.py:394
  118.3 6.0 collective-permute-start.9
  119.7 12.1 %collective-permute-start.13 = (bf16[128,1536]{1,0:T(8,128)(2,1)S(1)}, bf16[128,1536]{1,0:T(8,128)(2,1)S(1)}, u32[]{:S(2)}, u32[]{:S(2)}) collective-permute-start(bf16[128,1536]{1,0:T(8,128)(2,1)S(1)} %get-tuple-element.294), channel_id=1, source_target_pairs={{0,2},{2,4},{4,6},{6,0},{1,3},{3,5},{5,7},{7,1},{8,10},{10,12},{12... | collective-permute-start | bytes 1179656 | tf_op jit(solution)/shard_map/ppermute | solution.py:594
  119.8 34.6 %collective-permute-start.14 = (bf16[128,1536]{1,0:T(8,128)(2,1)S(1)}, bf16[128,1536]{1,0:T(8,128)(2,1)S(1)}, u32[]{:S(2)}, u32[]{:S(2)}) collective-permute-start(bf16[128,1536]{1,0:T(8,128)(2,1)S(1)} %get-tuple-element.293), channel_id=1, source_target_pairs={{0,4},{2,6},{4,0},{6,2},{1,5},{3,7},{5,1},{7,3},{8,12},{10,14},{12... | collective-permute-start | bytes 1179656 | tf_op jit(solution)/shard_map/ppermute | solution.py:594
  124.2 34.0 %collective-permute-start.15 = (bf16[128,1536]{1,0:T(8,128)(2,1)S(1)}, bf16[128,1536]{1,0:T(8,128)(2,1)S(1)}, u32[]{:S(2)}, u32[]{:S(2)}) collective-permute-start(bf16[128,1536]{1,0:T(8,128)(2,1)S(1)} %get-tuple-element.292), channel_id=1, source_target_pairs={{0,6},{2,0},{4,2},{6,4},{1,7},{3,1},{5,3},{7,5},{8,14},{10,8},{12,... | collective-permute-start | bytes 1179656 | tf_op jit(solution)/shard_map/ppermute | solution.py:594
  159.5 50.1 %copy-start.57 = (f32[1,128,2048]{2,1,0:T(8,128)S(1)}, f32[1,128,2048]{2,1,0:T(8,128)}, u32[]{:S(2)}) copy-start(f32[1,128,2048]{2,1,0:T(8,128)} %copy-done.56) | copy-start | bytes 3145732
  159.5 250.8 %reduce-scatter.2.cloned.1.call-start = ((), (), s32[]{:S(2)}) async-start(), calls=%async_computation.5 | async-start | bytes 11796480 | tf_op jit(solution)/shard_map/reduce_scatter | solution.py:1397
  163.5 60.1 %collective-permute-start.19 = (bf16[512,2048]{1,0:T(8,128)(2,1)}, bf16[512,2048]{1,0:T(8,128)(2,1)}, u32[]{:S(2)}, u32[]{:S(2)}) collective-permute-start(bf16[512,2048]{1,0:T(8,128)(2,1)} %ring_order.1.refs_0_.refs_2_), channel_id=1, source_target_pairs={{0,8},{8,0},{1,9},{9,1},{2,10},{10,2},{3,11},{11,3},{4,12},{12,4},... | collective-permute-start | bytes 6291464 | tf_op jit(solution)/shard_map/ppermute | solution.py:415
  163.5 14.9 %collective-permute-start.10 = (bf16[128,2048]{1,0:T(8,128)(2,1)}, bf16[128,2048]{1,0:T(8,128)(2,1)S(1)}, u32[]{:S(2)}, u32[]{:S(2)}) collective-permute-start(bf16[128,2048]{1,0:T(8,128)(2,1)} %bitcast.177), channel_id=1, source_target_pairs={{0,2},{2,4},{4,6},{6,0},{1,3},{3,5},{5,7},{7,1},{8,10},{10,12},{12... | collective-permute-start | bytes 1572872 | tf_op jit(solution)/shard_map/ppermute | solution.py:401
  163.5 46.0 %collective-permute-start.11 = (bf16[128,2048]{1,0:T(8,128)(2,1)S(1)}, bf16[128,2048]{1,0:T(8,128)(2,1)S(1)}, u32[]{:S(2)}, u32[]{:S(2)}) collective-permute-start(bf16[128,2048]{1,0:T(8,128)(2,1)S(1)} %bitcast.176), channel_id=1, source_target_pairs={{0,4},{2,6},{4,0},{6,2},{1,5},{3,7},{5,1},{7,3},{8,12},{10,14},{12... | collective-permute-start | bytes 1572872 | tf_op jit(solution)/shard_map/ppermute | solution.py:401
  163.6 46.1 %collective-permute-start.12 = (bf16[128,2048]{1,0:T(8,128)(2,1)S(1)}, bf16[128,2048]{1,0:T(8,128)(2,1)S(1)}, u32[]{:S(2)}, u32[]{:S(2)}) collective-permute-start(bf16[128,2048]{1,0:T(8,128)(2,1)S(1)} %bitcast.175), channel_id=1, source_target_pairs={{0,6},{2,0},{4,2},{6,4},{1,7},{3,1},{5,3},{7,5},{8,14},{10,8},{12,... | collective-permute-start | bytes 1572872 | tf_op jit(solution)/shard_map/ppermute | solution.py:401
  212.3 16.4 %collective-permute-start.16 = (bf16[128,2048]{1,0:T(8,128)(2,1)}, bf16[128,2048]{1,0:T(8,128)(2,1)}, u32[]{:S(2)}, u32[]{:S(2)}) collective-permute-start(bf16[128,2048]{1,0:T(8,128)(2,1)} %multiply_convert_fusion), channel_id=1, source_target_pairs={{0,2},{2,4},{4,6},{6,0},{1,3},{3,5},{5,7},{7,1},{8,10},{10,12},{12... | collective-permute-start | bytes 1572872 | tf_op jit(solution)/shard_map/ppermute | solution.py:394
  212.3 45.8 %collective-permute-start.17 = (bf16[128,2048]{1,0:T(8,128)(2,1)}, bf16[128,2048]{1,0:T(8,128)(2,1)}, u32[]{:S(2)}, u32[]{:S(2)}) collective-permute-start(bf16[128,2048]{1,0:T(8,128)(2,1)} %multiply_convert_fusion), channel_id=1, source_target_pairs={{0,4},{2,6},{4,0},{6,2},{1,5},{3,7},{5,1},{7,3},{8,12},{10,14},{12... | collective-permute-start | bytes 1572872 | tf_op jit(solution)/shard_map/ppermute | solution.py:394
  215.6 46.1 %collective-permute-start.18 = (bf16[128,2048]{1,0:T(8,128)(2,1)}, bf16[128,2048]{1,0:T(8,128)(2,1)}, u32[]{:S(2)}, u32[]{:S(2)}) collective-permute-start(bf16[128,2048]{1,0:T(8,128)(2,1)} %multiply_convert_fusion), channel_id=1, source_target_pairs={{0,6},{2,0},{4,2},{6,4},{1,7},{3,1},{5,3},{7,5},{8,14},{10,8},{12,... | collective-permute-start | bytes 1572872 | tf_op jit(solution)/shard_map/ppermute | solution.py:394
  266.2 8.3 %collective-permute-start.20 = (bf16[512,2048]{1,0:T(8,128)(2,1)S(1)}, bf16[512,2048]{1,0:T(8,128)(2,1)S(1)}, u32[]{:S(2)}, u32[]{:S(2)}) collective-permute-start(bf16[512,2048]{1,0:T(8,128)(2,1)S(1)} %constant_dynamic-update-slice_fusion.ffn_ref.refs_0_), channel_id=1, source_target_pairs={{0,8},{8,0},{1,9},{9,1},{2,10},{10,2},{3,11},{11,3},{4,12},{12,4},... | collective-permute-start | bytes 6291464 | tf_op jit(solution)/shard_map/ppermute | solution.py:415
  296.4 167.1 %all-gather.15.cloned.1.call-start = ((), (), s32[]{:S(2)}) async-start(), calls=%async_computation.7 | async-start | bytes 7077888 | tf_op jit(solution)/shard_map/all_gather | solution.py:1295
  304.8 54.7 %copy-start.80 = (f32[128,2048]{1,0:T(8,128)S(1)}, f32[128,2048]{1,0:T(8,128)}, u32[]{:S(2)}) copy-start(f32[128,2048]{1,0:T(8,128)} %copy-done.79) | copy-start | bytes 3145732
  304.8 54.7 %copy-start.93 = (f32[1,4,4,128]{3,1,2,0:T(4,128)S(1)}, f32[1,4,4,128]{3,1,2,0:T(4,128)}, u32[]{:S(2)}) copy-start(f32[1,4,4,128]{3,1,2,0:T(4,128)} %copy-done.92) | copy-start | bytes 24580
  304.8 4.2 collective-permute-start.21
  313.5 37.3 %collective-permute-start.24 = (bf16[128,2048]{1,0:T(8,128)(2,1)S(1)}, bf16[128,2048]{1,0:T(8,128)(2,1)S(1)}, u32[]{:S(2)}, u32[]{:S(2)}) collective-permute-start(bf16[128,2048]{1,0:T(8,128)(2,1)S(1)} %bitcast.180), channel_id=1, source_target_pairs={{0,6},{2,0},{4,2},{6,4},{1,7},{3,1},{5,3},{7,5},{8,14},{10,8},{12,... | collective-permute-start | bytes 1572872 | tf_op jit(solution)/shard_map/ppermute | solution.py:401
  313.5 37.2 %collective-permute-start.23 = (bf16[128,2048]{1,0:T(8,128)(2,1)S(1)}, bf16[128,2048]{1,0:T(8,128)(2,1)S(1)}, u32[]{:S(2)}, u32[]{:S(2)}) collective-permute-start(bf16[128,2048]{1,0:T(8,128)(2,1)S(1)} %bitcast.179), channel_id=1, source_target_pairs={{0,4},{2,6},{4,0},{6,2},{1,5},{3,7},{5,1},{7,3},{8,12},{10,14},{12... | collective-permute-start | bytes 1572872 | tf_op jit(solution)/shard_map/ppermute | solution.py:401
  314.5 44.9 %collective-permute-start.22 = (bf16[128,2048]{1,0:T(8,128)(2,1)S(1)}, bf16[128,2048]{1,0:T(8,128)(2,1)S(1)}, u32[]{:S(2)}, u32[]{:S(2)}) collective-permute-start(bf16[128,2048]{1,0:T(8,128)(2,1)S(1)} %bitcast.178), channel_id=1, source_target_pairs={{0,2},{2,4},{4,6},{6,0},{1,3},{3,5},{5,7},{7,1},{8,10},{10,12},{12... | collective-permute-start | bytes 1572872 | tf_op jit(solution)/shard_map/ppermute | solution.py:401
  361.4 15.6 %collective-permute-start.27 = (bf16[128,2048]{1,0:T(8,128)(2,1)S(1)}, bf16[128,2048]{1,0:T(8,128)(2,1)S(1)}, u32[]{:S(2)}, u32[]{:S(2)}) collective-permute-start(bf16[128,2048]{1,0:T(8,128)(2,1)S(1)} %get-tuple-element.282), channel_id=1, source_target_pairs={{0,6},{2,0},{4,2},{6,4},{1,7},{3,1},{5,3},{7,5},{8,14},{10,8},{12,... | collective-permute-start | bytes 1572872 | tf_op jit(solution)/shard_map/ppermute | solution.py:394
  364.6 33.0 %collective-permute-start.26 = (bf16[128,2048]{1,0:T(8,128)(2,1)S(1)}, bf16[128,2048]{1,0:T(8,128)(2,1)S(1)}, u32[]{:S(2)}, u32[]{:S(2)}) collective-permute-start(bf16[128,2048]{1,0:T(8,128)(2,1)S(1)} %get-tuple-element.282), channel_id=1, source_target_pairs={{0,4},{2,6},{4,0},{6,2},{1,5},{3,7},{5,1},{7,3},{8,12},{10,14},{12... | collective-permute-start | bytes 1572872 | tf_op jit(solution)/shard_map/ppermute | solution.py:394
  365.4 43.4 %collective-permute-start.25 = (bf16[128,2048]{1,0:T(8,128)(2,1)S(1)}, bf16[128,2048]{1,0:T(8,128)(2,1)S(1)}, u32[]{:S(2)}, u32[]{:S(2)}) collective-permute-start(bf16[128,2048]{1,0:T(8,128)(2,1)S(1)} %get-tuple-element.282), channel_id=1, source_target_pairs={{0,2},{2,4},{4,6},{6,0},{1,3},{3,5},{5,7},{7,1},{8,10},{10,12},{12... | collective-permute-start | bytes 1572872 | tf_op jit(solution)/shard_map/ppermute | solution.py:394
  412.4 181.3 %all-gather.17.cloned.1.call-start = ((), (), s32[]{:S(2)}) async-start(), calls=%async_computation.8 | async-start | bytes 14155776 | tf_op jit(solution)/shard_map/all_gather | solution.py:1295
  412.5 16.6 %collective-permute-start.29 = (bf16[512,2048]{1,0:T(8,128)(2,1)}, bf16[512,2048]{1,0:T(8,128)(2,1)S(1)}, u32[]{:S(2)}, u32[]{:S(2)}) collective-permute-start(bf16[512,2048]{1,0:T(8,128)(2,1)} %pad_maximum_fusion.refs_0_.refs_8_.refs_9_.refs_10_.refs_11_), channel_id=1, source_target_pairs={{0,8},{8,0},{1,9},{9,1},{2,10},{10,2},{3,11},{11,3},{4,12},{12,4},... | collective-permute-start | bytes 6291464 | tf_op jit(solution)/shard_map/ppermute | solution.py:415
  415.3 36.5 %collective-permute-start.31 = (bf16[128,1536]{1,0:T(8,128)(2,1)}, bf16[128,1536]{1,0:T(8,128)(2,1)}, u32[]{:S(2)}, u32[]{:S(2)}) collective-permute-start(bf16[128,1536]{1,0:T(8,128)(2,1)} %get-tuple-element.290), channel_id=1, source_target_pairs={{0,2},{2,4},{4,6},{6,0},{1,3},{3,5},{5,7},{7,1},{8,10},{10,12},{12... | collective-permute-start | bytes 1179656 | tf_op jit(solution)/shard_map/ppermute | solution.py:594
  417.8 34.6 %collective-permute-start.32 = (bf16[128,1536]{1,0:T(8,128)(2,1)}, bf16[128,1536]{1,0:T(8,128)(2,1)}, u32[]{:S(2)}, u32[]{:S(2)}) collective-permute-start(bf16[128,1536]{1,0:T(8,128)(2,1)} %get-tuple-element.289), channel_id=1, source_target_pairs={{0,4},{2,6},{4,0},{6,2},{1,5},{3,7},{5,1},{7,3},{8,12},{10,14},{12... | collective-permute-start | bytes 1179656 | tf_op jit(solution)/shard_map/ppermute | solution.py:594
  420.2 34.3 %collective-permute-start.33 = (bf16[128,1536]{1,0:T(8,128)(2,1)}, bf16[128,1536]{1,0:T(8,128)(2,1)}, u32[]{:S(2)}, u32[]{:S(2)}) collective-permute-start(bf16[128,1536]{1,0:T(8,128)(2,1)} %get-tuple-element.288), channel_id=1, source_target_pairs={{0,6},{2,0},{4,2},{6,4},{1,7},{3,1},{5,3},{7,5},{8,14},{10,8},{12,... | collective-permute-start | bytes 1179656 | tf_op jit(solution)/shard_map/ppermute | solution.py:594
  428.6 8.9 %collective-permute-start.28 = (bf16[512,256]{1,0:T(8,128)(2,1)S(1)}, bf16[512,256]{1,0:T(8,128)(2,1)S(1)}, u32[]{:S(2)}, u32[]{:S(2)}) collective-permute-start(bf16[512,256]{1,0:T(8,128)(2,1)S(1)} %bitcast.181), channel_id=1, source_target_pairs={{0,1},{1,0},{2,3},{3,2},{4,5},{5,4},{6,7},{7,6},{8,9},{9,8},{10,11... | collective-permute-start | bytes 786440 | tf_op jit(solution)/shard_map/ppermute | solution.py:1421
  436.4 12.0 %collective-permute-start.30 = (bf16[512,256]{1,0:T(8,128)(2,1)S(1)}, bf16[512,256]{1,0:T(8,128)(2,1)S(1)}, u32[]{:S(2)}, u32[]{:S(2)}) collective-permute-start(bf16[512,256]{1,0:T(8,128)(2,1)S(1)} %bitcast.182), channel_id=1, source_target_pairs={{0,1},{1,0},{2,3},{3,2},{4,5},{5,4},{6,7},{7,6},{8,9},{9,8},{10,11... | collective-permute-start | bytes 786440 | tf_op jit(solution)/shard_map/ppermute | solution.py:1421
  483.9 7.2 %collective-permute-start.34 = (bf16[2,512,2048]{2,1,0:T(8,128)(2,1)S(1)}, bf16[2,512,2048]{2,1,0:T(8,128)(2,1)S(1)}, u32[]{:S(2)}, u32[]{:S(2)}) collective-permute-start(bf16[2,512,2048]{2,1,0:T(8,128)(2,1)S(1)} %product.18), channel_id=1, source_target_pairs={{0,8},{8,0},{1,9},{9,1},{2,10},{10,2},{3,11},{11,3},{4,12},{12,4},... | collective-permute-start | bytes 12582920 | tf_op jit(solution)/shard_map/ppermute | solution.py:415
  484.2 27.8 %collective-permute-start.35 = (bf16[4,144,768]{2,1,0:T(8,128)(2,1)S(1)}, bf16[4,144,768]{2,1,0:T(8,128)(2,1)S(1)}, u32[]{:S(2)}, u32[]{:S(2)}) collective-permute-start(bf16[4,144,768]{2,1,0:T(8,128)(2,1)S(1)} %get-tuple-element.208), channel_id=1, source_target_pairs={{0,1},{1,16},{16,17},{17,0},{2,3},{3,18},{18,19},{19,2},{4,5},{5,2... | collective-permute-start | bytes 2654216 | tf_op jit(solution)/shard_map/ppermute | solution.py:401
  484.7 45.0 %collective-permute-start.36 = (bf16[4,144,768]{2,1,0:T(8,128)(2,1)S(1)}, bf16[4,144,768]{2,1,0:T(8,128)(2,1)S(1)}, u32[]{:S(2)}, u32[]{:S(2)}) collective-permute-start(bf16[4,144,768]{2,1,0:T(8,128)(2,1)S(1)} %get-tuple-element.207), channel_id=1, source_target_pairs={{0,16},{1,17},{16,0},{17,1},{2,18},{3,19},{18,2},{19,3},{4,20},{5,... | collective-permute-start | bytes 2654216 | tf_op jit(solution)/shard_map/ppermute | solution.py:401
  485.9 48.4 %collective-permute-start.37 = (bf16[4,144,768]{2,1,0:T(8,128)(2,1)S(1)}, bf16[4,144,768]{2,1,0:T(8,128)(2,1)S(1)}, u32[]{:S(2)}, u32[]{:S(2)}) collective-permute-start(bf16[4,144,768]{2,1,0:T(8,128)(2,1)S(1)} %get-tuple-element.206), channel_id=1, source_target_pairs={{0,17},{1,0},{16,1},{17,16},{2,19},{3,2},{18,3},{19,18},{4,21},{5,... | collective-permute-start | bytes 2654216 | tf_op jit(solution)/shard_map/ppermute | solution.py:401
  534.7 50.3 %copy-start.82 = (bf16[2,1,64,2048]{3,2,1,0:T(8,128)(2,1)S(1)}, bf16[2,1,64,2048]{3,2,1,0:T(8,128)(2,1)}, u32[]{:S(2)}) copy-start(bf16[2,1,64,2048]{3,2,1,0:T(8,128)(2,1)} %param.16) | copy-start | bytes 1572868
  535.6 49.7 %copy-start.94 = (f32[1,4,4,128]{3,2,1,0:T(4,128)S(1)}, f32[1,4,4,128]{3,2,1,0:T(4,128)}, u32[]{:S(2)}) copy-start(f32[1,4,4,128]{3,2,1,0:T(4,128)} %get-tuple-element.298) | copy-start | bytes 24580
  535.6 17.5 %all-to-all-start.1 = ((bf16[4,144,512]{2,1,0:T(8,128)(2,1)}), bf16[4,144,512]{2,1,0:T(8,128)(2,1)S(1)}, u32[]{:S(2)}, u32[]{:S(2)}) async-start(bf16[4,144,512]{2,1,0:T(8,128)(2,1)} %slice.98), calls=%async_computation.2 | async-start | bytes 1179648 | tf_op jit(solution)/shard_map/all_to_all | solution.py:1292
  553.1 63.5 %copy-start.28 = (bf16[4,144,768]{2,1,0:T(8,128)(2,1)}, bf16[4,144,768]{2,1,0:T(8,128)(2,1)S(1)}, u32[]{:S(2)}) copy-start(bf16[4,144,768]{2,1,0:T(8,128)(2,1)S(1)} %pad_maximum_fusion.1.refs_0_) | copy-start | bytes 2654212
  553.1 30.4 %collective-permute-start.41 = (bf16[4,144,768]{2,1,0:T(8,128)(2,1)S(1)}, bf16[4,144,768]{2,1,0:T(8,128)(2,1)}, u32[]{:S(2)}, u32[]{:S(2)}) collective-permute-start(bf16[4,144,768]{2,1,0:T(8,128)(2,1)S(1)} %pad_maximum_fusion.1.refs_0_), channel_id=1, source_target_pairs={{0,1},{1,16},{16,17},{17,0},{2,3},{3,18},{18,19},{19,2},{4,5},{5,2... | collective-permute-start | bytes 2654216 | tf_op jit(solution)/shard_map/ppermute | solution.py:394
  555.8 70.2 %collective-permute-start.38 = (bf16[2,128,2048]{2,1,0:T(8,128)(2,1)}, bf16[2,128,2048]{2,1,0:T(8,128)(2,1)}, u32[]{:S(2)}, u32[]{:S(2)}) collective-permute-start(bf16[2,128,2048]{2,1,0:T(8,128)(2,1)} %get-tuple-element.220), channel_id=1, source_target_pairs={{0,2},{2,4},{4,6},{6,0},{1,3},{3,5},{5,7},{7,1},{8,10},{10,12},{12... | collective-permute-start | bytes 3145736 | tf_op jit(solution)/shard_map/ppermute | solution.py:401
  557.3 89.1 %collective-permute-start.39 = (bf16[2,128,2048]{2,1,0:T(8,128)(2,1)}, bf16[2,128,2048]{2,1,0:T(8,128)(2,1)}, u32[]{:S(2)}, u32[]{:S(2)}) collective-permute-start(bf16[2,128,2048]{2,1,0:T(8,128)(2,1)} %get-tuple-element.221), channel_id=1, source_target_pairs={{0,4},{2,6},{4,0},{6,2},{1,5},{3,7},{5,1},{7,3},{8,12},{10,14},{12... | collective-permute-start | bytes 3145736 | tf_op jit(solution)/shard_map/ppermute | solution.py:401
  561.5 88.7 %collective-permute-start.40 = (bf16[2,128,2048]{2,1,0:T(8,128)(2,1)}, bf16[2,128,2048]{2,1,0:T(8,128)(2,1)}, u32[]{:S(2)}, u32[]{:S(2)}) collective-permute-start(bf16[2,128,2048]{2,1,0:T(8,128)(2,1)} %get-tuple-element.222), channel_id=1, source_target_pairs={{0,6},{2,0},{4,2},{6,4},{1,7},{3,1},{5,3},{7,5},{8,14},{10,8},{12,... | collective-permute-start | bytes 3145736 | tf_op jit(solution)/shard_map/ppermute | solution.py:401
  561.5 55.2 %collective-permute-start.42 = (bf16[4,144,768]{2,1,0:T(8,128)(2,1)S(1)}, bf16[4,144,768]{2,1,0:T(8,128)(2,1)}, u32[]{:S(2)}, u32[]{:S(2)}) collective-permute-start(bf16[4,144,768]{2,1,0:T(8,128)(2,1)S(1)} %pad_maximum_fusion.1.refs_0_), channel_id=1, source_target_pairs={{0,16},{1,17},{16,0},{17,1},{2,18},{3,19},{18,2},{19,3},{4,20},{5,... | collective-permute-start | bytes 2654216 | tf_op jit(solution)/shard_map/ppermute | solution.py:394
  583.5 33.1 %collective-permute-start.43 = (bf16[4,144,768]{2,1,0:T(8,128)(2,1)S(1)}, bf16[4,144,768]{2,1,0:T(8,128)(2,1)}, u32[]{:S(2)}, u32[]{:S(2)}) collective-permute-start(bf16[4,144,768]{2,1,0:T(8,128)(2,1)S(1)} %pad_maximum_fusion.1.refs_0_), channel_id=1, source_target_pairs={{0,17},{1,0},{16,1},{17,16},{2,19},{3,2},{18,3},{19,18},{4,21},{5,... | collective-permute-start | bytes 2654216 | tf_op jit(solution)/shard_map/ppermute | solution.py:394
  593.8 56.4 %copy-start.54 = (f32[2,128,2048]{2,1,0:T(8,128)S(1)}, f32[2,128,2048]{2,1,0:T(8,128)}, u32[]{:S(2)}) copy-start(f32[2,128,2048]{2,1,0:T(8,128)} %copy-done.53) | copy-start | bytes 6291460
  616.7 43.3 %collective-permute-start.44 = (bf16[4,144,768]{2,1,0:T(8,128)(2,1)S(1)}, bf16[4,144,768]{2,1,0:T(8,128)(2,1)}, u32[]{:S(2)}, u32[]{:S(2)}) collective-permute-start(bf16[4,144,768]{2,1,0:T(8,128)(2,1)S(1)} %pad_maximum_fusion.1.refs_0_), channel_id=1, source_target_pairs={{0,8},{8,0},{1,9},{9,1},{2,10},{10,2},{3,11},{11,3},{4,12},{12,4},... | collective-permute-start | bytes 2654216 | tf_op jit(solution)/shard_map/ppermute | solution.py:415
  616.8 43.2 %collective-permute-start.45 = (bf16[4,144,768]{2,1,0:T(8,128)(2,1)}, bf16[4,144,768]{2,1,0:T(8,128)(2,1)}, u32[]{:S(2)}, u32[]{:S(2)}) collective-permute-start(bf16[4,144,768]{2,1,0:T(8,128)(2,1)} %collective-permute-done.41.refs_1_), channel_id=1, source_target_pairs={{0,8},{8,0},{1,9},{9,1},{2,10},{10,2},{3,11},{11,3},{4,12},{12,4},... | collective-permute-start | bytes 2654216 | tf_op jit(solution)/shard_map/ppermute | solution.py:415
  626.0 34.0 %collective-permute-start.46 = (bf16[4,144,768]{2,1,0:T(8,128)(2,1)}, bf16[4,144,768]{2,1,0:T(8,128)(2,1)}, u32[]{:S(2)}, u32[]{:S(2)}) collective-permute-start(bf16[4,144,768]{2,1,0:T(8,128)(2,1)} %collective-permute-done.42.refs_2_), channel_id=1, source_target_pairs={{0,8},{8,0},{1,9},{9,1},{2,10},{10,2},{3,11},{11,3},{4,12},{12,4},... | collective-permute-start | bytes 2654216 | tf_op jit(solution)/shard_map/ppermute | solution.py:415
  646.4 13.6 %collective-permute-start.47 = (bf16[4,144,768]{2,1,0:T(8,128)(2,1)}, bf16[4,144,768]{2,1,0:T(8,128)(2,1)}, u32[]{:S(2)}, u32[]{:S(2)}) collective-permute-start(bf16[4,144,768]{2,1,0:T(8,128)(2,1)} %collective-permute-done.43.refs_3_), channel_id=1, source_target_pairs={{0,8},{8,0},{1,9},{9,1},{2,10},{10,2},{3,11},{11,3},{4,12},{12,4},... | collective-permute-start | bytes 2654216 | tf_op jit(solution)/shard_map/ppermute | solution.py:415
  (95 other events, 742.1 us)
Sparse Core Ops, SparseCore 0:
  9.6 53.5 all-gather.8
  71.9 45.0 all-gather.12
  159.6 68.2 all-gather.10
  296.5 93.1 reduce-scatter.1
  412.5 50.8 all-gather.14
  465.8 109.7 all-gather.16

commit v4 on v3

--- a/solution.py
+++ b/solution.py
@@ -1176,7 +1176,7 @@
 def ffn_gradients(n_shard, ffn_in, cot, d_pre, inner):
     rows, width = ffn_in[0].shape
     ff = inner[0].shape[1]
-    block = 256
+    block = min(512, width // n_shard)
     per = width // (n_shard * block)
     left = pl.BlockSpec((rows, block), lambda j: (0, j))
     wide = pl.BlockSpec((rows, 2 * ff), lambda j: (0, 0))

time: 681 us -> 680 us (level)
  no operation moved by 1% of the time
where the time goes in v4:
time: 680 us; the launch traced here: 678 us
  waiting for transfers between devices  364 us (54%)
  Pallas kernels  164 us (24%)
  starting transfers between devices  59.2 us (9%)
  local copies, waits for them, and re-layouts  51.7 us (8%)
  other arithmetic  22.9 us (3%)
  between operations  15.4 us (2%)
    ppermute x12, waiting for transfers between devices, send_terms(): lax.ppermute(pieces[count - k].astype(jnp.bfloat16), axis, [(i, (i + k) %...  157 us
    ppermute x16, waiting for transfers between devices, from_ring(): lax.ppermute(block, axis, [(i, (i + k) % count) for i in range(count)])  139 us
    unnamed x213, local copies, waits for them, and re-layouts  37.8 us
    ppermute x6, waiting for transfers between devices, exchange_ring(): lax.ppermute(piece_for(k), 'shard', [(i, (i + k) % count) for i in range(...  32.3 us
    pallas_call x10, Pallas kernels, product(): pl.pallas_call(partial(product_kernel, [(len(terms), contract) for terms,...  31.9 us
    pallas_call x1, Pallas kernels, lay_in(): pl.pallas_call(lay_in_kernel, grid=(n_hi * n_ctx, n_shard), in_specs=[pl....  22.9 us
    ppermute x16, starting transfers between devices, from_ring(): lax.ppermute(block, axis, [(i, (i + k) % count) for i in range(count)])  22.7 us
    pallas_call x1, Pallas kernels, ffn_gradients(): pl.pallas_call(ffn_gradients_kernel, grid=(width // block,), in_specs=[le...  14.4 us
  transfers between devices with their start and end apart: 56, of which 32 were waited for; matrix products, arithmetic and copies ran while one was open for 5% of the time, Pallas kernels for 19%

profile of v4, /device:TPU:14, one launch (start us, length us, event | category | flops | bytes accessed | tf_op | source)
XLA Modules:
  0.0 677.6 jit_solution(13935472667657456537)
XLA Ops:
  8.6 3.9 take_columns.2
  12.5 5.3 all-to-all-start
  22.3 4.3 take_columns.3
  26.6 18.2 %collective-permute-done.1 = bf16[1088]{0:T(1024)(128)(2,1)S(1)} collective-permute-done((bf16[1088]{0:T(1024)(128)(2,1)S(1)}, bf16[1088]{0:T(1024)(128)(2,1)S(1)}, u32[]{:S(2)}, u32[]{:S(2)}) %collective-permute-start.1) | collective-permute-done | bytes 2208 | tf_op jit(solution)/shard_map/ppermute | solution.py:394
  49.4 9.5 %collective-permute-done.4.refs_5_.refs_1_ = bf16[4,128,512]{2,1,0:T(8,128)(2,1)S(1)} collective-permute-done((bf16[4,128,512]{2,1,0:T(8,128)(2,1)S(1)}, bf16[4,128,512]{2,1,0:T(8,128)(2,1)S(1)}, u32[]{:S(2)}, u32[]{:S(2)}) %collective-permute-start.4) | collective-permute-done | bytes 524320 | tf_op jit(solution)/shard_map/ppermute | solution.py:394
  58.8 5.9 collective-permute-done.5.refs_6_.refs_2_
  64.8 4.2 norm_group.1.refs_0_.refs_1_.refs_2_.refs_3_
  76.2 7.0 %project.2 = (bf16[512,256]{1,0:T(8,128)(2,1)S(1)}, bf16[512,256]{1,0:T(8,128)(2,1)S(1)}, f32[512,384]{1,0:T(8,128)S(1)}) custom-call(s32[3]{0:T(128)S(1)} %copy-done.68, bf16[512,2048]{1,0:T(8,128)(2,1)S(1)} %copy-done.2, bf16[512,2048]{1,0:T(8,128)(2,1)S(1)} %copy-done.2, bf16[512,2048]{1,0:T(8,128)(2,1)S(1)} %copy-done.2, ...), custom_call_target="tpu_custom_call" | custom-call | tf_op jit(solution)/shard_map/project/pallas_call | solution.py:758
  84.9 7.0 %project.3 = (bf16[512,256]{1,0:T(8,128)(2,1)S(1)}, bf16[512,256]{1,0:T(8,128)(2,1)S(1)}, f32[512,384]{1,0:T(8,128)S(1)}) custom-call(s32[3]{0:T(128)S(1)} %copy-done.68, bf16[512,2048]{1,0:T(8,128)(2,1)} %collective-permute-done.7.refs_0_.refs_1_.refs_2_.refs_3_.refs_4_.refs_5_.refs_6_.refs_7_, ...), custom_call_target="tpu_custom_call" | custom-call | tf_op jit(solution)/shard_map/project/pallas_call | solution.py:758
  95.7 4.6 lay_order.1.refs_2_
  100.4 7.8 %collective-permute-done.8 = bf16[1024,256]{1,0:T(8,128)(2,1)} collective-permute-done((bf16[1024,256]{1,0:T(8,128)(2,1)}, bf16[1024,256]{1,0:T(8,128)(2,1)}, u32[]{:S(2)}, u32[]{:S(2)}) %collective-permute-start.8) | collective-permute-done | bytes 524320 | tf_op jit(solution)/shard_map/ppermute | solution.py:394
  109.3 2.8 attend.2
  112.1 2.8 attend.3
  119.8 4.4 collective-permute-start.14
  128.5 3.4 collective-permute-done.13.refs_1_
  131.8 22.6 %collective-permute-done.14.refs_2_ = bf16[128,1536]{1,0:T(8,128)(2,1)S(1)} collective-permute-done((bf16[128,1536]{1,0:T(8,128)(2,1)S(1)}, bf16[128,1536]{1,0:T(8,128)(2,1)S(1)}, u32[]{:S(2)}, u32[]{:S(2)}) %collective-permute-start.14) | collective-permute-done | bytes 393248 | tf_op jit(solution)/shard_map/ppermute | solution.py:594
  154.4 3.8 collective-permute-done.15.refs_3_
  159.6 3.9 ring_order.1.refs_0_.refs_2_
  166.3 12.1 %collective-permute-done.10 = bf16[128,2048]{1,0:T(8,128)(2,1)S(1)} collective-permute-done((bf16[128,2048]{1,0:T(8,128)(2,1)}, bf16[128,2048]{1,0:T(8,128)(2,1)S(1)}, u32[]{:S(2)}, u32[]{:S(2)}) %collective-permute-start.10) | collective-permute-done | bytes 524320 | tf_op jit(solution)/shard_map/ppermute | solution.py:401
  178.5 31.1 %collective-permute-done.11 = bf16[128,2048]{1,0:T(8,128)(2,1)S(1)} collective-permute-done((bf16[128,2048]{1,0:T(8,128)(2,1)S(1)}, bf16[128,2048]{1,0:T(8,128)(2,1)S(1)}, u32[]{:S(2)}, u32[]{:S(2)}) %collective-permute-start.11) | collective-permute-done | bytes 524320 | tf_op jit(solution)/shard_map/ppermute | solution.py:401
  212.3 3.3 collective-permute-start.17
  223.7 3.9 product.13
  228.7 29.4 %collective-permute-done.17 = bf16[128,2048]{1,0:T(8,128)(2,1)} collective-permute-done((bf16[128,2048]{1,0:T(8,128)(2,1)}, bf16[128,2048]{1,0:T(8,128)(2,1)}, u32[]{:S(2)}, u32[]{:S(2)}) %collective-permute-start.17) | collective-permute-done | bytes 524320 | tf_op jit(solution)/shard_map/ppermute | solution.py:394
  258.1 3.6 collective-permute-done.18
  266.3 3.4 copy-done.4
  269.7 4.7 inner_parts.2
  274.6 4.8 inner_parts.3
  280.5 14.4 %ffn_gradients.1 = bf16[4,512,2304]{2,1,0:T(8,128)(2,1)} custom-call(bf16[512,2048]{1,0:T(8,128)(2,1)} %copy-done.12, bf16[512,2048]{1,0:T(8,128)(2,1)} %copy-done.15, bf16[512,2048]{1,0:T(8,128)(2,1)} %ring_order.1.refs_0_.refs_2_, bf16[512,2048]{1,0:T(8,128)(2,1)} %collective-permute-done.19.refs_0_.refs_3_, ...), custom_call_target="tpu_custom_call" | custom-call | tf_op jit(solution)/shard_map/ffn_gradients/pallas_call | solution.py:1184
  295.8 2.8 copy-done.5
  300.0 4.2 product.14
  304.3 4.1 collective-permute-done.21.refs_2_
  308.4 4.4 product.15
  315.6 34.5 %collective-permute-done.24 = bf16[128,2048]{1,0:T(8,128)(2,1)S(1)} collective-permute-done((bf16[128,2048]{1,0:T(8,128)(2,1)S(1)}, bf16[128,2048]{1,0:T(8,128)(2,1)S(1)}, u32[]{:S(2)}, u32[]{:S(2)}) %collective-permute-start.24) | collective-permute-done | bytes 524320 | tf_op jit(solution)/shard_map/ppermute | solution.py:401
  350.1 8.7 %collective-permute-done.22 = bf16[128,2048]{1,0:T(8,128)(2,1)S(1)} collective-permute-done((bf16[128,2048]{1,0:T(8,128)(2,1)S(1)}, bf16[128,2048]{1,0:T(8,128)(2,1)S(1)}, u32[]{:S(2)}, u32[]{:S(2)}) %collective-permute-start.22) | collective-permute-done | bytes 524320 | tf_op jit(solution)/shard_map/ppermute | solution.py:401
  360.8 3.2 collective-permute-start.27
  365.5 10.9 %collective-permute-done.27 = bf16[128,2048]{1,0:T(8,128)(2,1)S(1)} collective-permute-done((bf16[128,2048]{1,0:T(8,128)(2,1)S(1)}, bf16[128,2048]{1,0:T(8,128)(2,1)S(1)}, u32[]{:S(2)}, u32[]{:S(2)}) %collective-permute-start.27) | collective-permute-done | bytes 524320 | tf_op jit(solution)/shard_map/ppermute | solution.py:394
  376.4 20.6 %collective-permute-done.26 = bf16[128,2048]{1,0:T(8,128)(2,1)S(1)} collective-permute-done((bf16[128,2048]{1,0:T(8,128)(2,1)S(1)}, bf16[128,2048]{1,0:T(8,128)(2,1)S(1)}, u32[]{:S(2)}, u32[]{:S(2)}) %collective-permute-start.26) | collective-permute-done | bytes 524320 | tf_op jit(solution)/shard_map/ppermute | solution.py:394
  397.0 11.1 %collective-permute-done.25 = bf16[128,2048]{1,0:T(8,128)(2,1)S(1)} collective-permute-done((bf16[128,2048]{1,0:T(8,128)(2,1)S(1)}, bf16[128,2048]{1,0:T(8,128)(2,1)S(1)}, u32[]{:S(2)}, u32[]{:S(2)}) %collective-permute-start.25) | collective-permute-done | bytes 524320 | tf_op jit(solution)/shard_map/ppermute | solution.py:394
  419.8 2.8 product.16
  422.8 4.5 attend_back.2
  429.8 4.4 attend_back.3
  437.6 2.8 keys_back.2
  440.3 7.5 %collective-permute-done.30.refs_2_ = bf16[512,256]{1,0:T(8,128)(2,1)S(1)} collective-permute-done((bf16[512,256]{1,0:T(8,128)(2,1)S(1)}, bf16[512,256]{1,0:T(8,128)(2,1)S(1)}, u32[]{:S(2)}, u32[]{:S(2)}) %collective-permute-start.30) | collective-permute-done | bytes 262176 | tf_op jit(solution)/shard_map/ppermute | solution.py:1421
  448.5 2.8 keys_back.3
  456.3 6.5 all-gather.15.cloned.1.call-done
  470.5 8.6 %head_gradients.1 = (bf16[4,144,768]{2,1,0:T(8,128)(2,1)S(1)}, bf16[4,144,768]{2,1,0:T(8,128)(2,1)S(1)}, bf16[4,144,768]{2,1,0:T(8,128)(2,1)S(1)}, bf16[4,144,768]{2,1,0:T(8,128)(2,1)S(1)}) custom-call(s32[3]{0:T(128)S(1)} %copy-done.69, bf16[512,2048]{1,0:T(8,128)(2,1)S(1)} %copy-done.3, bf16[512,2048]{1,0:T(8,128)(2,1)S(1)} %copy-done.3, ...), custom_call_target="tpu_custom_call" | custom-call | tf_op jit(solution)/shard_map/head_gradients/pallas_call | solution.py:1073
  479.2 4.1 product.18
  486.4 4.0 collective-permute-done.34.refs_4_
  490.5 5.2 product.19
  495.6 15.7 %collective-permute-done.35 = bf16[4,144,768]{2,1,0:T(8,128)(2,1)S(1)} collective-permute-done((bf16[4,144,768]{2,1,0:T(8,128)(2,1)S(1)}, bf16[4,144,768]{2,1,0:T(8,128)(2,1)S(1)}, u32[]{:S(2)}, u32[]{:S(2)}) %collective-permute-start.35) | collective-permute-done | bytes 884768 | tf_op jit(solution)/shard_map/ppermute | solution.py:401
  511.4 17.7 %collective-permute-done.36 = bf16[4,144,768]{2,1,0:T(8,128)(2,1)S(1)} collective-permute-done((bf16[4,144,768]{2,1,0:T(8,128)(2,1)S(1)}, bf16[4,144,768]{2,1,0:T(8,128)(2,1)S(1)}, u32[]{:S(2)}, u32[]{:S(2)}) %collective-permute-start.36) | collective-permute-done | bytes 884768 | tf_op jit(solution)/shard_map/ppermute | solution.py:401
  529.1 4.6 collective-permute-done.37
  535.0 5.3 all-to-all-start.1
  540.3 12.2 %all-to-all-done.1 = bf16[4,144,512]{2,1,0:T(8,128)(2,1)S(1)} async-done(((bf16[4,144,512]{2,1,0:T(8,128)(2,1)}), bf16[4,144,512]{2,1,0:T(8,128)(2,1)S(1)}, u32[]{:S(2)}, u32[]{:S(2)}) %all-to-all-start.1) | async-done | bytes 589856 | tf_op jit(solution)/shard_map/all_to_all | solution.py:1292
  556.7 4.2 collective-permute-start.39
  561.2 21.7 %collective-permute-done.41.refs_1_ = bf16[4,144,768]{2,1,0:T(8,128)(2,1)} collective-permute-done((bf16[4,144,768]{2,1,0:T(8,128)(2,1)S(1)}, bf16[4,144,768]{2,1,0:T(8,128)(2,1)}, u32[]{:S(2)}, u32[]{:S(2)}) %collective-permute-start.41) | collective-permute-done | bytes 884768 | tf_op jit(solution)/shard_map/ppermute | solution.py:394
  584.7 8.5 %lay_rows.1 = f32[1536,2048]{1,0:T(8,128)} custom-call(bf16[2,2,2,4,128,768]{5,4,3,2,1,0:T(8,128)(2,1)} %bitcast.185), custom_call_target="tpu_custom_call" | custom-call | tf_op jit(solution)/shard_map/lay_rows/pallas_call | solution.py:496
  593.2 22.9 %lay_in.1 = (f32[512,6144]{1,0:T(8,128)}, f32[512,6144]{1,0:T(8,128)}, f32[512,128]{1,0:T(8,128)}) custom-call(bf16[2,2,2,4,128,1536]{5,4,3,2,1,0:T(8,128)(2,1)} %bitcast.184, bf16[512,6144]{1,0:T(8,128)(2,1)} %gate_ref.1, bf16[512,6144]{1,0:T(8,128)(2,1)} %up_ref.1), custom_call_target="tpu_custom_call" | custom-call | tf_op jit(solution)/shard_map/lay_in/pallas_call | solution.py:465
  616.6 8.8 %collective-permute-done.38 = bf16[2,128,2048]{2,1,0:T(8,128)(2,1)} collective-permute-done((bf16[2,128,2048]{2,1,0:T(8,128)(2,1)}, bf16[2,128,2048]{2,1,0:T(8,128)(2,1)}, u32[]{:S(2)}, u32[]{:S(2)}) %collective-permute-start.38) | collective-permute-done | bytes 1048608 | tf_op jit(solution)/shard_map/ppermute | solution.py:401
  625.4 20.3 %collective-permute-done.39 = bf16[2,128,2048]{2,1,0:T(8,128)(2,1)} collective-permute-done((bf16[2,128,2048]{2,1,0:T(8,128)(2,1)}, bf16[2,128,2048]{2,1,0:T(8,128)(2,1)}, u32[]{:S(2)}, u32[]{:S(2)}) %collective-permute-start.39) | collective-permute-done | bytes 1048608 | tf_op jit(solution)/shard_map/ppermute | solution.py:401
  645.8 3.8 collective-permute-done.40
  649.5 3.8 convert_add_fusion
  655.7 3.6 fusion.11
  659.4 9.9 %lay_heads.1 = (f32[512,2048]{1,0:T(8,128)}, f32[512,1024]{1,0:T(8,128)}, f32[512,1024]{1,0:T(8,128)}, f32[512,2048]{1,0:T(8,128)}, f32[512,128]{1,0:T(8,128)S(1)}, /*index=5*/f32[16,768]{1,0:T(8,128)S(1)}) custom-call(s32[3]{0:T(128)S(1)} %copy-done.69, bf16[4,144,768]{2,1,0:T(8,128)(2,1)S(1)} %copy-done.29, ...), custom_call_target="tpu_custom_call" | custom-call | tf_op jit(solution)/shard_map/lay_heads/pallas_call | solution.py:561
  (369 shorter events, 109.5 us)
Async XLA Ops:
  7.2 88.4 %copy-start = (bf16[512,2048]{1,0:T(8,128)(2,1)S(1)}, bf16[512,2048]{1,0:T(8,128)(2,1)}, u32[]{:S(2)}) copy-start(bf16[512,2048]{1,0:T(8,128)(2,1)} %param.22) | copy-start | bytes 6291460
  7.2 57.6 %all-gather.9.cloned.1.call-start = ((), (), s32[]{:S(2)}) async-start(), calls=%async_computation.3 | async-start | bytes 2621440 | tf_op jit(solution)/shard_map/all_gather | solution.py:1301
  12.5 33.0 %all-to-all-start = ((bf16[4,128,512]{2,1,0:T(8,128)(2,1)}), bf16[4,128,512]{2,1,0:T(8,128)(2,1)S(1)}, u32[]{:S(2)}, u32[]{:S(2)}) async-start(bf16[4,128,512]{2,1,0:T(8,128)(2,1)} %take_columns.2), calls=%async_computation | async-start | bytes 1048576 | tf_op jit(solution)/shard_map/all_to_all | solution.py:1292
  17.8 141.7 %all-gather.13.cloned.1.call-start = ((), (), s32[]{:S(2)}) async-start(), calls=%async_computation.6 | async-start | bytes 2621440 | tf_op jit(solution)/shard_map/all_gather | solution.py:1346
  17.9 26.9 %collective-permute-start.1 = (bf16[1088]{0:T(1024)(128)(2,1)S(1)}, bf16[1088]{0:T(1024)(128)(2,1)S(1)}, u32[]{:S(2)}, u32[]{:S(2)}) collective-permute-start(bf16[1088]{0:T(1024)(128)(2,1)S(1)} %concatenate.35), channel_id=1, source_target_pairs={{0,2},{2,4},{4,6},{6,0},{1,3},{3,5},{5,7},{7,1},{8,10},{10,12},{12... | collective-permute-start | bytes 6536 | tf_op jit(solution)/shard_map/ppermute | solution.py:394
  19.4 25.5 %collective-permute-start.2 = (bf16[1088]{0:T(1024)(128)(2,1)S(1)}, bf16[1088]{0:T(1024)(128)(2,1)S(1)}, u32[]{:S(2)}, u32[]{:S(2)}) collective-permute-start(bf16[1088]{0:T(1024)(128)(2,1)S(1)} %concatenate.35), channel_id=1, source_target_pairs={{0,4},{2,6},{4,0},{6,2},{1,5},{3,7},{5,1},{7,3},{8,12},{10,14},{12... | collective-permute-start | bytes 6536 | tf_op jit(solution)/shard_map/ppermute | solution.py:394
  20.3 25.1 %collective-permute-start.3 = (bf16[1088]{0:T(1024)(128)(2,1)S(1)}, bf16[1088]{0:T(1024)(128)(2,1)S(1)}, u32[]{:S(2)}, u32[]{:S(2)}) collective-permute-start(bf16[1088]{0:T(1024)(128)(2,1)S(1)} %concatenate.35), channel_id=1, source_target_pairs={{0,6},{2,0},{4,2},{6,4},{1,7},{3,1},{5,3},{7,5},{8,14},{10,8},{12,... | collective-permute-start | bytes 6536 | tf_op jit(solution)/shard_map/ppermute | solution.py:394
  22.3 4.3 collective-permute-start
  45.4 13.4 %collective-permute-start.4 = (bf16[4,128,512]{2,1,0:T(8,128)(2,1)S(1)}, bf16[4,128,512]{2,1,0:T(8,128)(2,1)S(1)}, u32[]{:S(2)}, u32[]{:S(2)}) collective-permute-start(bf16[4,128,512]{2,1,0:T(8,128)(2,1)S(1)} %all-to-all-done.refs_4_.refs_0_), channel_id=1, source_target_pairs={{0,1},{1,16},{16,17},{17,0},{2,3},{3,18},{18,19},{19,2},{4,5},{5,2... | collective-permute-start | bytes 1572872 | tf_op jit(solution)/shard_map/ppermute | solution.py:394
  45.9 18.9 %collective-permute-start.5 = (bf16[4,128,512]{2,1,0:T(8,128)(2,1)S(1)}, bf16[4,128,512]{2,1,0:T(8,128)(2,1)}, u32[]{:S(2)}, u32[]{:S(2)}) collective-permute-start(bf16[4,128,512]{2,1,0:T(8,128)(2,1)S(1)} %all-to-all-done.refs_4_.refs_0_), channel_id=1, source_target_pairs={{0,16},{1,17},{16,0},{17,1},{2,18},{3,19},{18,2},{19,3},{4,20},{5,... | collective-permute-start | bytes 1572872 | tf_op jit(solution)/shard_map/ppermute | solution.py:394
  47.4 17.3 %collective-permute-start.6 = (bf16[4,128,512]{2,1,0:T(8,128)(2,1)S(1)}, bf16[4,128,512]{2,1,0:T(8,128)(2,1)}, u32[]{:S(2)}, u32[]{:S(2)}) collective-permute-start(bf16[4,128,512]{2,1,0:T(8,128)(2,1)S(1)} %all-to-all-done.refs_4_.refs_0_), channel_id=1, source_target_pairs={{0,17},{1,0},{16,1},{17,16},{2,19},{3,2},{18,3},{19,18},{4,21},{5,... | collective-permute-start | bytes 1572872 | tf_op jit(solution)/shard_map/ppermute | solution.py:394
  68.9 15.9 %collective-permute-start.7 = (bf16[512,2048]{1,0:T(8,128)(2,1)}, bf16[512,2048]{1,0:T(8,128)(2,1)}, u32[]{:S(2)}, u32[]{:S(2)}) collective-permute-start(bf16[512,2048]{1,0:T(8,128)(2,1)} %norm_group.1.refs_0_.refs_1_.refs_2_.refs_3_), channel_id=1, source_target_pairs={{0,8},{8,0},{1,9},{9,1},{2,10},{10,2},{3,11},{11,3},{4,12},{12,4},... | collective-permute-start | bytes 6291464 | tf_op jit(solution)/shard_map/ppermute | solution.py:415
  71.8 189.9 %all-gather.11.cloned.1.call-start = ((), (), s32[]{:S(2)}) async-start(), calls=%async_computation.4 | async-start | bytes 7864320 | tf_op jit(solution)/shard_map/all_gather | solution.py:1371
  93.5 14.6 %collective-permute-start.8 = (bf16[1024,256]{1,0:T(8,128)(2,1)}, bf16[1024,256]{1,0:T(8,128)(2,1)}, u32[]{:S(2)}, u32[]{:S(2)}) collective-permute-start(bf16[1024,256]{1,0:T(8,128)(2,1)} %pad_maximum_fusion.2), channel_id=1, source_target_pairs={{0,1},{1,0},{2,3},{3,2},{4,5},{5,4},{6,7},{7,6},{8,9},{9,8},{10,11... | collective-permute-start | bytes 1572872 | tf_op jit(solution)/shard_map/ppermute | solution.py:394
  118.3 6.0 collective-permute-start.9
  119.7 12.1 %collective-permute-start.13 = (bf16[128,1536]{1,0:T(8,128)(2,1)S(1)}, bf16[128,1536]{1,0:T(8,128)(2,1)S(1)}, u32[]{:S(2)}, u32[]{:S(2)}) collective-permute-start(bf16[128,1536]{1,0:T(8,128)(2,1)S(1)} %get-tuple-element.294), channel_id=1, source_target_pairs={{0,2},{2,4},{4,6},{6,0},{1,3},{3,5},{5,7},{7,1},{8,10},{10,12},{12... | collective-permute-start | bytes 1179656 | tf_op jit(solution)/shard_map/ppermute | solution.py:594
  119.8 34.6 %collective-permute-start.14 = (bf16[128,1536]{1,0:T(8,128)(2,1)S(1)}, bf16[128,1536]{1,0:T(8,128)(2,1)S(1)}, u32[]{:S(2)}, u32[]{:S(2)}) collective-permute-start(bf16[128,1536]{1,0:T(8,128)(2,1)S(1)} %get-tuple-element.293), channel_id=1, source_target_pairs={{0,4},{2,6},{4,0},{6,2},{1,5},{3,7},{5,1},{7,3},{8,12},{10,14},{12... | collective-permute-start | bytes 1179656 | tf_op jit(solution)/shard_map/ppermute | solution.py:594
  124.2 34.0 %collective-permute-start.15 = (bf16[128,1536]{1,0:T(8,128)(2,1)S(1)}, bf16[128,1536]{1,0:T(8,128)(2,1)S(1)}, u32[]{:S(2)}, u32[]{:S(2)}) collective-permute-start(bf16[128,1536]{1,0:T(8,128)(2,1)S(1)} %get-tuple-element.292), channel_id=1, source_target_pairs={{0,6},{2,0},{4,2},{6,4},{1,7},{3,1},{5,3},{7,5},{8,14},{10,8},{12,... | collective-permute-start | bytes 1179656 | tf_op jit(solution)/shard_map/ppermute | solution.py:594
  159.5 50.1 %copy-start.57 = (f32[1,128,2048]{2,1,0:T(8,128)S(1)}, f32[1,128,2048]{2,1,0:T(8,128)}, u32[]{:S(2)}) copy-start(f32[1,128,2048]{2,1,0:T(8,128)} %copy-done.56) | copy-start | bytes 3145732
  159.5 250.2 %reduce-scatter.2.cloned.1.call-start = ((), (), s32[]{:S(2)}) async-start(), calls=%async_computation.5 | async-start | bytes 11796480 | tf_op jit(solution)/shard_map/reduce_scatter | solution.py:1397
  163.5 60.1 %collective-permute-start.19 = (bf16[512,2048]{1,0:T(8,128)(2,1)}, bf16[512,2048]{1,0:T(8,128)(2,1)}, u32[]{:S(2)}, u32[]{:S(2)}) collective-permute-start(bf16[512,2048]{1,0:T(8,128)(2,1)} %ring_order.1.refs_0_.refs_2_), channel_id=1, source_target_pairs={{0,8},{8,0},{1,9},{9,1},{2,10},{10,2},{3,11},{11,3},{4,12},{12,4},... | collective-permute-start | bytes 6291464 | tf_op jit(solution)/shard_map/ppermute | solution.py:415
  163.5 14.9 %collective-permute-start.10 = (bf16[128,2048]{1,0:T(8,128)(2,1)}, bf16[128,2048]{1,0:T(8,128)(2,1)S(1)}, u32[]{:S(2)}, u32[]{:S(2)}) collective-permute-start(bf16[128,2048]{1,0:T(8,128)(2,1)} %bitcast.177), channel_id=1, source_target_pairs={{0,2},{2,4},{4,6},{6,0},{1,3},{3,5},{5,7},{7,1},{8,10},{10,12},{12... | collective-permute-start | bytes 1572872 | tf_op jit(solution)/shard_map/ppermute | solution.py:401
  163.5 46.0 %collective-permute-start.11 = (bf16[128,2048]{1,0:T(8,128)(2,1)S(1)}, bf16[128,2048]{1,0:T(8,128)(2,1)S(1)}, u32[]{:S(2)}, u32[]{:S(2)}) collective-permute-start(bf16[128,2048]{1,0:T(8,128)(2,1)S(1)} %bitcast.176), channel_id=1, source_target_pairs={{0,4},{2,6},{4,0},{6,2},{1,5},{3,7},{5,1},{7,3},{8,12},{10,14},{12... | collective-permute-start | bytes 1572872 | tf_op jit(solution)/shard_map/ppermute | solution.py:401
  163.6 46.1 %collective-permute-start.12 = (bf16[128,2048]{1,0:T(8,128)(2,1)S(1)}, bf16[128,2048]{1,0:T(8,128)(2,1)S(1)}, u32[]{:S(2)}, u32[]{:S(2)}) collective-permute-start(bf16[128,2048]{1,0:T(8,128)(2,1)S(1)} %bitcast.175), channel_id=1, source_target_pairs={{0,6},{2,0},{4,2},{6,4},{1,7},{3,1},{5,3},{7,5},{8,14},{10,8},{12,... | collective-permute-start | bytes 1572872 | tf_op jit(solution)/shard_map/ppermute | solution.py:401
  212.3 16.4 %collective-permute-start.16 = (bf16[128,2048]{1,0:T(8,128)(2,1)}, bf16[128,2048]{1,0:T(8,128)(2,1)}, u32[]{:S(2)}, u32[]{:S(2)}) collective-permute-start(bf16[128,2048]{1,0:T(8,128)(2,1)} %multiply_convert_fusion), channel_id=1, source_target_pairs={{0,2},{2,4},{4,6},{6,0},{1,3},{3,5},{5,7},{7,1},{8,10},{10,12},{12... | collective-permute-start | bytes 1572872 | tf_op jit(solution)/shard_map/ppermute | solution.py:394
  212.3 45.8 %collective-permute-start.17 = (bf16[128,2048]{1,0:T(8,128)(2,1)}, bf16[128,2048]{1,0:T(8,128)(2,1)}, u32[]{:S(2)}, u32[]{:S(2)}) collective-permute-start(bf16[128,2048]{1,0:T(8,128)(2,1)} %multiply_convert_fusion), channel_id=1, source_target_pairs={{0,4},{2,6},{4,0},{6,2},{1,5},{3,7},{5,1},{7,3},{8,12},{10,14},{12... | collective-permute-start | bytes 1572872 | tf_op jit(solution)/shard_map/ppermute | solution.py:394
  215.6 46.1 %collective-permute-start.18 = (bf16[128,2048]{1,0:T(8,128)(2,1)}, bf16[128,2048]{1,0:T(8,128)(2,1)}, u32[]{:S(2)}, u32[]{:S(2)}) collective-permute-start(bf16[128,2048]{1,0:T(8,128)(2,1)} %multiply_convert_fusion), channel_id=1, source_target_pairs={{0,6},{2,0},{4,2},{6,4},{1,7},{3,1},{5,3},{7,5},{8,14},{10,8},{12,... | collective-permute-start | bytes 1572872 | tf_op jit(solution)/shard_map/ppermute | solution.py:394
  266.2 8.3 %collective-permute-start.20 = (bf16[512,2048]{1,0:T(8,128)(2,1)S(1)}, bf16[512,2048]{1,0:T(8,128)(2,1)S(1)}, u32[]{:S(2)}, u32[]{:S(2)}) collective-permute-start(bf16[512,2048]{1,0:T(8,128)(2,1)S(1)} %constant_dynamic-update-slice_fusion.ffn_ref.refs_0_), channel_id=1, source_target_pairs={{0,8},{8,0},{1,9},{9,1},{2,10},{10,2},{3,11},{11,3},{4,12},{12,4},... | collective-permute-start | bytes 6291464 | tf_op jit(solution)/shard_map/ppermute | solution.py:415
  295.7 167.1 %all-gather.15.cloned.1.call-start = ((), (), s32[]{:S(2)}) async-start(), calls=%async_computation.7 | async-start | bytes 7077888 | tf_op jit(solution)/shard_map/all_gather | solution.py:1295
  304.2 54.7 %copy-start.80 = (f32[128,2048]{1,0:T(8,128)S(1)}, f32[128,2048]{1,0:T(8,128)}, u32[]{:S(2)}) copy-start(f32[128,2048]{1,0:T(8,128)} %copy-done.79) | copy-start | bytes 3145732
  304.2 54.7 %copy-start.93 = (f32[1,4,4,128]{3,1,2,0:T(4,128)S(1)}, f32[1,4,4,128]{3,1,2,0:T(4,128)}, u32[]{:S(2)}) copy-start(f32[1,4,4,128]{3,1,2,0:T(4,128)} %copy-done.92) | copy-start | bytes 24580
  304.2 4.2 collective-permute-start.21
  312.8 37.3 %collective-permute-start.24 = (bf16[128,2048]{1,0:T(8,128)(2,1)S(1)}, bf16[128,2048]{1,0:T(8,128)(2,1)S(1)}, u32[]{:S(2)}, u32[]{:S(2)}) collective-permute-start(bf16[128,2048]{1,0:T(8,128)(2,1)S(1)} %bitcast.180), channel_id=1, source_target_pairs={{0,6},{2,0},{4,2},{6,4},{1,7},{3,1},{5,3},{7,5},{8,14},{10,8},{12,... | collective-permute-start | bytes 1572872 | tf_op jit(solution)/shard_map/ppermute | solution.py:401
  312.9 37.2 %collective-permute-start.23 = (bf16[128,2048]{1,0:T(8,128)(2,1)S(1)}, bf16[128,2048]{1,0:T(8,128)(2,1)S(1)}, u32[]{:S(2)}, u32[]{:S(2)}) collective-permute-start(bf16[128,2048]{1,0:T(8,128)(2,1)S(1)} %bitcast.179), channel_id=1, source_target_pairs={{0,4},{2,6},{4,0},{6,2},{1,5},{3,7},{5,1},{7,3},{8,12},{10,14},{12... | collective-permute-start | bytes 1572872 | tf_op jit(solution)/shard_map/ppermute | solution.py:401
  313.9 44.9 %collective-permute-start.22 = (bf16[128,2048]{1,0:T(8,128)(2,1)S(1)}, bf16[128,2048]{1,0:T(8,128)(2,1)S(1)}, u32[]{:S(2)}, u32[]{:S(2)}) collective-permute-start(bf16[128,2048]{1,0:T(8,128)(2,1)S(1)} %bitcast.178), channel_id=1, source_target_pairs={{0,2},{2,4},{4,6},{6,0},{1,3},{3,5},{5,7},{7,1},{8,10},{10,12},{12... | collective-permute-start | bytes 1572872 | tf_op jit(solution)/shard_map/ppermute | solution.py:401
  360.8 15.6 %collective-permute-start.27 = (bf16[128,2048]{1,0:T(8,128)(2,1)S(1)}, bf16[128,2048]{1,0:T(8,128)(2,1)S(1)}, u32[]{:S(2)}, u32[]{:S(2)}) collective-permute-start(bf16[128,2048]{1,0:T(8,128)(2,1)S(1)} %get-tuple-element.282), channel_id=1, source_target_pairs={{0,6},{2,0},{4,2},{6,4},{1,7},{3,1},{5,3},{7,5},{8,14},{10,8},{12,... | collective-permute-start | bytes 1572872 | tf_op jit(solution)/shard_map/ppermute | solution.py:394
  364.0 33.0 %collective-permute-start.26 = (bf16[128,2048]{1,0:T(8,128)(2,1)S(1)}, bf16[128,2048]{1,0:T(8,128)(2,1)S(1)}, u32[]{:S(2)}, u32[]{:S(2)}) collective-permute-start(bf16[128,2048]{1,0:T(8,128)(2,1)S(1)} %get-tuple-element.282), channel_id=1, source_target_pairs={{0,4},{2,6},{4,0},{6,2},{1,5},{3,7},{5,1},{7,3},{8,12},{10,14},{12... | collective-permute-start | bytes 1572872 | tf_op jit(solution)/shard_map/ppermute | solution.py:394
  364.8 43.4 %collective-permute-start.25 = (bf16[128,2048]{1,0:T(8,128)(2,1)S(1)}, bf16[128,2048]{1,0:T(8,128)(2,1)S(1)}, u32[]{:S(2)}, u32[]{:S(2)}) collective-permute-start(bf16[128,2048]{1,0:T(8,128)(2,1)S(1)} %get-tuple-element.282), channel_id=1, source_target_pairs={{0,2},{2,4},{4,6},{6,0},{1,3},{3,5},{5,7},{7,1},{8,10},{10,12},{12... | collective-permute-start | bytes 1572872 | tf_op jit(solution)/shard_map/ppermute | solution.py:394
  411.8 181.3 %all-gather.17.cloned.1.call-start = ((), (), s32[]{:S(2)}) async-start(), calls=%async_computation.8 | async-start | bytes 14155776 | tf_op jit(solution)/shard_map/all_gather | solution.py:1295
  411.9 16.6 %collective-permute-start.29 = (bf16[512,2048]{1,0:T(8,128)(2,1)}, bf16[512,2048]{1,0:T(8,128)(2,1)S(1)}, u32[]{:S(2)}, u32[]{:S(2)}) collective-permute-start(bf16[512,2048]{1,0:T(8,128)(2,1)} %pad_maximum_fusion.refs_0_.refs_8_.refs_9_.refs_10_.refs_11_), channel_id=1, source_target_pairs={{0,8},{8,0},{1,9},{9,1},{2,10},{10,2},{3,11},{11,3},{4,12},{12,4},... | collective-permute-start | bytes 6291464 | tf_op jit(solution)/shard_map/ppermute | solution.py:415
  414.7 36.5 %collective-permute-start.31 = (bf16[128,1536]{1,0:T(8,128)(2,1)}, bf16[128,1536]{1,0:T(8,128)(2,1)}, u32[]{:S(2)}, u32[]{:S(2)}) collective-permute-start(bf16[128,1536]{1,0:T(8,128)(2,1)} %get-tuple-element.290), channel_id=1, source_target_pairs={{0,2},{2,4},{4,6},{6,0},{1,3},{3,5},{5,7},{7,1},{8,10},{10,12},{12... | collective-permute-start | bytes 1179656 | tf_op jit(solution)/shard_map/ppermute | solution.py:594
  417.2 34.6 %collective-permute-start.32 = (bf16[128,1536]{1,0:T(8,128)(2,1)}, bf16[128,1536]{1,0:T(8,128)(2,1)}, u32[]{:S(2)}, u32[]{:S(2)}) collective-permute-start(bf16[128,1536]{1,0:T(8,128)(2,1)} %get-tuple-element.289), channel_id=1, source_target_pairs={{0,4},{2,6},{4,0},{6,2},{1,5},{3,7},{5,1},{7,3},{8,12},{10,14},{12... | collective-permute-start | bytes 1179656 | tf_op jit(solution)/shard_map/ppermute | solution.py:594
  419.5 34.3 %collective-permute-start.33 = (bf16[128,1536]{1,0:T(8,128)(2,1)}, bf16[128,1536]{1,0:T(8,128)(2,1)}, u32[]{:S(2)}, u32[]{:S(2)}) collective-permute-start(bf16[128,1536]{1,0:T(8,128)(2,1)} %get-tuple-element.288), channel_id=1, source_target_pairs={{0,6},{2,0},{4,2},{6,4},{1,7},{3,1},{5,3},{7,5},{8,14},{10,8},{12,... | collective-permute-start | bytes 1179656 | tf_op jit(solution)/shard_map/ppermute | solution.py:594
  428.0 8.9 %collective-permute-start.28 = (bf16[512,256]{1,0:T(8,128)(2,1)S(1)}, bf16[512,256]{1,0:T(8,128)(2,1)S(1)}, u32[]{:S(2)}, u32[]{:S(2)}) collective-permute-start(bf16[512,256]{1,0:T(8,128)(2,1)S(1)} %bitcast.181), channel_id=1, source_target_pairs={{0,1},{1,0},{2,3},{3,2},{4,5},{5,4},{6,7},{7,6},{8,9},{9,8},{10,11... | collective-permute-start | bytes 786440 | tf_op jit(solution)/shard_map/ppermute | solution.py:1421
  435.8 12.0 %collective-permute-start.30 = (bf16[512,256]{1,0:T(8,128)(2,1)S(1)}, bf16[512,256]{1,0:T(8,128)(2,1)S(1)}, u32[]{:S(2)}, u32[]{:S(2)}) collective-permute-start(bf16[512,256]{1,0:T(8,128)(2,1)S(1)} %bitcast.182), channel_id=1, source_target_pairs={{0,1},{1,0},{2,3},{3,2},{4,5},{5,4},{6,7},{7,6},{8,9},{9,8},{10,11... | collective-permute-start | bytes 786440 | tf_op jit(solution)/shard_map/ppermute | solution.py:1421
  483.2 7.2 %collective-permute-start.34 = (bf16[2,512,2048]{2,1,0:T(8,128)(2,1)S(1)}, bf16[2,512,2048]{2,1,0:T(8,128)(2,1)S(1)}, u32[]{:S(2)}, u32[]{:S(2)}) collective-permute-start(bf16[2,512,2048]{2,1,0:T(8,128)(2,1)S(1)} %product.18), channel_id=1, source_target_pairs={{0,8},{8,0},{1,9},{9,1},{2,10},{10,2},{3,11},{11,3},{4,12},{12,4},... | collective-permute-start | bytes 12582920 | tf_op jit(solution)/shard_map/ppermute | solution.py:415
  483.6 27.8 %collective-permute-start.35 = (bf16[4,144,768]{2,1,0:T(8,128)(2,1)S(1)}, bf16[4,144,768]{2,1,0:T(8,128)(2,1)S(1)}, u32[]{:S(2)}, u32[]{:S(2)}) collective-permute-start(bf16[4,144,768]{2,1,0:T(8,128)(2,1)S(1)} %get-tuple-element.208), channel_id=1, source_target_pairs={{0,1},{1,16},{16,17},{17,0},{2,3},{3,18},{18,19},{19,2},{4,5},{5,2... | collective-permute-start | bytes 2654216 | tf_op jit(solution)/shard_map/ppermute | solution.py:401
  484.0 45.0 %collective-permute-start.36 = (bf16[4,144,768]{2,1,0:T(8,128)(2,1)S(1)}, bf16[4,144,768]{2,1,0:T(8,128)(2,1)S(1)}, u32[]{:S(2)}, u32[]{:S(2)}) collective-permute-start(bf16[4,144,768]{2,1,0:T(8,128)(2,1)S(1)} %get-tuple-element.207), channel_id=1, source_target_pairs={{0,16},{1,17},{16,0},{17,1},{2,18},{3,19},{18,2},{19,3},{4,20},{5,... | collective-permute-start | bytes 2654216 | tf_op jit(solution)/shard_map/ppermute | solution.py:401
  485.2 48.4 %collective-permute-start.37 = (bf16[4,144,768]{2,1,0:T(8,128)(2,1)S(1)}, bf16[4,144,768]{2,1,0:T(8,128)(2,1)S(1)}, u32[]{:S(2)}, u32[]{:S(2)}) collective-permute-start(bf16[4,144,768]{2,1,0:T(8,128)(2,1)S(1)} %get-tuple-element.206), channel_id=1, source_target_pairs={{0,17},{1,0},{16,1},{17,16},{2,19},{3,2},{18,3},{19,18},{4,21},{5,... | collective-permute-start | bytes 2654216 | tf_op jit(solution)/shard_map/ppermute | solution.py:401
  534.1 50.3 %copy-start.82 = (bf16[2,1,64,2048]{3,2,1,0:T(8,128)(2,1)S(1)}, bf16[2,1,64,2048]{3,2,1,0:T(8,128)(2,1)}, u32[]{:S(2)}) copy-start(bf16[2,1,64,2048]{3,2,1,0:T(8,128)(2,1)} %param.16) | copy-start | bytes 1572868
  535.0 49.7 %copy-start.94 = (f32[1,4,4,128]{3,2,1,0:T(4,128)S(1)}, f32[1,4,4,128]{3,2,1,0:T(4,128)}, u32[]{:S(2)}) copy-start(f32[1,4,4,128]{3,2,1,0:T(4,128)} %get-tuple-element.298) | copy-start | bytes 24580
  535.0 17.5 %all-to-all-start.1 = ((bf16[4,144,512]{2,1,0:T(8,128)(2,1)}), bf16[4,144,512]{2,1,0:T(8,128)(2,1)S(1)}, u32[]{:S(2)}, u32[]{:S(2)}) async-start(bf16[4,144,512]{2,1,0:T(8,128)(2,1)} %slice.98), calls=%async_computation.2 | async-start | bytes 1179648 | tf_op jit(solution)/shard_map/all_to_all | solution.py:1292
  552.5 63.5 %copy-start.28 = (bf16[4,144,768]{2,1,0:T(8,128)(2,1)}, bf16[4,144,768]{2,1,0:T(8,128)(2,1)S(1)}, u32[]{:S(2)}) copy-start(bf16[4,144,768]{2,1,0:T(8,128)(2,1)S(1)} %pad_maximum_fusion.1.refs_0_) | copy-start | bytes 2654212
  552.5 30.4 %collective-permute-start.41 = (bf16[4,144,768]{2,1,0:T(8,128)(2,1)S(1)}, bf16[4,144,768]{2,1,0:T(8,128)(2,1)}, u32[]{:S(2)}, u32[]{:S(2)}) collective-permute-start(bf16[4,144,768]{2,1,0:T(8,128)(2,1)S(1)} %pad_maximum_fusion.1.refs_0_), channel_id=1, source_target_pairs={{0,1},{1,16},{16,17},{17,0},{2,3},{3,18},{18,19},{19,2},{4,5},{5,2... | collective-permute-start | bytes 2654216 | tf_op jit(solution)/shard_map/ppermute | solution.py:394
  555.2 70.2 %collective-permute-start.38 = (bf16[2,128,2048]{2,1,0:T(8,128)(2,1)}, bf16[2,128,2048]{2,1,0:T(8,128)(2,1)}, u32[]{:S(2)}, u32[]{:S(2)}) collective-permute-start(bf16[2,128,2048]{2,1,0:T(8,128)(2,1)} %get-tuple-element.220), channel_id=1, source_target_pairs={{0,2},{2,4},{4,6},{6,0},{1,3},{3,5},{5,7},{7,1},{8,10},{10,12},{12... | collective-permute-start | bytes 3145736 | tf_op jit(solution)/shard_map/ppermute | solution.py:401
  556.7 89.1 %collective-permute-start.39 = (bf16[2,128,2048]{2,1,0:T(8,128)(2,1)}, bf16[2,128,2048]{2,1,0:T(8,128)(2,1)}, u32[]{:S(2)}, u32[]{:S(2)}) collective-permute-start(bf16[2,128,2048]{2,1,0:T(8,128)(2,1)} %get-tuple-element.221), channel_id=1, source_target_pairs={{0,4},{2,6},{4,0},{6,2},{1,5},{3,7},{5,1},{7,3},{8,12},{10,14},{12... | collective-permute-start | bytes 3145736 | tf_op jit(solution)/shard_map/ppermute | solution.py:401
  560.8 88.7 %collective-permute-start.40 = (bf16[2,128,2048]{2,1,0:T(8,128)(2,1)}, bf16[2,128,2048]{2,1,0:T(8,128)(2,1)}, u32[]{:S(2)}, u32[]{:S(2)}) collective-permute-start(bf16[2,128,2048]{2,1,0:T(8,128)(2,1)} %get-tuple-element.222), channel_id=1, source_target_pairs={{0,6},{2,0},{4,2},{6,4},{1,7},{3,1},{5,3},{7,5},{8,14},{10,8},{12,... | collective-permute-start | bytes 3145736 | tf_op jit(solution)/shard_map/ppermute | solution.py:401
  560.9 55.2 %collective-permute-start.42 = (bf16[4,144,768]{2,1,0:T(8,128)(2,1)S(1)}, bf16[4,144,768]{2,1,0:T(8,128)(2,1)}, u32[]{:S(2)}, u32[]{:S(2)}) collective-permute-start(bf16[4,144,768]{2,1,0:T(8,128)(2,1)S(1)} %pad_maximum_fusion.1.refs_0_), channel_id=1, source_target_pairs={{0,16},{1,17},{16,0},{17,1},{2,18},{3,19},{18,2},{19,3},{4,20},{5,... | collective-permute-start | bytes 2654216 | tf_op jit(solution)/shard_map/ppermute | solution.py:394
  582.9 33.1 %collective-permute-start.43 = (bf16[4,144,768]{2,1,0:T(8,128)(2,1)S(1)}, bf16[4,144,768]{2,1,0:T(8,128)(2,1)}, u32[]{:S(2)}, u32[]{:S(2)}) collective-permute-start(bf16[4,144,768]{2,1,0:T(8,128)(2,1)S(1)} %pad_maximum_fusion.1.refs_0_), channel_id=1, source_target_pairs={{0,17},{1,0},{16,1},{17,16},{2,19},{3,2},{18,3},{19,18},{4,21},{5,... | collective-permute-start | bytes 2654216 | tf_op jit(solution)/shard_map/ppermute | solution.py:394
  593.1 56.4 %copy-start.54 = (f32[2,128,2048]{2,1,0:T(8,128)S(1)}, f32[2,128,2048]{2,1,0:T(8,128)}, u32[]{:S(2)}) copy-start(f32[2,128,2048]{2,1,0:T(8,128)} %copy-done.53) | copy-start | bytes 6291460
  616.1 43.3 %collective-permute-start.44 = (bf16[4,144,768]{2,1,0:T(8,128)(2,1)S(1)}, bf16[4,144,768]{2,1,0:T(8,128)(2,1)}, u32[]{:S(2)}, u32[]{:S(2)}) collective-permute-start(bf16[4,144,768]{2,1,0:T(8,128)(2,1)S(1)} %pad_maximum_fusion.1.refs_0_), channel_id=1, source_target_pairs={{0,8},{8,0},{1,9},{9,1},{2,10},{10,2},{3,11},{11,3},{4,12},{12,4},... | collective-permute-start | bytes 2654216 | tf_op jit(solution)/shard_map/ppermute | solution.py:415
  616.1 43.2 %collective-permute-start.45 = (bf16[4,144,768]{2,1,0:T(8,128)(2,1)}, bf16[4,144,768]{2,1,0:T(8,128)(2,1)}, u32[]{:S(2)}, u32[]{:S(2)}) collective-permute-start(bf16[4,144,768]{2,1,0:T(8,128)(2,1)} %collective-permute-done.41.refs_1_), channel_id=1, source_target_pairs={{0,8},{8,0},{1,9},{9,1},{2,10},{10,2},{3,11},{11,3},{4,12},{12,4},... | collective-permute-start | bytes 2654216 | tf_op jit(solution)/shard_map/ppermute | solution.py:415
  625.4 34.0 %collective-permute-start.46 = (bf16[4,144,768]{2,1,0:T(8,128)(2,1)}, bf16[4,144,768]{2,1,0:T(8,128)(2,1)}, u32[]{:S(2)}, u32[]{:S(2)}) collective-permute-start(bf16[4,144,768]{2,1,0:T(8,128)(2,1)} %collective-permute-done.42.refs_2_), channel_id=1, source_target_pairs={{0,8},{8,0},{1,9},{9,1},{2,10},{10,2},{3,11},{11,3},{4,12},{12,4},... | collective-permute-start | bytes 2654216 | tf_op jit(solution)/shard_map/ppermute | solution.py:415
  645.8 13.6 %collective-permute-start.47 = (bf16[4,144,768]{2,1,0:T(8,128)(2,1)}, bf16[4,144,768]{2,1,0:T(8,128)(2,1)}, u32[]{:S(2)}, u32[]{:S(2)}) collective-permute-start(bf16[4,144,768]{2,1,0:T(8,128)(2,1)} %collective-permute-done.43.refs_3_), channel_id=1, source_target_pairs={{0,8},{8,0},{1,9},{9,1},{2,10},{10,2},{3,11},{11,3},{4,12},{12,4},... | collective-permute-start | bytes 2654216 | tf_op jit(solution)/shard_map/ppermute | solution.py:415
  (95 other events, 742.1 us)
Sparse Core Ops, SparseCore 0:
  9.6 53.5 all-gather.8
  71.9 45.0 all-gather.12
  159.6 68.2 all-gather.10
  295.9 93.1 reduce-scatter.1
  411.9 50.8 all-gather.14
  465.2 109.7 all-gather.16
